TPU v7x, 32 devices: a whole 2x2x4 slice. The times are simulated.
32 devices in a mesh: dp: 8 (over z, x), tensor: 4 (over y, core).
Axes of the slice: x: 2, y: 2, z: 4, core: 2. Of those that a mesh axis runs over, the one named last changes fastest.
Arguments:
- tokens: bfloat16 [16, 1024, 1536], P(None, 'dp', 'tensor'), may hold values from -6 to 6
- out_grad: bfloat16 [10240, 1536], P('dp', 'tensor'), may hold values from -6 to 6
- lengths: int32 [16], replicated, may hold values from 1 to 1024, as said below
- deal: int32 [16], replicated, may hold values from 0 to 15, as said below
- mixer_gain: bfloat16 [1536], P(('tensor', 'dp')), may hold values from 0.5 to 1.5
- inner_weight: bfloat16 [1536, 3072], P('dp', 'tensor'), may hold values from -0.15625 to 0.15625
- gate_weight: bfloat16 [1536, 3072], P('dp', 'tensor'), may hold values from -0.15625 to 0.15625
- conv_taps: bfloat16 [4, 3072], P(None, ('tensor', 'dp')), may hold values from -3 to 3
- conv_bias: bfloat16 [3072], P(('tensor', 'dp')), may hold values from -3 to 3
- proj_weight: bfloat16 [3072, 128], P(('tensor', 'dp')), may hold values from -0.109375 to 0.109375
- proj_gains: bfloat16 [128], P('dp'), may hold values from 0.5 to 1.5
- step_weight: bfloat16 [96, 128], P(None, ('tensor', 'dp')), may hold values from -0.625 to 0.625
- step_bias: bfloat16 [128], P(('tensor', 'dp')), may hold values from -6 to -2.5
- log_rate: bfloat16 [128], P(('tensor', 'dp')), may hold values from -0.5 to 1
- skip_gain: bfloat16 [3072], P(('tensor', 'dp')), may hold values from 0.5 to 1.5
- out_weight: bfloat16 [3072, 1536], P('tensor', 'dp'), may hold values from -0.3125 to 0.3125
- ffn_gain: bfloat16 [1536], P(('tensor', 'dp')), may hold values from 0.5 to 1.5
- ffn_gate: bfloat16 [1536, 4096], P('dp', 'tensor'), may hold values from -0.15625 to 0.15625
- ffn_up: bfloat16 [1536, 4096], P('dp', 'tensor'), may hold values from -0.15625 to 0.15625
- ffn_down: bfloat16 [4096, 1536], P('tensor', 'dp'), may hold values from -0.1875 to 0.1875
Outputs:
- output: bfloat16 [10240, 1536], P('dp', 'tensor')
- tokens_grad: bfloat16 [16, 1024, 1536], P(None, 'dp', 'tensor')
- grad_mixer_gain: float32 [1536], P(('tensor', 'dp'))
- grad_inner_weight: float32 [1536, 3072], P('dp', 'tensor')
- grad_gate_weight: float32 [1536, 3072], P('dp', 'tensor')
- grad_conv_taps: float32 [4, 3072], P(None, ('tensor', 'dp'))
- grad_conv_bias: float32 [3072], P(('tensor', 'dp'))
- grad_proj_weight: float32 [3072, 128], P(('tensor', 'dp'))
- grad_proj_gains: float32 [128], P('dp')
- grad_step_weight: float32 [96, 128], P(None, ('tensor', 'dp'))
- grad_step_bias: float32 [128], P(('tensor', 'dp'))
- grad_log_rate: float32 [128], P(('tensor', 'dp'))
- grad_skip_gain: float32 [3072], P(('tensor', 'dp'))
- grad_out_weight: float32 [3072, 1536], P('tensor', 'dp')
- grad_ffn_gain: float32 [1536], P(('tensor', 'dp'))
- grad_ffn_gate: float32 [1536, 4096], P('dp', 'tensor')
- grad_ffn_up: float32 [1536, 4096], P('dp', 'tensor')
- grad_ffn_down: float32 [4096, 1536], P('tensor', 'dp')
Inputs may be any that keep to these rules, and one draw needn't show every extreme that they name: In deal order the sequences come in pairs whose lengths add up to at most 1280, the first of a pair being at least 512 long; so the 2 sequences dealt to one dp index fill at most 1280 packed rows, and in every draw the rows of one dp index are all filled and some sequence is exactly 1024 long. `deal`: A permutation of the sequence indices.
All inputs are finite; a program needn't handle non-finite values.
Results may differ from a plain program's by a relative error of at most 0.022.
Values may be sent and summed in bfloat16 or wider, within the bound.
No kernel may reach another device: no remote copies, remote signals or barrier semaphores. Data moves between devices by JAX's collectives and lax.ppermute only.
A program may use at most 256 MiB of HBM per device.

v0:
```python
import jax
import jax.numpy as jnp
from jax import lax
from jax.sharding import PartitionSpec as P

D = 1536
NS = 16
KC = 4
R = 96
LMAX = 1024
SPAN = 256
SPG = 2
GCAP = 1280


HIGHEST = lax.Precision.HIGHEST
EPSILON = 1e-06


def contract(left, right, left_dim, right_dim):
    return lax.dot_general(
        left, right, (((left_dim,), (right_dim,)), ((), ())), preferred_element_type=jnp.float32
    )


def row_norm(values, gain_part):
    scale = lax.rsqrt(jnp.mean(values * values, axis=-1, keepdims=True) + EPSILON)
    return values * scale * gain_part


def feature_stats(partial_rows):
    return lax.psum(partial_rows, "tensor")


def norm_columns(values, gain_part):
    mean_square = feature_stats(jnp.sum(values * values, axis=1)) / D
    inverse = lax.rsqrt(mean_square + EPSILON)
    return (values * inverse[:, None] * gain_part, inverse)


def norm_columns_back(values, inverse, gain_part, upstream):
    normed = values * inverse[:, None]
    gain_grad = jnp.sum(upstream * normed, axis=0)
    scaled = upstream * gain_part
    along_mean = feature_stats(jnp.sum(scaled * normed, axis=1)) / D
    return (inverse[:, None] * (scaled - normed * along_mean[:, None]), gain_grad)


def gather_features(values):
    return lax.all_gather(values, "tensor", axis=1, tiled=True)


def sum_features(terms):
    return lax.psum_scatter(terms, "tensor", scatter_dimension=1, tiled=True)


def conv_silu(inner_pre, conv_taps, conv_bias, segment):
    row_count = inner_pre.shape[0]
    running_sum = conv_bias + conv_taps[KC - 1] * inner_pre
    for offset in range(1, KC):
        earlier = jnp.concatenate(
            [
                jnp.zeros((offset, inner_pre.shape[1]), inner_pre.dtype),
                inner_pre[: row_count - offset],
            ],
            axis=0,
        )
        linked = jnp.concatenate(
            [jnp.zeros((offset,), jnp.bool_), segment[offset:] == segment[: row_count - offset]]
        )
        running_sum = running_sum + conv_taps[KC - 1 - offset] * jnp.where(
            linked[:, None], earlier, 0.0
        )
    return jax.nn.silu(running_sum)


def scan_blocks(values, step_size, log_decay, input_b, output_c, segment):
    row_count, head_count, head_width = values.shape
    blocks = row_count // SPAN
    causal = jnp.arange(SPAN)[:, None] >= jnp.arange(SPAN)[None, :]

    def one_block(running, pieces):
        ssm_state, seg_in = running
        block_values, block_steps, block_rates, block_in, block_out, block_segs = pieces
        cumulative = jnp.cumsum(block_rates, axis=0)
        linked = (causal & (block_segs[:, None] == block_segs[None, :]))[:, :, None]
        spread = cumulative[:, None, :] - cumulative[None, :, :]
        decays = jnp.where(linked, jnp.exp(jnp.where(linked, spread, 0.0)), 0.0)
        scores = jnp.dot(block_out, block_in.T, precision=HIGHEST)
        mixing = decays * scores[:, :, None]
        weighted = block_steps[:, :, None] * block_values
        inside = jnp.einsum("tsh,shp->thp", mixing, weighted, precision=HIGHEST)
        carried = (block_segs == seg_in).astype(jnp.float32)[:, None] * jnp.exp(cumulative)
        from_state = (
            jnp.einsum("tn,hnp->thp", block_out, ssm_state, precision=HIGHEST) * carried[:, :, None]
        )
        last_seg = block_segs[SPAN - 1]
        tail_weight = (
            jnp.exp(cumulative[SPAN - 1][None, :] - cumulative)
            * (block_segs == last_seg).astype(jnp.float32)[:, None]
        )
        fresh_state = jnp.einsum(
            "sn,shp->hnp", block_in, tail_weight[:, :, None] * weighted, precision=HIGHEST
        )
        keep_factor = jnp.exp(cumulative[SPAN - 1]) * (last_seg == seg_in).astype(jnp.float32)
        return (
            (fresh_state + keep_factor[:, None, None] * ssm_state, last_seg),
            inside + from_state,
        )

    shaped = (
        values.reshape(blocks, SPAN, head_count, head_width),
        step_size.reshape(blocks, SPAN, head_count),
        log_decay.reshape(blocks, SPAN, head_count),
        input_b.reshape(blocks, SPAN, -1),
        output_c.reshape(blocks, SPAN, -1),
        segment.reshape(blocks, SPAN),
    )
    initial = (jnp.zeros((head_count, input_b.shape[1], head_width), jnp.float32), jnp.int32(-1))
    unused, result = lax.scan(jax.checkpoint(one_block), initial, shaped)
    return result.reshape(row_count, head_count, head_width)


def mixer_core(
    projected, conv_in, gate_pre, step_weight, step_bias, log_rate, skip_gain, proj_gains, segment
):
    row_count = conv_in.shape[0]
    step_low = row_norm(projected[:, :R], proj_gains[:R])
    input_b = row_norm(projected[:, R : R + NS], proj_gains[R : R + NS])
    output_c = row_norm(projected[:, R + NS :], proj_gains[R + NS :])
    step_size = jax.nn.softplus(jnp.dot(step_low, step_weight, precision=HIGHEST) + step_bias)
    log_decay = -step_size * jnp.exp(log_rate)
    head_count = step_size.shape[1]
    values = conv_in.reshape(row_count, head_count, -1)
    scanned = scan_blocks(values, step_size, log_decay, input_b, output_c, segment)
    mixed_out = scanned.reshape(row_count, -1) + skip_gain * conv_in
    return mixed_out * jax.nn.silu(gate_pre)


def forward_pass(packed, weights, segment, live_rows, with_output):
    (
        mixer_gain,
        inner_weight,
        gate_weight,
        conv_taps,
        conv_bias,
        proj_weight,
        proj_gains,
        step_weight,
        step_bias,
        log_rate,
        skip_gain,
        out_weight,
        ffn_gain,
        ffn_gate,
        ffn_up,
        ffn_down,
    ) = weights
    normed_in, inverse_in = norm_columns(packed, mixer_gain.astype(jnp.float32))
    mixer_rows = gather_features(normed_in.astype(jnp.bfloat16))
    inner_pre = jnp.dot(mixer_rows, inner_weight, preferred_element_type=jnp.float32)
    gate_pre = jnp.dot(mixer_rows, gate_weight, preferred_element_type=jnp.float32)
    conv_out = conv_silu(
        inner_pre, conv_taps.astype(jnp.float32), conv_bias.astype(jnp.float32), segment
    ).astype(jnp.bfloat16)
    projected = lax.psum(
        jnp.dot(conv_out, proj_weight, preferred_element_type=jnp.float32), "tensor"
    )
    gated = mixer_core(
        projected,
        conv_out.astype(jnp.float32),
        gate_pre,
        step_weight.astype(jnp.float32),
        step_bias.astype(jnp.float32),
        log_rate.astype(jnp.float32),
        skip_gain.astype(jnp.float32),
        proj_gains.astype(jnp.float32),
        segment,
    ).astype(jnp.bfloat16)
    residual = packed + sum_features(jnp.dot(gated, out_weight, preferred_element_type=jnp.float32))
    normed_mid, inverse_mid = norm_columns(residual, ffn_gain.astype(jnp.float32))
    ffn_rows = gather_features(normed_mid.astype(jnp.bfloat16))
    gate_ffn = jnp.dot(ffn_rows, ffn_gate, preferred_element_type=jnp.float32)
    up_ffn = jnp.dot(ffn_rows, ffn_up, preferred_element_type=jnp.float32)
    hidden = (jax.nn.silu(gate_ffn) * up_ffn).astype(jnp.bfloat16)
    stored = (
        inverse_in,
        mixer_rows,
        inner_pre,
        gate_pre,
        conv_out,
        projected,
        gated,
        residual,
        inverse_mid,
        ffn_rows,
        gate_ffn,
        up_ffn,
        hidden,
    )
    if with_output:
        final_rows = residual + sum_features(
            jnp.dot(hidden, ffn_down, preferred_element_type=jnp.float32)
        )
        return (jnp.where(live_rows[:, None], final_rows, 0.0).astype(jnp.bfloat16), stored)
    return (None, stored)


def per_device(
    tokens,
    out_grad,
    lengths,
    deal,
    mixer_gain,
    inner_weight,
    gate_weight,
    conv_taps,
    conv_bias,
    proj_weight,
    proj_gains,
    step_weight,
    step_bias,
    log_rate,
    skip_gain,
    out_weight,
    ffn_gain,
    ffn_gate,
    ffn_up,
    ffn_down,
):
    group_index = lax.axis_index("dp")
    packed_lengths = lengths[deal]
    group_lengths = lax.dynamic_slice_in_dim(packed_lengths, group_index * SPG, SPG)
    starts = jnp.cumsum(group_lengths) - group_lengths
    filled = jnp.sum(group_lengths)
    row_ids = jnp.arange(GCAP, dtype=jnp.int32)
    slot_ids = jnp.arange(SPG, dtype=jnp.int32)
    live_rows = row_ids < filled
    segment = jnp.sum((row_ids[:, None] >= starts[None, :]).astype(jnp.int32), axis=1) - 1
    segment = jnp.where(live_rows, segment, SPG)
    seg_start = jnp.sum(
        jnp.where(segment[:, None] == slot_ids[None, :], starts[None, :], 0), axis=1
    )
    source_rows = jnp.where(live_rows, segment * LMAX + row_ids - seg_start, 0)
    position = jnp.arange(LMAX, dtype=jnp.int32)
    slot_live = (position[None, :] < group_lengths[:, None]).reshape(-1)
    slot_rows = jnp.where(slot_live, (starts[:, None] + position[None, :]).reshape(-1), 0)

    def arrive(received):
        flat_rows = received.reshape(SPG * LMAX, -1)
        return jnp.where(live_rows[:, None], flat_rows[source_rows], 0.0).astype(jnp.float32)

    ordered = tokens[deal]
    packed = arrive(lax.all_to_all(ordered, "dp", split_axis=0, concat_axis=1, tiled=True))
    weights = (
        lax.all_gather(mixer_gain, "dp", axis=0, tiled=True),
        lax.all_gather(inner_weight, "dp", axis=0, tiled=True),
        lax.all_gather(gate_weight, "dp", axis=0, tiled=True),
        lax.all_gather(conv_taps, "dp", axis=1, tiled=True),
        lax.all_gather(conv_bias, "dp", axis=0, tiled=True),
        lax.all_gather(proj_weight, "dp", axis=0, tiled=True),
        lax.all_gather(proj_gains, "dp", axis=0, tiled=True),
        lax.all_gather(step_weight, "dp", axis=1, tiled=True),
        lax.all_gather(step_bias, "dp", axis=0, tiled=True),
        lax.all_gather(log_rate, "dp", axis=0, tiled=True),
        lax.all_gather(skip_gain, "dp", axis=0, tiled=True),
        lax.all_gather(out_weight, "dp", axis=1, tiled=True),
        lax.all_gather(ffn_gain, "dp", axis=0, tiled=True),
        lax.all_gather(ffn_gate, "dp", axis=0, tiled=True),
        lax.all_gather(ffn_up, "dp", axis=0, tiled=True),
        lax.all_gather(ffn_down, "dp", axis=1, tiled=True),
    )
    output, unused = forward_pass(packed, weights, segment, live_rows, True)
    packed_again = arrive(lax.all_to_all(ordered, "dp", split_axis=0, concat_axis=1, tiled=True))
    weights_again = (
        lax.all_gather(mixer_gain, "dp", axis=0, tiled=True),
        lax.all_gather(inner_weight, "dp", axis=0, tiled=True),
        lax.all_gather(gate_weight, "dp", axis=0, tiled=True),
        lax.all_gather(conv_taps, "dp", axis=1, tiled=True),
        lax.all_gather(conv_bias, "dp", axis=0, tiled=True),
        lax.all_gather(proj_weight, "dp", axis=0, tiled=True),
        lax.all_gather(proj_gains, "dp", axis=0, tiled=True),
        lax.all_gather(step_weight, "dp", axis=1, tiled=True),
        lax.all_gather(step_bias, "dp", axis=0, tiled=True),
        lax.all_gather(log_rate, "dp", axis=0, tiled=True),
        lax.all_gather(skip_gain, "dp", axis=0, tiled=True),
        lax.all_gather(out_weight, "dp", axis=1, tiled=True),
        lax.all_gather(ffn_gain, "dp", axis=0, tiled=True),
        lax.all_gather(ffn_gate, "dp", axis=0, tiled=True),
        lax.all_gather(ffn_up, "dp", axis=0, tiled=True),
        lax.all_gather(ffn_down, "dp", axis=1, tiled=True),
    )
    unused_out, stored = forward_pass(packed_again, weights_again, segment, live_rows, False)
    (
        inverse_in,
        mixer_rows,
        inner_pre,
        gate_pre,
        conv_out,
        projected,
        gated,
        residual,
        inverse_mid,
        ffn_rows,
        gate_ffn,
        up_ffn,
        hidden,
    ) = stored
    (
        gain_all,
        inner_all,
        gate_all,
        taps_all,
        bias_all,
        proj_all,
        gains_all,
        step_w_all,
        step_b_all,
        rate_all,
        skip_all,
        out_all,
        ffn_gain_all,
        ffn_gate_all,
        ffn_up_all,
        ffn_down_all,
    ) = weights_again
    out_cot = jnp.where(live_rows[:, None], out_grad, 0.0)
    cot_rows = gather_features(out_cot)
    hidden_grad = contract(cot_rows, ffn_down_all, 1, 1)
    down_grad = contract(hidden, cot_rows, 0, 0)
    logistic = jax.nn.sigmoid(gate_ffn)
    activated = gate_ffn * logistic
    gate_grad = (hidden_grad * up_ffn * logistic * (1.0 + gate_ffn * (1.0 - logistic))).astype(
        jnp.bfloat16
    )
    up_grad = (hidden_grad * activated).astype(jnp.bfloat16)
    ffn_gate_grad = contract(ffn_rows, gate_grad, 0, 0)
    ffn_up_grad = contract(ffn_rows, up_grad, 0, 0)
    mid_grad = sum_features(
        contract(gate_grad, ffn_gate_all, 1, 1) + contract(up_grad, ffn_up_all, 1, 1)
    )
    mid_back, ffn_gain_grad = norm_columns_back(
        residual, inverse_mid, ffn_gain_all.astype(jnp.float32), mid_grad
    )
    residual_grad = out_cot.astype(jnp.float32) + mid_back
    ffn_grads = (
        lax.psum_scatter(
            ffn_gain_grad.astype(jnp.bfloat16), "dp", scatter_dimension=0, tiled=True
        ).astype(jnp.float32),
        lax.psum_scatter(
            ffn_gate_grad.astype(jnp.bfloat16), "dp", scatter_dimension=0, tiled=True
        ).astype(jnp.float32),
        lax.psum_scatter(
            ffn_up_grad.astype(jnp.bfloat16), "dp", scatter_dimension=0, tiled=True
        ).astype(jnp.float32),
        lax.psum_scatter(
            down_grad.astype(jnp.bfloat16), "dp", scatter_dimension=1, tiled=True
        ).astype(jnp.float32),
    )
    branch_rows = gather_features(residual_grad.astype(jnp.bfloat16))
    gated_grad = contract(branch_rows, out_all, 1, 1)
    out_weight_grad = contract(gated, branch_rows, 0, 0)

    def core_piece(proj_in, conv_in, gate_in, step_w, step_b, rate_in, skip_in, gains_in):
        return mixer_core(
            proj_in, conv_in, gate_in, step_w, step_b, rate_in, skip_in, gains_in, segment
        )

    unused_core, core_pull = jax.vjp(
        core_piece,
        projected,
        conv_out.astype(jnp.float32),
        gate_pre,
        step_w_all.astype(jnp.float32),
        step_b_all.astype(jnp.float32),
        rate_all.astype(jnp.float32),
        skip_all.astype(jnp.float32),
        gains_all.astype(jnp.float32),
    )
    (
        proj_part,
        conv_core_grad,
        gate_pre_grad,
        step_w_grad,
        step_b_grad,
        rate_grad,
        skip_grad,
        gains_part,
    ) = core_pull(gated_grad)
    proj_total, gains_grad = (
        lax.psum(proj_part.astype(jnp.bfloat16), "tensor").astype(jnp.float32),
        lax.psum(gains_part.astype(jnp.bfloat16), "tensor").astype(jnp.float32),
    )
    proj_low = proj_total.astype(jnp.bfloat16)
    conv_grad = conv_core_grad + contract(proj_low, proj_all, 1, 1)
    proj_weight_grad = contract(conv_out, proj_low, 0, 0)

    def conv_piece(inner_in, taps_in, bias_in):
        return conv_silu(inner_in, taps_in, bias_in, segment)

    unused_conv, conv_pull = jax.vjp(
        conv_piece, inner_pre, taps_all.astype(jnp.float32), bias_all.astype(jnp.float32)
    )
    inner_grad, taps_grad, bias_grad = conv_pull(conv_grad)
    inner_low = inner_grad.astype(jnp.bfloat16)
    gate_low = gate_pre_grad.astype(jnp.bfloat16)
    inner_weight_grad = contract(mixer_rows, inner_low, 0, 0)
    gate_weight_grad = contract(mixer_rows, gate_low, 0, 0)
    in_grad = sum_features(
        contract(inner_low, inner_all, 1, 1) + contract(gate_low, gate_all, 1, 1)
    )
    in_back, mixer_gain_grad = norm_columns_back(
        packed_again, inverse_in, gain_all.astype(jnp.float32), in_grad
    )
    mixer_grads = (
        lax.psum_scatter(
            mixer_gain_grad.astype(jnp.bfloat16), "dp", scatter_dimension=0, tiled=True
        ).astype(jnp.float32),
        lax.psum_scatter(
            inner_weight_grad.astype(jnp.bfloat16), "dp", scatter_dimension=0, tiled=True
        ).astype(jnp.float32),
        lax.psum_scatter(
            gate_weight_grad.astype(jnp.bfloat16), "dp", scatter_dimension=0, tiled=True
        ).astype(jnp.float32),
        lax.psum_scatter(
            taps_grad.astype(jnp.bfloat16), "dp", scatter_dimension=1, tiled=True
        ).astype(jnp.float32),
        lax.psum_scatter(
            bias_grad.astype(jnp.bfloat16), "dp", scatter_dimension=0, tiled=True
        ).astype(jnp.float32),
        lax.psum_scatter(
            proj_weight_grad.astype(jnp.bfloat16), "dp", scatter_dimension=0, tiled=True
        ).astype(jnp.float32),
        lax.psum_scatter(
            gains_grad.astype(jnp.bfloat16), "dp", scatter_dimension=0, tiled=True
        ).astype(jnp.float32),
        lax.psum_scatter(
            step_w_grad.astype(jnp.bfloat16), "dp", scatter_dimension=1, tiled=True
        ).astype(jnp.float32),
        lax.psum_scatter(
            step_b_grad.astype(jnp.bfloat16), "dp", scatter_dimension=0, tiled=True
        ).astype(jnp.float32),
        lax.psum_scatter(
            rate_grad.astype(jnp.bfloat16), "dp", scatter_dimension=0, tiled=True
        ).astype(jnp.float32),
        lax.psum_scatter(
            skip_grad.astype(jnp.bfloat16), "dp", scatter_dimension=0, tiled=True
        ).astype(jnp.float32),
        lax.psum_scatter(
            out_weight_grad.astype(jnp.bfloat16), "dp", scatter_dimension=1, tiled=True
        ).astype(jnp.float32),
    )
    grad_packed = (residual_grad + in_back).astype(jnp.bfloat16)
    slots_back = jnp.where(slot_live[:, None], grad_packed[slot_rows], 0.0)
    slots_back = slots_back.reshape(SPG, LMAX, -1)
    returned = lax.all_to_all(slots_back, "dp", split_axis=1, concat_axis=0, tiled=True)
    inverse_deal = jnp.zeros_like(deal).at[deal].set(jnp.arange(deal.shape[0], dtype=jnp.int32))
    tokens_grad = returned[inverse_deal]
    return (
        output,
        tokens_grad,
        mixer_grads[0],
        mixer_grads[1],
        mixer_grads[2],
        mixer_grads[3],
        mixer_grads[4],
        mixer_grads[5],
        mixer_grads[6],
        mixer_grads[7],
        mixer_grads[8],
        mixer_grads[9],
        mixer_grads[10],
        mixer_grads[11],
        ffn_grads[0],
        ffn_grads[1],
        ffn_grads[2],
        ffn_grads[3],
    )


def solution(mesh):
    return jax.shard_map(
        per_device,
        mesh=mesh,
        in_specs=(
            P(None, "dp", "tensor"),
            P("dp", "tensor"),
            P(),
            P(),
            P(("tensor", "dp")),
            P("dp", "tensor"),
            P("dp", "tensor"),
            P(None, ("tensor", "dp")),
            P(("tensor", "dp")),
            P(("tensor", "dp"), None),
            P("dp"),
            P(None, ("tensor", "dp")),
            P(("tensor", "dp")),
            P(("tensor", "dp")),
            P(("tensor", "dp")),
            P("tensor", "dp"),
            P(("tensor", "dp")),
            P("dp", "tensor"),
            P("dp", "tensor"),
            P("tensor", "dp"),
        ),
        out_specs=(
            P("dp", "tensor"),
            P(None, "dp", "tensor"),
            P(("tensor", "dp")),
            P("dp", "tensor"),
            P("dp", "tensor"),
            P(None, ("tensor", "dp")),
            P(("tensor", "dp")),
            P(("tensor", "dp"), None),
            P("dp"),
            P(None, ("tensor", "dp")),
            P(("tensor", "dp")),
            P(("tensor", "dp")),
            P(("tensor", "dp")),
            P("tensor", "dp"),
            P(("tensor", "dp")),
            P("dp", "tensor"),
            P("dp", "tensor"),
            P("tensor", "dp"),
        ),
        check_vma=False,
    )
```

profile of v0, /device:TPU:0, one launch (start us, length us, event | category | flops | bytes accessed | tf_op | source)
XLA Modules:
  0.0 2352.9 jit_solution(768247374184377048)
XLA Ops:
  22.9 45.7 %all-reduce.36 = (bf16[32]{0:T(256)(128)(2,1)S(1)}, bf16[384]{0:T(512)(128)(2,1)S(1)}, bf16[768]{0:T(1024)(128)(2,1)S(1)}, bf16[128]{0:T(256)(128)(2,1)S(1)}, bf...) all-reduce(bf16[32]{0:T(256)(128)(2,1)S(1)} %dynamic-update-slice.4, ...), channel_id=1, replica_groups=mesh['dp'=8,'tensor'=4] {'dp'}, use_global_device_ids=true, to_apply=%add.24 | all-reduce | flops 2496 | bytes 9984
  93.8 28.5 %all-gather = bf16[8,96,4]{1,2,0:T(4,128)(2,1)S(1)} all-gather(bf16[1,96,4]{1,2,0:T(4,128)(2,1)S(1)} %bitcast.587), channel_id=1, replica_groups=mesh['dp'=8,'tensor'=4] {'dp'}, dimensions={0}, use_global_device_ids=true | all-gather | bytes 6912 | tf_op jit(solution)/shard_map/all_gather | solution.py:259
  122.4 30.6 %all_gather.83 = bf16[768,128]{1,0:T(8,128)(2,1)S(1)} all-gather(bf16[96,128]{1,0:T(8,128)(2,1)S(1)} %copy-done.67), channel_id=1, replica_groups=mesh['dp'=8,'tensor'=4] {'dp'}, dimensions={0}, use_global_device_ids=true | all-gather | bytes 221184 | tf_op jit(solution)/shard_map/all_gather | solution.py:261
  169.5 18.2 all-gather.1
  218.4 187.0 %while.67 = (s32[]{:T(128)}, f32[32,16,24]{2,1,0:T(8,128)S(1)}, s32[]{:T(128)}, f32[5,256,32,24]{1,0,3,2:T(8,128)}, f32[5,256,32]{1,2,0:T(8,128)}, /*index=5*/s3...) while((s32[]{:T(128)}, f32[32,16,24]{2,1,0:T(8,128)S(1)}, ...), condition=%wide.region_13.14_spmd.clone, body=%wide.region_10.13_spmd.clone.sunk | while | flops 702760064 | bytes 8518238 | solution.py:120
  236.8 14.5 dynamic_update_slice.93
  274.2 14.5 dynamic_update_slice.93
  311.6 14.5 dynamic_update_slice.93
  349.0 14.5 dynamic_update_slice.93
  386.4 14.5 dynamic_update_slice.93
  437.6 66.0 %reduce-scatter.15.cloned.1.call-done = f32[1280,384]{1,0:T(8,128)} async-done(((f32[1280,1536]{1,0:T(8,128)}), f32[1280,384]{1,0:T(8,128)}) %reduce-scatter.15.cloned.1.call-update) | async-done | bytes 1966096 | tf_op jit(solution)/shard_map/reduce_scatter | solution.py:54
  516.8 49.6 %all-gather.23.cloned.1.call-done = bf16[1536,1024]{1,0:T(8,128)(2,1)} async-done(((bf16[192,1024]{1,0:T(8,128)(2,1)}), bf16[1536,1024]{1,0:T(8,128)(2,1)}) %all-gather.23.cloned.1.call-update) | async-done | bytes 3145744 | tf_op jit(solution)/shard_map/all_gather | solution.py:269
  566.4 33.8 %all-gather.21.cloned.1.call-done = bf16[1280,1536]{1,0:T(8,128)(2,1)} async-done(((bf16[1280,384]{1,0:T(8,128)(2,1)}), bf16[1280,1536]{1,0:T(8,128)(2,1)}) %all-gather.21.cloned.1.call-update) | async-done | bytes 3932176 | tf_op jit(solution)/shard_map/all_gather | solution.py:50
  609.8 53.3 %all-gather.25.cloned.1.call-done = bf16[1536,1024]{1,0:T(8,128)(2,1)} async-done(((bf16[192,1024]{1,0:T(8,128)(2,1)}), bf16[1536,1024]{1,0:T(8,128)(2,1)}) %all-gather.25.cloned.1.call-update) | async-done | bytes 3145744 | tf_op jit(solution)/shard_map/all_gather | solution.py:270
  672.9 51.6 %all-gather.27.cloned.1.call-done = bf16[1024,1536]{0,1:T(8,128)(2,1)} async-done(((bf16[1024,192]{0,1:T(8,128)(2,1)}), bf16[1024,1536]{0,1:T(8,128)(2,1)}) %all-gather.27.cloned.1.call-update) | async-done | bytes 3145744 | tf_op jit(solution)/shard_map/all_gather | solution.py:271
  724.5 33.3 %all-gather.29.cloned.1.call-done = bf16[1280,1536]{1,0:T(8,128)(2,1)} async-done(((bf16[1280,384]{1,0:T(8,128)(2,1)}), bf16[1280,1536]{1,0:T(8,128)(2,1)}) %all-gather.29.cloned.1.call-update) | async-done | bytes 3932176 | tf_op jit(solution)/shard_map/all_gather | solution.py:50
  781.7 69.0 %reduce-scatter.19.cloned.1.call-done = f32[1280,384]{1,0:T(8,128)} async-done(((f32[1280,1536]{1,0:T(8,128)}), f32[1280,384]{1,0:T(8,128)}) %reduce-scatter.19.cloned.1.call-update) | async-done | bytes 1966096 | tf_op jit(solution)/shard_map/reduce_scatter | solution.py:54
  865.9 198.0 %while.68 = (s32[]{:T(128)}, f32[32,16,24]{2,1,0:T(8,128)S(1)}, s32[]{:T(128)}, f32[5,256,32,24]{1,0,3,2:T(8,128)}, f32[5,32,16,24]{1,2,3,0:T(8,128)}, /*index=5...) while((s32[]{:T(128)}, f32[32,16,24]{2,1,0:T(8,128)S(1)}, ...), condition=%wide.region_24.25_spmd.clone, body=%wide.region_21.24_spmd.clone.sunk | while | flops 702772352 | bytes 8961147 | solution.py:120
  1107.3 419.1 %while.69 = (s32[]{:T(128)}, f32[32,16,24]{0,1,2:T(8,128)S(1)}, f32[5,256,32,24]{1,0,3,2:T(8,128)}, f32[5,256,32]{1,0,2:T(8,128)}, f32[5,256,32]{1,0,2:T(8,128)}...) while((s32[]{:T(128)}, f32[32,16,24]{0,1,2:T(8,128)S(1)}, ...), condition=%wide.region_38.39_spmd.clone, body=%wide.region_25.38_spmd.clone.sunk | while | flops 1470879104 | bytes 29037188 | solution.py:120
  1173.4 14.4 dynamic_update_slice.99
  1257.0 14.4 dynamic_update_slice.99
  1550.3 21.2 all-reduce.42.cloned.1.call-done
  1672.0 63.3 %reduce-scatter.17.cloned.1.call-done = f32[1280,384]{1,0:T(8,128)} async-done(((f32[1280,1536]{1,0:T(8,128)}), f32[1280,384]{1,0:T(8,128)}) %reduce-scatter.17.cloned.1.call-update) | async-done | bytes 1966096 | tf_op jit(solution)/shard_map/reduce_scatter | solution.py:54
  1769.4 65.3 %reduce-scatter.31.cloned.1.call-done = bf16[192,1024]{1,0:T(8,128)(2,1)} async-done(((bf16[1536,1024]{1,0:T(8,128)(2,1)}), bf16[192,1024]{1,0:T(8,128)(2,1)}) %reduce-scatter.31.cloned.1.call-update) | async-done | bytes 393232 | tf_op jit(solution)/shard_map/reduce_scatter | solution.py:350
  1836.6 75.1 %reduce-scatter.33.cloned.1.call-done = bf16[192,1024]{1,0:T(8,128)(2,1)} async-done(((bf16[1536,1024]{1,0:T(8,128)(2,1)}), bf16[192,1024]{1,0:T(8,128)(2,1)}) %reduce-scatter.33.cloned.1.call-update) | async-done | bytes 393232 | tf_op jit(solution)/shard_map/reduce_scatter | solution.py:353
  1913.7 75.0 %reduce-scatter.35.cloned.1.call-done = bf16[1024,192]{0,1:T(8,128)(2,1)} async-done(((bf16[1024,1536]{0,1:T(8,128)(2,1)}), bf16[1024,192]{0,1:T(8,128)(2,1)}) %reduce-scatter.35.cloned.1.call-update) | async-done | bytes 393232 | tf_op jit(solution)/shard_map/reduce_scatter | solution.py:356
  1991.3 61.3 %reduce-scatter.37.cloned.1.call-done = bf16[96,4]{1,0:T(8,128)(2,1)} async-done(((bf16[768,4]{1,0:T(8,128)(2,1)}), bf16[96,4]{1,0:T(8,128)(2,1)}) %reduce-scatter.37.cloned.1.call-update) | async-done | bytes 784
  2054.0 62.6 %reduce-scatter.27.cloned.1.call-done = bf16[96,128]{1,0:T(8,128)(2,1)} async-done(((bf16[768,128]{1,0:T(8,128)(2,1)}), bf16[96,128]{1,0:T(8,128)(2,1)}) %reduce-scatter.27.cloned.1.call-update) | async-done | bytes 24592 | tf_op jit(solution)/shard_map/reduce_scatter | solution.py:431
  2118.0 70.2 %reduce-scatter.29.cloned.1.call-done = bf16[768,192]{0,1:T(8,128)(2,1)} async-done(((bf16[768,1536]{0,1:T(8,128)(2,1)}), bf16[768,192]{0,1:T(8,128)(2,1)}) %reduce-scatter.29.cloned.1.call-update) | async-done | bytes 294928 | tf_op jit(solution)/shard_map/reduce_scatter | solution.py:449
  2189.9 70.0 %reduce-scatter.25.cloned.1.call-done = bf16[192,768]{1,0:T(8,128)(2,1)} async-done(((bf16[1536,768]{1,0:T(8,128)(2,1)}), bf16[192,768]{1,0:T(8,128)(2,1)}) %reduce-scatter.25.cloned.1.call-update) | async-done | bytes 294928 | tf_op jit(solution)/shard_map/reduce_scatter | solution.py:422
  2261.7 35.6 %all-reduce.35 = (bf16[384]{0:T(512)(128)(2,1)S(1)}, bf16[768]{0:T(1024)(128)(2,1)S(1)}, bf16[128]{0:T(256)(128)(2,1)S(1)}, bf16[96,32]{0,1:T(8,128)(2,1)S(1)}, ...) all-reduce(bf16[384]{0:T(512)(128)(2,1)S(1)} %get-tuple-element.105, ...), channel_id=6, replica_groups=mesh['dp'=8,'tensor'=4] {'dp'}, use_global_device_ids=true, to_apply=%region_48.49.clone | all-reduce | flops 5568 | bytes 22272
  2297.4 34.1 %reduce-scatter.23.cloned.1.call-done = bf16[192,768]{1,0:T(8,128)(2,1)} async-done(((bf16[1536,768]{1,0:T(8,128)(2,1)}), bf16[192,768]{1,0:T(8,128)(2,1)}) %reduce-scatter.23.cloned.1.call-update) | async-done | bytes 294928 | tf_op jit(solution)/shard_map/reduce_scatter | solution.py:419
  (1053 shorter events, 1094.5 us)
Async XLA Ops:
  7.3 146.0 %all-gather.15.cloned.1.call-start = ((), (), s32[]{:S(2)}) async-start(), calls=%async_computation.15 | async-start | bytes 2654208 | tf_op jit(solution)/shard_map/all_gather | solution.py:257
  10.6 69.7 %all-to-all-start = ((bf16[16,128,384]{2,1,0:T(8,128)(2,1)}), bf16[16,128,384]{2,1,0:T(8,128)(2,1)S(1)}, u32[]{:S(2)}, u32[]{:S(2)}) async-start(bf16[16,128,384]{2,1,0:T(8,128)(2,1)} %gather_fusion.1), calls=%async_computation | async-start | bytes 3145728 | tf_op jit(solution)/shard_map/all_to_all | solution.py:254
  17.9 135.4 %all-gather.13.cloned.1.call-start = ((), (), s32[]{:S(2)}) async-start(), calls=%async_computation.14 | async-start | bytes 4915200 | tf_op jit(solution)/shard_map/all_gather | solution.py:50
  72.3 787.0 %copy-start.36 = (pred[1280]{0:T(1024)(128)(4,1)}, pred[1280]{0:T(1024)(128)(4,1)S(1)}, u32[]{:S(2)}) copy-start(pred[1280]{0:T(1024)(128)(4,1)S(1)} %iota_compare_fusion.4) | copy-start | bytes 3844
  92.3 113.2 %all-reduce.40.cloned.1.call-start = ((), (), s32[]{:S(2)}) async-start(), calls=%async_computation.16 | async-start | bytes 1310720 | tf_op jit(solution)/shard_map/psum | solution.py:166
  168.1 249.7 %all-gather.17.cloned.1.call-start = ((), (), s32[]{:S(2)}) async-start(), calls=%async_computation.17 | async-start | bytes 2654208 | tf_op jit(solution)/shard_map/all_gather | solution.py:258
  168.7 259.4 %all-gather.19.cloned.1.call-start = ((), (), s32[]{:S(2)}) async-start(), calls=%async_computation.18 | async-start | bytes 2654208 | tf_op jit(solution)/shard_map/all_gather | solution.py:267
  169.3 334.2 %reduce-scatter.15.cloned.1.call-start = ((), (), s32[]{:S(2)}) async-start(), calls=%async_computation.19 | async-start | bytes 9830400 | tf_op jit(solution)/shard_map/reduce_scatter | solution.py:54
  189.0 887.3 %copy-start.86 = (f32[768]{0:T(1024)}, f32[768]{0:T(1024)S(1)}, u32[]{:S(2)}) copy-start(f32[768]{0:T(1024)S(1)} %convert_element_type.292) | copy-start | bytes 9220
  436.7 129.7 %all-gather.23.cloned.1.call-start = ((), (), s32[]{:S(2)}) async-start(), calls=%async_computation.21 | async-start | bytes 3538944 | tf_op jit(solution)/shard_map/all_gather | solution.py:269
  437.5 162.7 %all-gather.21.cloned.1.call-start = ((), (), s32[]{:S(2)}) async-start(), calls=%async_computation.20 | async-start | bytes 4915200 | tf_op jit(solution)/shard_map/all_gather | solution.py:50
  437.5 421.8 %copy-start.53 = (f32[384]{0:T(512)}, f32[384]{0:T(512)S(1)}, u32[]{:S(2)}) copy-start(f32[384]{0:T(512)S(1)} %convert_element_type.294) | copy-start | bytes 4612
  512.8 150.3 %all-gather.25.cloned.1.call-start = ((), (), s32[]{:S(2)}) async-start(), calls=%async_computation.22 | async-start | bytes 3538944 | tf_op jit(solution)/shard_map/all_gather | solution.py:270
  513.6 210.9 %all-gather.27.cloned.1.call-start = ((), (), s32[]{:S(2)}) async-start(), calls=%async_computation.23 | async-start | bytes 3538944 | tf_op jit(solution)/shard_map/all_gather | solution.py:271
  514.2 243.6 %all-gather.29.cloned.1.call-start = ((), (), s32[]{:S(2)}) async-start(), calls=%async_computation.25 | async-start | bytes 4915200 | tf_op jit(solution)/shard_map/all_gather | solution.py:50
  516.8 334.0 %reduce-scatter.19.cloned.1.call-start = ((), (), s32[]{:S(2)}) async-start(), calls=%async_computation.26 | async-start | bytes 9830400 | tf_op jit(solution)/shard_map/reduce_scatter | solution.py:54
  781.6 294.7 %all-gather.31.cloned.1.call-start = ((), (), s32[]{:S(2)}) async-start(), calls=%async_computation.27 | async-start | bytes 4915200 | tf_op jit(solution)/shard_map/all_gather | solution.py:50
  862.4 709.1 %all-reduce.42.cloned.1.call-start = ((), (), s32[]{:S(2)}) async-start(), calls=%async_computation.28 | async-start | bytes 655360 | tf_op jit(solution)/shard_map/psum | solution.py:391
  1107.3 424.7 %copy-start.6 = (f32[1280,128]{1,0:T(8,128)S(1)}, f32[1280,128]{1,0:T(8,128)}, u32[]{:S(2)}) copy-start(f32[1280,128]{1,0:T(8,128)} %all-reduce.40.cloned.1.call-done) | copy-start | bytes 1966084
  1537.9 125.8 %reduce-scatter.21.cloned.1.call-start = ((), (), s32[]{:S(2)}) async-start(), calls=%async_computation.29 | async-start | bytes 9830400 | tf_op jit(solution)/shard_map/reduce_scatter | solution.py:54
  1594.6 140.7 %reduce-scatter.17.cloned.1.call-start = ((), (), s32[]{:S(2)}) async-start(), calls=%async_computation.24 | async-start | bytes 9830400 | tf_op jit(solution)/shard_map/reduce_scatter | solution.py:54
  1605.9 228.7 %reduce-scatter.31.cloned.1.call-start = ((), (), s32[]{:S(2)}) async-start(), calls=%async_computation.34 | async-start | bytes 3538944 | tf_op jit(solution)/shard_map/reduce_scatter | solution.py:350
  1615.5 296.2 %reduce-scatter.33.cloned.1.call-start = ((), (), s32[]{:S(2)}) async-start(), calls=%async_computation.35 | async-start | bytes 3538944 | tf_op jit(solution)/shard_map/reduce_scatter | solution.py:353
  1625.4 363.3 %reduce-scatter.35.cloned.1.call-start = ((), (), s32[]{:S(2)}) async-start(), calls=%async_computation.36 | async-start | bytes 3538944 | tf_op jit(solution)/shard_map/reduce_scatter | solution.py:356
  1634.9 417.7 %reduce-scatter.37.cloned.1.call-start = ((), (), s32[]{:S(2)}) async-start(), calls=%async_computation.37 | async-start | bytes 221184
  1635.9 480.7 %reduce-scatter.27.cloned.1.call-start = ((), (), s32[]{:S(2)}) async-start(), calls=%async_computation.32 | async-start | bytes 221184 | tf_op jit(solution)/shard_map/reduce_scatter | solution.py:431
  1637.4 550.7 %reduce-scatter.29.cloned.1.call-start = ((), (), s32[]{:S(2)}) async-start(), calls=%async_computation.33 | async-start | bytes 2654208 | tf_op jit(solution)/shard_map/reduce_scatter | solution.py:449
  1645.1 614.8 %reduce-scatter.25.cloned.1.call-start = ((), (), s32[]{:S(2)}) async-start(), calls=%async_computation.31 | async-start | bytes 2654208 | tf_op jit(solution)/shard_map/reduce_scatter | solution.py:422
  1652.0 679.5 %reduce-scatter.23.cloned.1.call-start = ((), (), s32[]{:S(2)}) async-start(), calls=%async_computation.30 | async-start | bytes 2654208 | tf_op jit(solution)/shard_map/reduce_scatter | solution.py:419
  1760.3 583.2 %all-to-all-start.1 = ((bf16[2,1024,384]{2,0,1:T(2,128)(2,1)}), bf16[2,1024,384]{2,0,1:T(2,128)(2,1)S(1)}, u32[]{:S(2)}, u32[]{:S(2)}) async-start(bf16[2,1024,384]{2,0,1:T(2,128)(2,1)} %broadcast_select_fusion.1), calls=%async_computation.5 | async-start | bytes 3145728 | tf_op jit(solution)/shard_map/all_to_all | solution.py:456
  1766.0 495.7 %copy-start.88 = (bf16[384]{0:T(512)(128)(2,1)S(1)}, bf16[384]{0:T(512)(128)(2,1)}, u32[]{:S(2)}) copy-start(bf16[384]{0:T(512)(128)(2,1)} %get-tuple-element.1048) | copy-start | bytes 2308
  1766.0 495.7 %copy-start.91 = (bf16[768]{0:T(1024)(128)(2,1)S(1)}, bf16[768]{0:T(1024)(128)(2,1)}, u32[]{:S(2)}) copy-start(bf16[768]{0:T(1024)(128)(2,1)} %get-tuple-element.1163) | copy-start | bytes 4612
  (155 other events, 3026.1 us)
Sparse Core Ops, SparseCore 0:
  10.3 74.1 all-gather.14
  92.5 44.9 all-gather.12
  168.3 32.2 all-reduce.39
  202.6 52.2 all-gather.16
  256.9 50.3 all-gather.18
  436.9 66.6 reduce-scatter.14
  505.9 60.4 all-gather.22
  568.6 31.5 all-gather.20
  602.6 60.4 all-gather.24
  665.4 59.0 all-gather.26
  726.1 31.5 all-gather.28
  781.7 68.9 reduce-scatter.18
  862.6 34.0 all-gather.30
  1538.0 33.4 all-reduce.41
  1594.7 68.9 reduce-scatter.20
  1666.3 68.9 reduce-scatter.16
  1738.7 95.8 reduce-scatter.30
  1838.1 73.5 reduce-scatter.32
  1915.3 73.3 reduce-scatter.34
  1992.3 60.2 reduce-scatter.36
  2056.4 60.1 reduce-scatter.26
  2120.1 67.9 reduce-scatter.28
  2191.6 68.2 reduce-scatter.24
  2263.2 68.2 reduce-scatter.22
where the time goes:
time: 2380 us; the launch traced here: 2350 us
  waiting for transfers between devices  970 us (41%)
  local copies, waits for them, and re-layouts  517 us (22%)
  matrix products  480 us (20%)
  blocking collectives  188 us (8%)
  other arithmetic  140 us (6%)
    dynamic_update_slice x65, local copies, waits for them, and re-layouts, scan_blocks(): unused, result = lax.scan(jax.checkpoint(one_block), initial, shaped)  257 us
    reduce_scatter x4, waiting for transfers between devices, sum_features(): return lax.psum_scatter(terms, 'tensor', scatter_dimension=1, tiled=True)  202 us
    dot_general x20, matrix products, one_block(): inside = jnp.einsum('tsh,shp->thp', mixing, weighted, precision=HIGHEST)  195 us
    dot_general x14, matrix products, contract(): lax.dot_general(left, right, (((left_dim,), (right_dim,)), ((), ())), pre...  103 us
    unnamed x2, blocking collectives  81.3 us
    reduce_scatter x1, waiting for transfers between devices, per_device(): lax.psum_scatter(ffn_up_grad.astype(jnp.bfloat16), 'dp', scatter_dimensio...  75.1 us
    reduce_scatter x1, waiting for transfers between devices, per_device(): lax.psum_scatter(down_grad.astype(jnp.bfloat16), 'dp', scatter_dimension=...  75 us
    reduce_scatter x1, waiting for transfers between devices, per_device(): lax.psum_scatter(out_weight_grad.astype(jnp.bfloat16), 'dp', scatter_dime...  70.2 us
  transfers between devices with their start and end apart: 26, of which 19 were waited for; matrix products, arithmetic and copies ran while one was open for 26% of the time, Pallas kernels for 0%

commit v1 on v0

v1 whole, which is shorter than its diff:
```python
import functools

import jax
import jax.numpy as jnp
from jax import lax
from jax.experimental import pallas as pl
from jax.experimental.pallas import tpu as pltpu
from jax.sharding import PartitionSpec as P

D = 1536
NS = 16
KC = 4
R = 96
LMAX = 1024
SPG = 2
GCAP = 1280
HEAD_WIDTH = 24


HIGHEST = lax.Precision.HIGHEST
EPSILON = 1e-06


def contract(left, right, left_dim, right_dim):
    return lax.dot_general(
        left, right, (((left_dim,), (right_dim,)), ((), ())), preferred_element_type=jnp.float32
    )


def conv_silu(inner_pre, conv_taps, conv_bias, segment):
    row_count = inner_pre.shape[0]
    running_sum = conv_bias + conv_taps[KC - 1] * inner_pre
    for offset in range(1, KC):
        earlier = jnp.concatenate(
            [
                jnp.zeros((offset, inner_pre.shape[1]), inner_pre.dtype),
                inner_pre[: row_count - offset],
            ],
            axis=0,
        )
        linked = jnp.concatenate(
            [jnp.zeros((offset,), jnp.bool_), segment[offset:] == segment[: row_count - offset]]
        )
        running_sum = running_sum + conv_taps[KC - 1 - offset] * jnp.where(
            linked[:, None], earlier, 0.0
        )
    return jax.nn.silu(running_sum)


LANES = 128
CHUNK = 128


def mixed_dot(left, right, left_dim=1, right_dim=0):
    return lax.dot_general(
        left.astype(jnp.bfloat16),
        right.astype(jnp.bfloat16),
        (((left_dim,), (right_dim,)), ((), ())),
        preferred_element_type=jnp.float32,
    )


def fine_dot(left, right, left_dim=1, right_dim=0):
    left_high, right_high = left.astype(jnp.bfloat16), right.astype(jnp.bfloat16)
    left_low = (left - left_high.astype(jnp.float32)).astype(jnp.bfloat16)
    right_low = (right - right_high.astype(jnp.float32)).astype(jnp.bfloat16)
    return (
        mixed_dot(left_high, right_high, left_dim, right_dim)
        + mixed_dot(left_high, right_low, left_dim, right_dim)
        + mixed_dot(left_low, right_high, left_dim, right_dim)
    )


def exact_dot(left, right, left_dim=1, right_dim=0):
    return lax.dot_general(
        left,
        right,
        (((left_dim,), (right_dim,)), ((), ())),
        precision=HIGHEST,
        preferred_element_type=jnp.float32,
    )


def split_dot(values, zero_one, right_dim, terms):
    total = None
    rest = values
    for term in range(terms):
        part = rest.astype(jnp.bfloat16)
        product = mixed_dot(part, zero_one, 1, right_dim)
        total = product if total is None else total + product
        if term + 1 < terms:
            rest = rest - part.astype(jnp.float32)
    return total


def tile_heads(tile, head_width, channel_count):
    first = tile * LANES
    heads = []
    for head in range(channel_count // head_width):
        low = max(head * head_width - first, 0)
        high = min((head + 1) * head_width - first, LANES)
        if low < high:
            heads.append((head, low, high))
    return heads


def chunk_setup(bounds_ref, chunk_index, proj, params_ref, step_w):
    first_row = chunk_index * CHUNK
    row_axis = lax.broadcasted_iota(jnp.int32, (CHUNK, LANES), 0)
    lane_axis = lax.broadcasted_iota(jnp.int32, (CHUNK, LANES), 1)

    def segment_of(position):
        result = jnp.int32(0)
        for edge in range(SPG):
            result = result + (position >= bounds_ref[edge]).astype(jnp.int32)
        return result

    row_seg = segment_of(row_axis + first_row)
    lane_seg = segment_of(lane_axis + first_row)
    seg_in = segment_of(jnp.maximum(first_row - 1, 0))
    seg_last = segment_of(first_row + CHUNK - 1)
    same = row_seg == lane_seg
    lower = row_axis >= lane_axis
    carried = (row_seg == seg_in).astype(jnp.float32)
    tail = (row_seg == seg_last).astype(jnp.float32)
    keep = (seg_last == seg_in).astype(jnp.float32)

    def group_of(index):
        return (index >= R).astype(jnp.int32) + (index >= R + NS).astype(jnp.int32)

    group_row, group_lane = group_of(row_axis), group_of(lane_axis)
    group_mean = jnp.where(
        group_row == group_lane, jnp.where(group_lane == 0, 1.0 / R, 1.0 / NS), 0.0
    )
    gains = params_ref[0:1, :]
    step_b = params_ref[1:2, :]
    rate = jnp.exp(params_ref[2:3, :])
    scale = lax.rsqrt(exact_dot(proj * proj, group_mean) + EPSILON)
    unit = proj * scale
    normed = unit * gains
    step_pre = exact_dot(normed, step_w) + step_b
    step_size = jnp.maximum(step_pre, 0.0) + jnp.log1p(jnp.exp(-jnp.abs(step_pre)))
    log_decay = -step_size * rate
    cumulative = exact_dot(lower.astype(jnp.float32), log_decay)
    low_lanes = lane_axis < NS
    input_b = jnp.where(low_lanes, pltpu.roll(normed, LANES - R, 1), 0.0)
    output_c = jnp.where(low_lanes, pltpu.roll(normed, LANES - R - NS, 1), 0.0)
    last = cumulative[CHUNK - 1 : CHUNK, :]
    return dict(
        lane_axis=lane_axis,
        same=same,
        lower=lower,
        group_mean=group_mean,
        gains=gains,
        rate=rate,
        scale=scale,
        unit=unit,
        normed=normed,
        step_pre=step_pre,
        step_size=step_size,
        log_decay=log_decay,
        cumulative=cumulative,
        input_b=input_b,
        output_c=output_c,
        head_in=jnp.exp(cumulative) * carried,
        head_out=jnp.exp(last - cumulative) * tail,
        head_keep=jnp.exp(last) * keep,
    )


def scan_forward_kernel(
    head_width,
    bounds_ref,
    proj_ref,
    conv_ref,
    gate_ref,
    params_ref,
    step_w_ref,
    skip_ref,
    expand_ref,
    gated_ref,
    scanned_ref,
    states_ref,
    state_ref,
):
    chunk_index = pl.program_id(0)

    @pl.when(chunk_index == 0)
    def _():
        state_ref[...] = jnp.zeros_like(state_ref)

    state = state_ref[...]
    states_ref[0] = state
    prep = chunk_setup(bounds_ref, chunk_index, proj_ref[...], params_ref, step_w_ref[...])
    expand = expand_ref[...]
    channel_count = conv_ref.shape[1]
    conv_in = conv_ref[...].astype(jnp.float32)
    weighted = split_dot(prep["step_size"], expand, 0, 2) * conv_in
    weighted_parts = [weighted.astype(jnp.bfloat16)]
    weighted_parts.append((weighted - weighted_parts[0].astype(jnp.float32)).astype(jnp.bfloat16))
    tail_values = split_dot(prep["head_out"], expand, 0, 2) * weighted
    keep = split_dot(jnp.broadcast_to(prep["head_keep"], (8, LANES)), expand, 0, 2)[0:1, :]
    b_rows = prep["input_b"].T[0:NS, :]
    state_ref[...] = keep * state + fine_dot(b_rows, tail_values)
    scores = exact_dot(prep["output_c"], prep["input_b"], 1, 1)
    scores = jnp.where(prep["same"] & prep["lower"], scores, 0.0)
    from_state = split_dot(prep["head_in"], expand, 0, 2) * fine_dot(
        prep["output_c"][:, 0:NS], state
    )
    cumulative = prep["cumulative"]
    cumulative_t = cumulative.T
    lane_axis = prep["lane_axis"]
    for tile in range(channel_count // LANES):
        columns = slice(tile * LANES, (tile + 1) * LANES)
        parts = [part[:, columns] for part in weighted_parts]
        mixing, masked = [], [[], []]
        for head, low, high in tile_heads(tile, head_width, channel_count):
            spread = cumulative[:, head : head + 1] - cumulative_t[head : head + 1, :]
            mixing.append((scores * jnp.exp(jnp.minimum(spread, 0.0))).astype(jnp.bfloat16))
            own = (lane_axis >= low) & (lane_axis < high)
            for part, kept in zip(parts, masked):
                kept.append(jnp.where(own, part, jnp.zeros_like(part)))
        mixing = jnp.concatenate(mixing, axis=1)
        inside = mixed_dot(mixing, jnp.concatenate(masked[0], axis=0)) + mixed_dot(
            mixing, jnp.concatenate(masked[1], axis=0)
        )
        scanned = inside + from_state[:, columns]
        scanned_ref[:, columns] = scanned
        gate = gate_ref[:, columns].astype(jnp.float32)
        mixed_out = scanned + skip_ref[:, columns] * conv_in[:, columns]
        gated_ref[:, columns] = (mixed_out * (gate / (1.0 + jnp.exp(-gate)))).astype(jnp.bfloat16)


def scan_backward_kernel(
    head_width,
    bounds_ref,
    upstream_ref,
    proj_ref,
    conv_ref,
    gate_ref,
    scanned_ref,
    states_ref,
    params_ref,
    step_w_ref,
    skip_ref,
    expand_ref,
    proj_grad_ref,
    conv_grad_ref,
    gate_grad_ref,
    step_w_grad_ref,
    rows_grad_ref,
    skip_grad_ref,
    state_grad_ref,
):
    step = pl.program_id(0)
    chunk_index = pl.num_programs(0) - 1 - step

    @pl.when(step == 0)
    def _():
        state_grad_ref[...] = jnp.zeros_like(state_grad_ref)
        step_w_grad_ref[...] = jnp.zeros_like(step_w_grad_ref)
        rows_grad_ref[...] = jnp.zeros_like(rows_grad_ref)
        skip_grad_ref[...] = jnp.zeros_like(skip_grad_ref)

    state = states_ref[0]
    state_grad = state_grad_ref[...]
    step_w = step_w_ref[...]
    prep = chunk_setup(bounds_ref, chunk_index, proj_ref[...], params_ref, step_w)
    expand = expand_ref[...]
    channel_count = conv_ref.shape[1]
    conv_in = conv_ref[...].astype(jnp.float32)
    step_wide = split_dot(prep["step_size"], expand, 0, 2)
    weighted = step_wide * conv_in
    weighted_low = weighted.astype(jnp.bfloat16)
    out_wide = split_dot(prep["head_out"], expand, 0, 2)
    in_wide = split_dot(prep["head_in"], expand, 0, 2)
    keep = split_dot(jnp.broadcast_to(prep["head_keep"], (8, LANES)), expand, 0, 2)[0:1, :]
    tail_values = out_wide * weighted
    b_rows = prep["input_b"].T[0:NS, :]
    c_rows = prep["output_c"].T[0:NS, :]
    state_out = keep * state + fine_dot(b_rows, tail_values)

    gate = gate_ref[...].astype(jnp.float32)
    upstream = upstream_ref[...].astype(jnp.float32)
    scanned = scanned_ref[...]
    logistic = 1.0 / (1.0 + jnp.exp(-gate))
    mixed_grad = upstream * (gate * logistic)
    mixed_out = scanned + skip_ref[...] * conv_in
    gate_grad_ref[...] = (
        upstream * mixed_out * (logistic * (1.0 + gate * (1.0 - logistic)))
    ).astype(jnp.bfloat16)
    skip_grad_ref[0:1, :] += jnp.sum(mixed_grad * conv_in, axis=0, keepdims=True)
    grad_low = mixed_grad.astype(jnp.bfloat16)
    grad_round = grad_low.astype(jnp.float32)

    pad_rows = jnp.zeros((LANES - NS, channel_count), jnp.float32)
    state_tall = jnp.concatenate([state, pad_rows], axis=0)
    state_grad_tall = jnp.concatenate([state_grad, pad_rows], axis=0)
    from_in = in_wide * grad_round
    c_grad = mixed_dot(from_in, state_tall, 1, 1)
    b_grad = mixed_dot(tail_values, state_grad_tall, 1, 1)
    weighted_grad = out_wide * fine_dot(prep["input_b"][:, 0:NS], state_grad)
    state_grad_ref[...] = keep * state_grad + fine_dot(c_rows, from_in)

    row_axis = lax.broadcasted_iota(jnp.int32, (CHUNK, LANES), 0)
    upper = prep["same"] & (row_axis <= prep["lane_axis"])
    scores_t = jnp.where(upper, exact_dot(prep["input_b"], prep["output_c"], 1, 1), 0.0)
    cumulative = prep["cumulative"]
    cumulative_t = cumulative.T
    lane_axis = prep["lane_axis"]
    scores_grad = jnp.zeros((CHUNK, LANES), jnp.float32)
    inside_grads = []
    for tile in range(channel_count // LANES):
        columns = slice(tile * LANES, (tile + 1) * LANES)
        values = weighted_low[:, columns]
        grads = grad_low[:, columns]
        mixing, masked_values, masked_grads, decays = [], [], [], []
        for head, low, high in tile_heads(tile, head_width, channel_count):
            spread = cumulative_t[head : head + 1, :] - cumulative[:, head : head + 1]
            decay = jnp.exp(jnp.minimum(spread, 0.0))
            decays.append(decay)
            mixing.append((scores_t * decay).astype(jnp.bfloat16))
            own = (lane_axis >= low) & (lane_axis < high)
            masked_values.append(jnp.where(own, values, jnp.zeros_like(values)))
            masked_grads.append(jnp.where(own, grads, jnp.zeros_like(grads)))
        pair_grads = mixed_dot(jnp.concatenate(masked_values, axis=0), grads, 1, 1)
        for place, decay in enumerate(decays):
            scores_grad = scores_grad + decay * pair_grads[place * CHUNK : (place + 1) * CHUNK, :]
        inside_grads.append(
            mixed_dot(jnp.concatenate(mixing, axis=1), jnp.concatenate(masked_grads, axis=0))
        )
    weighted_grad = weighted_grad + jnp.concatenate(inside_grads, axis=1)
    scores_grad = jnp.where(upper, scores_grad, 0.0)
    b_grad = b_grad + mixed_dot(scores_grad, prep["output_c"])
    c_grad = c_grad + mixed_dot(scores_grad.T, prep["input_b"])
    conv_grad_ref[...] = mixed_grad * skip_ref[...] + weighted_grad * step_wide
    spread_grad = split_dot(
        grad_round * scanned - weighted * weighted_grad, expand, 1, 3
    )
    edge = jnp.broadcast_to(
        jnp.sum(state_out * state_grad, axis=0, keepdims=True), (8, channel_count)
    )
    edge_grad = split_dot(edge, expand, 1, 3)[0:1, :]
    spread_grad = spread_grad + jnp.where(row_axis == CHUNK - 1, edge_grad, 0.0)
    decay_grad = exact_dot((row_axis <= lane_axis).astype(jnp.float32), spread_grad)
    step_grad = split_dot(weighted_grad * conv_in, expand, 1, 2) - decay_grad * prep["rate"]
    step_pre = prep["step_pre"]
    pre_grad = step_grad / (1.0 + jnp.exp(-step_pre))
    step_w_grad_ref[...] += exact_dot(prep["normed"].T, pre_grad)
    normed_grad = (
        exact_dot(pre_grad, step_w, 1, 1)
        + pltpu.roll(b_grad, R, 1)
        + pltpu.roll(c_grad, R + NS, 1)
    )
    unit = prep["unit"]
    rows_grad_ref[0:1, :] += jnp.sum(normed_grad * unit, axis=0, keepdims=True)
    rows_grad_ref[1:2, :] += jnp.sum(pre_grad, axis=0, keepdims=True)
    rows_grad_ref[2:3, :] += jnp.sum(decay_grad * prep["log_decay"], axis=0, keepdims=True)
    unit_grad = normed_grad * prep["gains"]
    along = exact_dot(unit_grad * unit, prep["group_mean"], 1, 1)
    proj_grad_ref[...] = prep["scale"] * (unit_grad - unit * along)


def scan_operands(step_weight, step_bias, log_rate, skip_gain, proj_gains, head_width):
    head_count = step_bias.shape[0]
    channel_count = skip_gain.shape[0]

    def lane_row(values):
        return jnp.pad(values.astype(jnp.float32), (0, LANES - values.shape[0]))[None, :]

    params = jnp.concatenate(
        [
            lane_row(proj_gains),
            lane_row(step_bias),
            lane_row(log_rate),
            jnp.zeros((5, LANES), jnp.float32),
        ],
        axis=0,
    )
    step_w = jnp.pad(
        step_weight.astype(jnp.float32), ((0, LANES - R), (0, LANES - head_count))
    )
    skip = skip_gain.astype(jnp.float32)[None, :]
    owner = lax.broadcasted_iota(jnp.int32, (LANES, channel_count), 1) // head_width
    head = lax.broadcasted_iota(jnp.int32, (LANES, channel_count), 0)
    return params, step_w, skip, (owner == head).astype(jnp.bfloat16)


def whole(shape):
    return pl.BlockSpec(shape, lambda i, *_: (0,) * len(shape))


def scan_forward(bounds, projected, conv_out, gate_pre, operands, head_width):
    params, step_w, skip, expand = operands
    rows, channels = conv_out.shape
    chunks = rows // CHUNK

    def chunk_rows(width):
        return pl.BlockSpec((CHUNK, width), lambda i, *_: (i, 0))

    return pl.pallas_call(
        functools.partial(scan_forward_kernel, head_width),
        out_shape=(
            jax.ShapeDtypeStruct((rows, channels), jnp.bfloat16),
            jax.ShapeDtypeStruct((rows, channels), jnp.float32),
            jax.ShapeDtypeStruct((chunks, NS, channels), jnp.float32),
        ),
        grid_spec=pltpu.PrefetchScalarGridSpec(
            num_scalar_prefetch=1,
            grid=(chunks,),
            in_specs=[
                chunk_rows(LANES),
                chunk_rows(channels),
                chunk_rows(channels),
                whole(params.shape),
                whole(step_w.shape),
                whole(skip.shape),
                whole(expand.shape),
            ],
            out_specs=[
                chunk_rows(channels),
                chunk_rows(channels),
                pl.BlockSpec((1, NS, channels), lambda i, *_: (i, 0, 0)),
            ],
            scratch_shapes=[pltpu.VMEM((NS, channels), jnp.float32)],
        ),
        cost_estimate=pl.CostEstimate(
            flops=40_000_000_000, bytes_accessed=14_000_000, transcendentals=6_000_000
        ),
        name="scan_forward",
    )(bounds, projected, conv_out, gate_pre, params, step_w, skip, expand)


def scan_backward(bounds, upstream, projected, conv_out, gate_pre, scanned, states, operands, head_width):
    params, step_w, skip, expand = operands
    rows, channels = conv_out.shape
    chunks = rows // CHUNK

    def chunk_rows(width):
        return pl.BlockSpec((CHUNK, width), lambda i, *_: (chunks - 1 - i, 0))

    return pl.pallas_call(
        functools.partial(scan_backward_kernel, head_width),
        out_shape=(
            jax.ShapeDtypeStruct((rows, LANES), jnp.float32),
            jax.ShapeDtypeStruct((rows, channels), jnp.float32),
            jax.ShapeDtypeStruct((rows, channels), jnp.bfloat16),
            jax.ShapeDtypeStruct((LANES, LANES), jnp.float32),
            jax.ShapeDtypeStruct((8, LANES), jnp.float32),
            jax.ShapeDtypeStruct((8, channels), jnp.float32),
        ),
        grid_spec=pltpu.PrefetchScalarGridSpec(
            num_scalar_prefetch=1,
            grid=(chunks,),
            in_specs=[
                chunk_rows(channels),
                chunk_rows(LANES),
                chunk_rows(channels),
                chunk_rows(channels),
                chunk_rows(channels),
                pl.BlockSpec((1, NS, channels), lambda i, *_: (chunks - 1 - i, 0, 0)),
                whole(params.shape),
                whole(step_w.shape),
                whole(skip.shape),
                whole(expand.shape),
            ],
            out_specs=[
                chunk_rows(LANES),
                chunk_rows(channels),
                chunk_rows(channels),
                whole((LANES, LANES)),
                whole((8, LANES)),
                whole((8, channels)),
            ],
            scratch_shapes=[pltpu.VMEM((NS, channels), jnp.float32)],
        ),
        cost_estimate=pl.CostEstimate(
            flops=80_000_000_000, bytes_accessed=24_000_000, transcendentals=8_000_000
        ),
        name="scan_backward",
    )(bounds, upstream, projected, conv_out, gate_pre, scanned, states, params, step_w, skip, expand)


PLACES = (0, 2, 1, 3)


def swap_pairs(size, flip):
    return [(index, index ^ flip) for index in range(size)]


class Wires:
    def __init__(self, dp_size, tensor_size):
        self.dp_size = dp_size
        self.tensor_size = tensor_size
        self.staged = tensor_size == 4 and dp_size == 8
        self.group = lax.axis_index("dp")
        self.lane = lax.axis_index("tensor")
        self.outer = self.group // 2
        self.inner = self.group % 2
        self.turn = jnp.bitwise_xor(self.lane, self.outer)

    def over_tensor(self, values, flip):
        return lax.ppermute(values, "tensor", swap_pairs(self.tensor_size, flip))

    def over_dp(self, values, flip):
        return lax.ppermute(values, "dp", swap_pairs(self.dp_size, flip))

    def place_of(self, distance):
        block = jnp.bitwise_xor(self.turn, distance)
        return (block & 1) * 2 + (block >> 1)


    def gather_features(self, values):
        if not self.staged:
            return lax.all_gather(values, "tensor", axis=1, tiled=True)
        across = self.over_tensor(values, 2)
        beside = self.over_tensor(values, 1)
        diagonal = self.over_tensor(across, 1)
        return jnp.concatenate([values, across, beside, diagonal], axis=1)

    def sum_features(self, project):
        width = D // self.tensor_size
        if not self.staged:
            return lax.psum_scatter(
                project(slice(0, D)), "tensor", scatter_dimension=1, tiled=True
            )
        sent = project(slice(2 * width, 4 * width)).astype(jnp.bfloat16)
        kept = project(slice(0, 2 * width))
        total = kept + self.over_tensor(sent, 1).astype(jnp.float32)
        across = self.over_tensor(total[:, width:].astype(jnp.bfloat16), 2)
        return total[:, :width] + across.astype(jnp.float32)

    def sum_small(self, values):
        if not self.staged:
            return lax.psum(values, "tensor")
        values = values + self.over_tensor(values, 1)
        return values + self.over_tensor(values, 2)

    def sum_rows(self, values, wire):
        if not self.staged:
            return lax.psum(values.astype(wire), "tensor").astype(jnp.float32)
        half = values.shape[0] // 2
        core = self.lane % 2
        kept = lax.dynamic_slice_in_dim(values, core * half, half)
        sent = lax.dynamic_slice_in_dim(values, (1 - core) * half, half)
        total = kept + self.over_tensor(sent.astype(wire), 1).astype(jnp.float32)
        total = total + self.over_tensor(total.astype(wire), 2).astype(jnp.float32)
        other = self.over_tensor(total.astype(wire), 1).astype(jnp.float32)
        total = total.astype(wire).astype(jnp.float32)
        first = jnp.where(core == 0, total, other)
        second = jnp.where(core == 0, other, total)
        return jnp.concatenate([first, second], axis=0)


    def gather_pieces(self, shard):
        same = [shard] + [self.over_dp(shard, 2 * distance) for distance in range(1, self.dp_size // 2)]
        return same, [self.over_dp(piece, 1) for piece in same]

    def gather_weights(self, shards):
        if not self.staged:
            return [lax.all_gather(shard, "dp", axis=0, tiled=True) for shard in shards], shards[0]
        widths = [shard.shape[1] for shard in shards]
        shard = shards[0] if len(shards) == 1 else jnp.concatenate(shards, axis=1)
        same, other = self.gather_pieces(shard)
        places = jnp.stack([self.place_of(distance) for distance in range(4)] + [self.inner])
        return arrange_weights(places.astype(jnp.int32), same, other, widths), other[3]

    def sum_weights(self, grad):
        if not self.staged:
            return lax.psum_scatter(
                grad.astype(jnp.bfloat16), "dp", scatter_dimension=0, tiled=True
            ).astype(jnp.float32)
        width = grad.shape[1]
        blocks = grad.reshape(4, 2, D // 8, width)
        sent = lax.dynamic_index_in_dim(blocks, 1 - self.inner, 1, keepdims=False)
        kept = lax.dynamic_index_in_dim(blocks, self.inner, 1, keepdims=False)
        got = self.over_dp(sent.astype(jnp.bfloat16), 1)
        total = (kept.astype(jnp.float32) + got.astype(jnp.float32)).astype(jnp.bfloat16)
        pieces = [
            lax.dynamic_index_in_dim(total, self.place_of(distance), 0, keepdims=False)
            for distance in range(4)
        ]
        result = pieces[0].astype(jnp.float32)
        for distance in range(1, 4):
            result = result + self.over_dp(pieces[distance], 2 * distance).astype(jnp.float32)
        return result

    def gather_rows(self, block):
        if not self.staged:
            return lax.all_gather(block, "dp", axis=0, tiled=False)
        same = jnp.stack(
            [block] + [self.over_dp(block, 2 * distance) for distance in range(1, 4)]
        )
        other = self.over_dp(same, 1)
        both = jnp.stack([same, other], axis=1).reshape((8,) + block.shape)
        index = jnp.arange(8, dtype=jnp.int32)
        return both[jnp.bitwise_xor(index, self.group)]

    def sum_blocks(self, blocks):
        if not self.staged:
            return lax.psum_scatter(blocks, "dp", scatter_dimension=0, tiled=False)
        paired = blocks.reshape((4, 2) + blocks.shape[1:])
        sent = lax.dynamic_index_in_dim(paired, 1 - self.inner, 1, keepdims=False)
        kept = lax.dynamic_index_in_dim(paired, self.inner, 1, keepdims=False)
        total = kept + self.over_dp(sent, 1)
        result = lax.dynamic_index_in_dim(total, self.outer, 0, keepdims=False)
        for distance in range(1, 4):
            piece = lax.dynamic_index_in_dim(
                total, jnp.bitwise_xor(self.outer, distance), 0, keepdims=False
            )
            result = result + self.over_dp(piece, 2 * distance)
        return result

    def exchange(self, blocks):
        got = [blocks[0]]
        for flip in range(1, self.dp_size):
            got.append(self.over_dp(blocks[flip], flip))
        return jnp.stack(got)


def arrange_kernel(widths, places_ref, *refs):
    same, other, outs = refs[:4], refs[4:8], refs[8:]
    step = pl.program_id(0)
    rows = same[0].shape[0]
    first = pl.multiple_of(places_ref[4] * rows, 16)
    second = pl.multiple_of((1 - places_ref[4]) * rows, 16)
    for distance in range(4):

        @pl.when(step == distance)
        def _(distance=distance):
            start = 0
            for out, width in zip(outs, widths):
                columns = slice(start, start + width)
                out[pl.ds(first, rows), :] = same[distance][:, columns]
                out[pl.ds(second, rows), :] = other[distance][:, columns]
                start += width


def arrange_weights(places, same, other, widths):
    rows, width = same[0].shape
    return pl.pallas_call(
        functools.partial(arrange_kernel, widths),
        out_shape=[jax.ShapeDtypeStruct((8 * rows, part), jnp.bfloat16) for part in widths],
        grid_spec=pltpu.PrefetchScalarGridSpec(
            num_scalar_prefetch=1,
            grid=(4,),
            in_specs=[whole((rows, width))] * 8,
            out_specs=[
                pl.BlockSpec((2 * rows, part), lambda i, places_ref: (places_ref[i], 0))
                for part in widths
            ],
        ),
        cost_estimate=pl.CostEstimate(
            flops=0, bytes_accessed=32 * rows * width, transcendentals=0
        ),
        name="arrange_weights",
    )(places, *same, *other)


def pack_rows(parts):
    blocks = parts[0].shape[0]
    flat = jnp.concatenate([part.reshape(blocks, -1) for part in parts], axis=1)
    size = flat.shape[1]
    rows = -(-size // (16 * LANES)) * 16
    flat = jnp.pad(flat, ((0, 0), (0, rows * LANES - size)))
    return flat.reshape(blocks, rows, LANES)


def unpack_rows(packed, shapes):
    blocks = packed.shape[0]
    flat = packed.reshape(blocks, -1)
    parts, start = [], 0
    for shape in shapes:
        size = 1
        for extent in shape:
            size *= extent
        parts.append(flat[:, start : start + size].reshape((blocks,) + shape))
        start += size
    return parts


def after(values, earlier):
    return lax.optimization_barrier((values, earlier))[0]


def row_scale(wires, values):
    mean_square = wires.sum_small(jnp.sum(values * values, axis=1).reshape(-1, LANES)) / D
    return lax.rsqrt(mean_square + EPSILON).reshape(-1)


def norm_back(wires, values, inverse, gain, upstream):
    normed = values * inverse[:, None]
    gain_grad = jnp.sum(upstream * normed, axis=0)
    scaled = upstream * gain
    along = jnp.sum(scaled * normed, axis=1).reshape(-1, LANES)
    along = wires.sum_small(along).reshape(-1) / D
    return inverse[:, None] * (scaled - normed * along[:, None]), gain_grad


def per_device(
    dp_size,
    tensor_size,
    tokens,
    out_grad,
    lengths,
    deal,
    mixer_gain,
    inner_weight,
    gate_weight,
    conv_taps,
    conv_bias,
    proj_weight,
    proj_gains,
    step_weight,
    step_bias,
    log_rate,
    skip_gain,
    out_weight,
    ffn_gain,
    ffn_gate,
    ffn_up,
    ffn_down,
):
    wires = Wires(dp_size, tensor_size)
    group = wires.group
    bf16, f32 = jnp.bfloat16, jnp.float32

    packed_lengths = lengths[deal]
    group_lengths = lax.dynamic_slice_in_dim(packed_lengths, group * SPG, SPG)
    starts = jnp.cumsum(group_lengths) - group_lengths
    filled = jnp.sum(group_lengths)
    bounds = jnp.concatenate([starts[1:], filled[None]]).astype(jnp.int32)
    row_ids = jnp.arange(GCAP, dtype=jnp.int32)
    live_rows = row_ids < filled
    segment = jnp.sum((row_ids[:, None] >= bounds[None, :]).astype(jnp.int32), axis=1)
    slot = jnp.minimum(segment, SPG - 1)
    position = row_ids - jnp.where(slot == 0, 0, starts[slot])
    span = LMAX // dp_size
    ranks = jnp.arange(dp_size, dtype=jnp.int32)
    source_rows = (
        jnp.bitwise_xor(position // span, group) * (SPG * span) + slot * span + position % span
    )
    source_rows = jnp.where(live_rows, source_rows, 0)

    dealt = deal.reshape(dp_size, SPG)[jnp.bitwise_xor(ranks, group)]
    arrived = wires.exchange(tokens[dealt.reshape(-1)].reshape((dp_size, SPG) + tokens.shape[1:]))
    flat_rows = arrived.reshape(dp_size * SPG * span, -1)
    packed = jnp.where(live_rows[:, None], flat_rows[source_rows], 0.0).astype(f32)

    small_shapes = [
        proj_weight.shape,
        mixer_gain.shape,
        conv_taps.shape,
        conv_bias.shape,
        proj_gains.shape,
        step_weight.shape,
        step_bias.shape,
        log_rate.shape,
        skip_gain.shape,
        ffn_gain.shape,
    ]
    small = pack_rows(
        [
            part[None]
            for part in (
                proj_weight,
                mixer_gain,
                conv_taps,
                conv_bias,
                proj_gains,
                step_weight,
                step_bias,
                log_rate,
                skip_gain,
                ffn_gain,
            )
        ]
    )[0]
    small = unpack_rows(wires.gather_rows(small), small_shapes)

    def along_last(part):
        return jnp.moveaxis(part, 0, -2).reshape(part.shape[1:-1] + (-1,))

    proj_all = small[0].reshape(-1, small[0].shape[-1])
    gain_all, taps_all, bias_all, gains_all, step_w_all, step_b_all, rate_all, skip_all, ffn_gain_all = [
        along_last(part).astype(f32) for part in small[1:]
    ]

    (inner_all, gate_all), mark = wires.gather_weights(
        list(after((inner_weight, gate_weight), arrived))
    )
    (out_all,), mark = wires.gather_weights([after(out_weight.T, mark)])
    (ffn_gate_all, ffn_up_all), mark = wires.gather_weights(
        list(after((ffn_gate, ffn_up), mark))
    )
    (ffn_down_all,), mark = wires.gather_weights([after(ffn_down.T, mark)])

    inverse_in = row_scale(wires, packed)
    mixer_rows = wires.gather_features((packed * inverse_in[:, None] * gain_all).astype(bf16))
    inner_pre = contract(mixer_rows, inner_all, 1, 0)
    gate_pre = contract(mixer_rows, gate_all, 1, 0)
    conv_out = conv_silu(inner_pre, taps_all, bias_all, segment).astype(bf16)
    projected = wires.sum_rows(contract(conv_out, proj_all, 1, 0), f32)
    operands = scan_operands(step_w_all, step_b_all, rate_all, skip_all, gains_all, HEAD_WIDTH)
    gated, scanned, states = scan_forward(
        bounds, projected, conv_out, gate_pre, operands, HEAD_WIDTH
    )
    residual = packed + wires.sum_features(lambda rows: contract(gated, out_all[rows], 1, 1))

    inverse_mid = row_scale(wires, residual)
    ffn_rows = wires.gather_features((residual * inverse_mid[:, None] * ffn_gain_all).astype(bf16))
    gate_ffn = contract(ffn_rows, ffn_gate_all, 1, 0)
    up_ffn = contract(ffn_rows, ffn_up_all, 1, 0)
    logistic = jax.nn.sigmoid(gate_ffn)
    activated = gate_ffn * logistic
    hidden = (activated * up_ffn).astype(bf16)
    final_rows = residual + wires.sum_features(
        lambda rows: contract(hidden, ffn_down_all[rows], 1, 1)
    )
    output = jnp.where(live_rows[:, None], final_rows, 0.0).astype(bf16)

    out_cot = jnp.where(live_rows[:, None], out_grad, 0.0).astype(bf16)
    cot_rows = wires.gather_features(out_cot)
    hidden_grad = contract(cot_rows, ffn_down_all, 1, 0)
    gate_grad = (hidden_grad * up_ffn * logistic * (1.0 + gate_ffn * (1.0 - logistic))).astype(bf16)
    up_grad = (hidden_grad * activated).astype(bf16)
    mid_grad = wires.sum_features(
        lambda rows: contract(gate_grad, ffn_gate_all[rows], 1, 1)
        + contract(up_grad, ffn_up_all[rows], 1, 1)
    )
    ffn_down_grad = wires.sum_weights(contract(cot_rows, hidden, 0, 0).astype(bf16)).T
    ffn_gate_grad = wires.sum_weights(contract(ffn_rows, gate_grad, 0, 0).astype(bf16))
    ffn_up_grad = wires.sum_weights(contract(ffn_rows, up_grad, 0, 0).astype(bf16))
    mid_back, ffn_gain_grad = norm_back(wires, residual, inverse_mid, ffn_gain_all, mid_grad)
    residual_grad = out_cot.astype(f32) + mid_back

    branch_rows = wires.gather_features(residual_grad.astype(bf16))
    gated_grad = contract(branch_rows, out_all, 1, 0)
    out_weight_grad = wires.sum_weights(contract(branch_rows, gated, 0, 0).astype(bf16)).T
    proj_part, conv_core_grad, gate_low, step_w_part, row_parts, skip_part = scan_backward(
        bounds, gated_grad, projected, conv_out, gate_pre, scanned, states, operands, HEAD_WIDTH
    )
    head_count = step_b_all.shape[0]
    gains_grad = wires.sum_small(row_parts)[0]
    proj_low = wires.sum_rows(proj_part, bf16).astype(bf16)
    conv_grad = conv_core_grad + contract(proj_low, proj_all, 1, 1)
    proj_weight_grad = contract(conv_out, proj_low, 0, 0)

    def conv_piece(inner_in, taps_in, bias_in):
        return conv_silu(inner_in, taps_in, bias_in, segment)

    unused_conv, conv_pull = jax.vjp(conv_piece, inner_pre, taps_all, bias_all)
    inner_grad, taps_grad, bias_grad = conv_pull(conv_grad)
    inner_low = inner_grad.astype(bf16)
    in_grad = wires.sum_features(
        lambda rows: contract(inner_low, inner_all[rows], 1, 1)
        + contract(gate_low, gate_all[rows], 1, 1)
    )
    gate_weight_grad = wires.sum_weights(contract(mixer_rows, gate_low, 0, 0).astype(bf16))
    inner_weight_grad = wires.sum_weights(contract(mixer_rows, inner_low, 0, 0).astype(bf16))
    in_back, mixer_gain_grad = norm_back(wires, packed, inverse_in, gain_all, in_grad)

    grad_packed = (residual_grad + in_back).astype(bf16)
    place = jnp.arange(span, dtype=jnp.int32)
    slot_position = (jnp.bitwise_xor(ranks, group) * span)[:, None, None] + place[None, None, :]
    slot_live = slot_position < group_lengths[None, :, None]
    slot_rows = jnp.where(slot_live, starts[None, :, None] + slot_position, 0).reshape(-1)
    leaving = jnp.where(slot_live.reshape(-1)[:, None], grad_packed[slot_rows], 0.0)
    returned = wires.exchange(leaving.reshape(dp_size, SPG, span, -1))
    inverse_deal = jnp.zeros_like(deal).at[deal].set(
        jnp.arange(deal.shape[0], dtype=jnp.int32)
    )
    came_from = jnp.bitwise_xor(inverse_deal // SPG, group) * SPG + inverse_deal % SPG
    tokens_grad = returned.reshape((dp_size * SPG, span, -1))[came_from]

    def by_index(part):
        split = part.reshape(part.shape[:-1] + (dp_size, part.shape[-1] // dp_size))
        return jnp.moveaxis(split, -2, 0)

    small_grads = pack_rows(
        [
            proj_weight_grad.reshape(dp_size, -1, proj_weight_grad.shape[1]),
            by_index(mixer_gain_grad),
            by_index(taps_grad),
            by_index(bias_grad),
            by_index(gains_grad),
            by_index(step_w_part[:R, :head_count]),
            by_index(row_parts[1, :head_count]),
            by_index(row_parts[2, :head_count]),
            by_index(skip_part[0]),
            by_index(ffn_gain_grad),
        ]
    )
    (
        proj_weight_grad,
        mixer_gain_grad,
        taps_grad,
        bias_grad,
        gains_grad,
        step_w_grad,
        step_b_grad,
        rate_grad,
        skip_grad,
        ffn_gain_grad,
    ) = [part[0] for part in unpack_rows(wires.sum_blocks(small_grads)[None], small_shapes)]
    return (
        output,
        tokens_grad,
        mixer_gain_grad,
        inner_weight_grad,
        gate_weight_grad,
        taps_grad,
        bias_grad,
        proj_weight_grad,
        gains_grad,
        step_w_grad,
        step_b_grad,
        rate_grad,
        skip_grad,
        out_weight_grad,
        ffn_gain_grad,
        ffn_gate_grad,
        ffn_up_grad,
        ffn_down_grad,
    )


def solution(mesh):
    return jax.shard_map(
        functools.partial(per_device, mesh.shape["dp"], mesh.shape["tensor"]),
        mesh=mesh,
        in_specs=(
            P(None, "dp", "tensor"),
            P("dp", "tensor"),
            P(),
            P(),
            P(("tensor", "dp")),
            P("dp", "tensor"),
            P("dp", "tensor"),
            P(None, ("tensor", "dp")),
            P(("tensor", "dp")),
            P(("tensor", "dp"), None),
            P("dp"),
            P(None, ("tensor", "dp")),
            P(("tensor", "dp")),
            P(("tensor", "dp")),
            P(("tensor", "dp")),
            P("tensor", "dp"),
            P(("tensor", "dp")),
            P("dp", "tensor"),
            P("dp", "tensor"),
            P("tensor", "dp"),
        ),
        out_specs=(
            P("dp", "tensor"),
            P(None, "dp", "tensor"),
            P(("tensor", "dp")),
            P("dp", "tensor"),
            P("dp", "tensor"),
            P(None, ("tensor", "dp")),
            P(("tensor", "dp")),
            P(("tensor", "dp"), None),
            P("dp"),
            P(None, ("tensor", "dp")),
            P(("tensor", "dp")),
            P(("tensor", "dp")),
            P(("tensor", "dp")),
            P("tensor", "dp"),
            P(("tensor", "dp")),
            P("dp", "tensor"),
            P("dp", "tensor"),
            P("tensor", "dp"),
        ),
        check_vma=False,
    )
```

time: 2380 us -> 913 us (0.38)
  waiting for transfers between devices: 970 us -> 391 us
  local copies, waits for them, and re-layouts: 517 us -> 68.9 us
  matrix products: 480 us -> 134 us
  blocking collectives: 188 us -> 0 us
  starting transfers between devices: 14.7 us -> 156 us
  Pallas kernels: 0 us -> 92.6 us
  other arithmetic: 140 us -> 63.9 us
    reduce_scatter x11 -> x0, waiting for transfers between devices: 654 us -> none  [the longest x4 202 us: sum_features(): return lax.psum_scatter(terms, 'tensor', scatter_dimension=1, tiled=True)]
    ppermute x0 -> x110, waiting for transfers between devices: none -> 391 us  [the longest x74 356 us: over_dp(): return lax.ppermute(values, 'dp', swap_pairs(self.dp_size, flip))]
    dot_general x100 -> x0, matrix products: 377 us -> none  [the longest x20 195 us: one_block(): inside = jnp.einsum('tsh,shp->thp', mixing, weighted, precision=HIGHEST)]
    dynamic_update_slice x65 -> x0, local copies, waits for them, and re-layouts: 257 us -> none  [scan_blocks(): unused, result = lax.scan(jax.checkpoint(one_block), initial, shaped)]
    all_gather x10 -> x0, waiting for transfers between devices: 222 us -> none  [the longest x4 67.1 us: gather_features(): return lax.all_gather(values, 'tensor', axis=1, tiled=True)]
    ppermute x0 -> x110, starting transfers between devices: none -> 156 us  [the longest x74 139 us: over_dp(): return lax.ppermute(values, 'dp', swap_pairs(self.dp_size, flip))]
    pallas_call x0 -> x6, Pallas kernels: none -> 92.6 us  [the longest x1 44.6 us: scan_backward(): pl.pallas_call(functools.partial(scan_backward_kernel, head_width), out_s...]
    unnamed x2 -> x0, blocking collectives: 81.3 us -> none
  transfers between devices with their start and end apart: 26 -> 110, of which waited for: 19 -> 43; matrix products, arithmetic and copies ran while one was open for 26% -> 20% of each run, Pallas kernels for 0% -> 2%
where the time goes in v1:
time: 913 us; the launch traced here: 909 us
  waiting for transfers between devices  391 us (43%)
  starting transfers between devices  156 us (17%)
  matrix products  134 us (15%)
  Pallas kernels  92.6 us (10%)
  local copies, waits for them, and re-layouts  68.9 us (8%)
  other arithmetic  63.9 us (7%)
    ppermute x74, waiting for transfers between devices, over_dp(): return lax.ppermute(values, 'dp', swap_pairs(self.dp_size, flip))  356 us
    ppermute x74, starting transfers between devices, over_dp(): return lax.ppermute(values, 'dp', swap_pairs(self.dp_size, flip))  139 us
    dot_general x27, matrix products, contract(): lax.dot_general(left, right, (((left_dim,), (right_dim,)), ((), ())), pre...  134 us
    pallas_call x1, Pallas kernels, scan_backward(): pl.pallas_call(functools.partial(scan_backward_kernel, head_width), out_s...  44.6 us
    ppermute x36, waiting for transfers between devices, over_tensor(): return lax.ppermute(values, 'tensor', swap_pairs(self.tensor_size, flip))  35.1 us
    pallas_call x1, Pallas kernels, scan_forward(): pl.pallas_call(functools.partial(scan_forward_kernel, head_width), out_sh...  26.3 us
    pallas_call x4, Pallas kernels, arrange_weights(): pl.pallas_call(functools.partial(arrange_kernel, widths), out_shape=[jax....  21.8 us
  transfers between devices with their start and end apart: 110, of which 43 were waited for; matrix products, arithmetic and copies ran while one was open for 20% of the time, Pallas kernels for 2%

profile of v1, /device:TPU:0, one launch (start us, length us, event | category | flops | bytes accessed | tf_op | source)
XLA Modules:
  0.0 909.4 jit_solution(11443275493377132057)
XLA Ops:
  39.9 11.4 %collective-permute-done.4 = bf16[2,128,384]{2,1,0:T(8,128)(2,1)S(1)} collective-permute-done((bf16[2,128,384]{2,1,0:T(8,128)(2,1)}, bf16[2,128,384]{2,1,0:T(8,128)(2,1)S(1)}, u32[]{:S(2)}, u32[]{:S(2)}) %collective-permute-start.4) | collective-permute-done | bytes 196640 | tf_op jit(solution)/shard_map/ppermute | solution.py:506
  64.0 8.4 collective-permute-start.16
  89.8 24.7 %collective-permute-done.17.refs_2_ = bf16[192,1536]{1,0:T(8,128)(2,1)} collective-permute-done((bf16[192,1536]{1,0:T(8,128)(2,1)S(1)}, bf16[192,1536]{1,0:T(8,128)(2,1)}, u32[]{:S(2)}, u32[]{:S(2)}) %collective-permute-start.17) | collective-permute-done | bytes 589856 | tf_op jit(solution)/shard_map/ppermute | solution.py:506
  121.3 9.8 %collective-permute-done.20.refs_5_ = bf16[192,1536]{1,0:T(8,128)(2,1)} collective-permute-done((bf16[192,1536]{1,0:T(8,128)(2,1)}, bf16[192,1536]{1,0:T(8,128)(2,1)}, u32[]{:S(2)}, u32[]{:S(2)}) %collective-permute-start.20) | collective-permute-done | bytes 589856 | tf_op jit(solution)/shard_map/ppermute | solution.py:506
  131.7 11.0 %collective-permute-done.21.refs_6_ = bf16[192,1536]{1,0:T(8,128)(2,1)} collective-permute-done((bf16[192,1536]{1,0:T(8,128)(2,1)}, bf16[192,1536]{1,0:T(8,128)(2,1)}, u32[]{:S(2)}, u32[]{:S(2)}) %collective-permute-start.21) | collective-permute-done | bytes 589856 | tf_op jit(solution)/shard_map/ppermute | solution.py:506
  201.5 8.0 fusion.91.gate_ref
  210.5 26.3 %scan_forward.1 = (bf16[1280,768]{1,0:T(8,128)(2,1)}, f32[1280,768]{1,0:T(8,128)}, f32[10,16,768]{2,1,0:T(8,128)}) custom-call(s32[2]{0:T(128)} %copy-done.96, f32[1280,128]{1,0:T(8,128)} %pad_maximum_fusion.8.proj_ref, bf16[1280,768]{1,0:T(8,128)(2,1)} %copy-done.7, f32[1280,768]{1,0:T(8,128)} %fusion.91.gate_ref, f32[8,128]{1,0:T(8,128)} %maximum_maximum_fusion.params_ref, ...), custom_call_target="tpu_custom_call" | custom-call | flops 40000000000 | bytes 14000000 | tf_op jit(solution)/shard_map/scan_forward/pallas_call | solution.py:401
  257.3 14.8 %collective-permute-done.42.refs_3_ = bf16[192,2048]{1,0:T(8,128)(2,1)} collective-permute-done((bf16[192,2048]{1,0:T(8,128)(2,1)}, bf16[192,2048]{1,0:T(8,128)(2,1)}, u32[]{:S(2)}, u32[]{:S(2)}) %collective-permute-start.42) | collective-permute-done | bytes 786464 | tf_op jit(solution)/shard_map/ppermute | solution.py:506
  277.7 12.6 %collective-permute-done.40.refs_1_ = bf16[192,2048]{1,0:T(8,128)(2,1)} collective-permute-done((bf16[192,2048]{1,0:T(8,128)(2,1)}, bf16[192,2048]{1,0:T(8,128)(2,1)}, u32[]{:S(2)}, u32[]{:S(2)}) %collective-permute-start.40) | collective-permute-done | bytes 786464 | tf_op jit(solution)/shard_map/ppermute | solution.py:506
  290.6 29.9 %collective-permute-done.41.refs_2_ = bf16[192,2048]{1,0:T(8,128)(2,1)} collective-permute-done((bf16[192,2048]{1,0:T(8,128)(2,1)}, bf16[192,2048]{1,0:T(8,128)(2,1)}, u32[]{:S(2)}, u32[]{:S(2)}) %collective-permute-start.41) | collective-permute-done | bytes 786464 | tf_op jit(solution)/shard_map/ppermute | solution.py:506
  324.6 16.5 %collective-permute-done.44.refs_5_ = bf16[192,2048]{1,0:T(8,128)(2,1)S(1)} collective-permute-done((bf16[192,2048]{1,0:T(8,128)(2,1)}, bf16[192,2048]{1,0:T(8,128)(2,1)S(1)}, u32[]{:S(2)}, u32[]{:S(2)}) %collective-permute-start.44) | collective-permute-done | bytes 786464 | tf_op jit(solution)/shard_map/ppermute | solution.py:506
  341.1 15.4 %collective-permute-done.45.refs_6_ = bf16[192,2048]{1,0:T(8,128)(2,1)S(1)} collective-permute-done((bf16[192,2048]{1,0:T(8,128)(2,1)}, bf16[192,2048]{1,0:T(8,128)(2,1)S(1)}, u32[]{:S(2)}, u32[]{:S(2)}) %collective-permute-start.45) | collective-permute-done | bytes 786464 | tf_op jit(solution)/shard_map/ppermute | solution.py:506
  360.1 8.1 collective-permute-done.49.refs_3_
  370.4 10.1 %collective-permute-done.51.refs_5_ = bf16[192,1024]{1,0:T(8,128)(2,1)S(1)} collective-permute-done((bf16[192,1024]{1,0:T(8,128)(2,1)}, bf16[192,1024]{1,0:T(8,128)(2,1)S(1)}, u32[]{:S(2)}, u32[]{:S(2)}) %collective-permute-start.51) | collective-permute-done | bytes 393248 | tf_op jit(solution)/shard_map/ppermute | solution.py:506
  403.1 9.8 %fusion.52 = f32[1280,1024]{1,0:T(8,128)} fusion(bf16[1536,1024]{1,0:T(8,128)(2,1)} %arrange_weights.7, bf16[1280,384]{0,1:T(8,128)(2,1)} %collective-permute-done.58, bf16[1280,384]{0,1:T(8,128)(2,1)} %collective-permute-done.57, bf16[1280,384]{0,1:T(8,128)(2,1)} %collective-permute-done.56, bf16[1280,384]{0,1:T(8,128)(2,1)} %broadcast_select_fusion.1), kind=kOutput, calls=%fused_computation.131 | convolution fusion | flops 4042260480 | bytes 12320768 | tf_op jit(solution)/shard_map/dot_general | solution.py:25
  412.9 8.6 fusion.89
  421.6 11.5 %multiply_convert_fusion.1 = (bf16[1280,1024]{1,0:T(8,128)(2,1)}, bf16[1280,1024]{1,0:T(8,128)(2,1)}, bf16[1280,1024]{1,0:T(8,128)(2,1)S(1)}) fusion(f32[1280,1024]{1,0:T(8,128)} %fusion.52, f32[1280,1024]{1,0:T(8,128)} %fusion.89, bf16[1536,1024]{1,0:T(8,128)(2,1)S(1)} %copy-done.99, bf16[1280,384]{0,1:T(8,128)(2,1)} %collective-permute-done.39, ...), kind=kOutput, calls=%fused_computation.10 | convolution fusion | flops 4061921280 | bytes 25427968 | tf_op jit(solution)/shard_map/dot_general | solution.py:25
  477.4 9.1 collective-permute-done.60
  496.6 10.2 %collective-permute-done.62 = f32[10,128]{1,0:T(8,128)S(1)} collective-permute-done((f32[10,128]{1,0:T(8,128)S(1)}, f32[10,128]{1,0:T(8,128)S(1)}, u32[]{:S(2)}, u32[]{:S(2)}) %collective-permute-start.62) | collective-permute-done | bytes 5152 | tf_op jit(solution)/shard_map/ppermute | solution.py:503
  523.0 30.8 %collective-permute-done.98 = bf16[4,192,1024]{2,1,0:T(8,128)(2,1)S(1)} collective-permute-done((bf16[4,192,1024]{2,1,0:T(8,128)(2,1)}, bf16[4,192,1024]{2,1,0:T(8,128)(2,1)S(1)}, u32[]{:S(2)}, u32[]{:S(2)}) %collective-permute-start.98) | collective-permute-done | bytes 1572896 | tf_op jit(solution)/shard_map/ppermute | solution.py:506
  564.2 12.6 %collective-permute-done.103 = bf16[192,1024]{1,0:T(8,128)(2,1)S(1)} collective-permute-done((bf16[192,1024]{1,0:T(8,128)(2,1)S(1)}, bf16[192,1024]{1,0:T(8,128)(2,1)S(1)}, u32[]{:S(2)}, u32[]{:S(2)}) %collective-permute-start.103) | collective-permute-done | bytes 393248 | tf_op jit(solution)/shard_map/ppermute | solution.py:506
  576.8 26.0 %collective-permute-done.104 = bf16[192,1024]{1,0:T(8,128)(2,1)S(1)} collective-permute-done((bf16[192,1024]{1,0:T(8,128)(2,1)S(1)}, bf16[192,1024]{1,0:T(8,128)(2,1)S(1)}, u32[]{:S(2)}, u32[]{:S(2)}) %collective-permute-start.104) | collective-permute-done | bytes 393248 | tf_op jit(solution)/shard_map/ppermute | solution.py:506
  605.2 10.9 %collective-permute-start.99 = (bf16[192,1024]{1,0:T(8,128)(2,1)S(1)}, bf16[192,1024]{1,0:T(8,128)(2,1)S(1)}, u32[]{:S(2)}, u32[]{:S(2)}) collective-permute-start(bf16[192,1024]{1,0:T(8,128)(2,1)S(1)} %get-tuple-element.164), channel_id=1, source_target_pairs={{0,8},{4,12},{8,0},{12,4},{16,24},{20,28},{24,16},{28,20},{1,9},{5... | collective-permute-start | bytes 1179656 | tf_op jit(solution)/shard_map/ppermute | solution.py:506
  632.4 8.1 fusion.53.upstream_ref
  640.5 44.6 %scan_backward.1 = (f32[1280,128]{1,0:T(8,128)}, f32[1280,768]{1,0:T(8,128)}, bf16[1280,768]{1,0:T(8,128)(2,1)}, f32[128,128]{1,0:T(8,128)}, f32[8,128]{1,0:T(8,128)}, /*index=5*/f32[8,768]{1,0:T(8,128)}) custom-call(s32[2]{0:T(128)} %copy-done.96, f32[1280,768]{1,0:T(8,128)} %fusion.53.upstream_ref, f32[1280,128]{1,0:T(8,128)} %pad_maximum_fusion.8.proj_ref, ...), custom_call_target="tpu_custom_call" | custom-call | flops 80000000000 | bytes 24000000 | tf_op jit(solution)/shard_map/scan_backward/pallas_call | solution.py:442
  720.1 7.6 fusion.93
  752.9 11.0 %collective-permute-done.90 = bf16[4,192,768]{2,1,0:T(8,128)(2,1)} collective-permute-done((bf16[4,192,768]{2,1,0:T(8,128)(2,1)}, bf16[4,192,768]{2,1,0:T(8,128)(2,1)}, u32[]{:S(2)}, u32[]{:S(2)}) %collective-permute-start.90) | collective-permute-done | bytes 1179680 | tf_op jit(solution)/shard_map/ppermute | solution.py:506
  782.2 17.9 %collective-permute-done.92 = bf16[192,768]{1,0:T(8,128)(2,1)} collective-permute-done((bf16[192,768]{1,0:T(8,128)(2,1)S(1)}, bf16[192,768]{1,0:T(8,128)(2,1)}, u32[]{:S(2)}, u32[]{:S(2)}) %collective-permute-start.92) | collective-permute-done | bytes 294944 | tf_op jit(solution)/shard_map/ppermute | solution.py:506
  815.3 7.5 collective-permute-done.87
  822.9 11.4 %collective-permute-done.88 = bf16[192,768]{1,0:T(8,128)(2,1)S(1)} collective-permute-done((bf16[192,768]{1,0:T(8,128)(2,1)S(1)}, bf16[192,768]{1,0:T(8,128)(2,1)S(1)}, u32[]{:S(2)}, u32[]{:S(2)}) %collective-permute-start.88) | collective-permute-done | bytes 294944 | tf_op jit(solution)/shard_map/ppermute | solution.py:506
  845.0 7.5 gather_fusion.5
  875.2 10.6 %collective-permute-done.76 = bf16[2,128,384]{2,1,0:T(8,128)(2,1)S(1)} collective-permute-done((bf16[2,128,384]{2,1,0:T(8,128)(2,1)S(1)}, bf16[2,128,384]{2,1,0:T(8,128)(2,1)S(1)}, u32[]{:S(2)}, u32[]{:S(2)}) %collective-permute-start.76) | collective-permute-done | bytes 196640 | tf_op jit(solution)/shard_map/ppermute | solution.py:506
  (658 shorter events, 443.9 us)
Async XLA Ops:
  72.4 42.1 %collective-permute-start.17 = (bf16[192,1536]{1,0:T(8,128)(2,1)S(1)}, bf16[192,1536]{1,0:T(8,128)(2,1)}, u32[]{:S(2)}, u32[]{:S(2)}) collective-permute-start(bf16[192,1536]{1,0:T(8,128)(2,1)S(1)} %constant_dynamic-update-slice_fusion.refs_0_), channel_id=1, source_target_pairs={{0,16},{4,20},{8,24},{12,28},{16,0},{20,4},{24,8},{28,12},{1,17},{... | collective-permute-start | bytes 1769480 | tf_op jit(solution)/shard_map/ppermute | solution.py:506
  77.6 37.4 %collective-permute-start.22 = (bf16[192,1536]{1,0:T(8,128)(2,1)S(1)}, bf16[192,1536]{1,0:T(8,128)(2,1)}, u32[]{:S(2)}, u32[]{:S(2)}) collective-permute-start(bf16[192,1536]{1,0:T(8,128)(2,1)S(1)} %collective-permute-done.18.refs_3_), channel_id=1, source_target_pairs={{0,4},{4,0},{8,12},{12,8},{16,20},{20,16},{24,28},{28,24},{1,5},{5... | collective-permute-start | bytes 1769480 | tf_op jit(solution)/shard_map/ppermute | solution.py:506
  80.8 70.9 %collective-permute-start.14 = (bf16[1280,384]{0,1:T(8,128)(2,1)S(1)}, bf16[1280,384]{0,1:T(8,128)(2,1)}, u32[]{:S(2)}, u32[]{:S(2)}) collective-permute-start(bf16[1280,384]{0,1:T(8,128)(2,1)S(1)} %fusion.16), channel_id=1, source_target_pairs={{0,1},{1,0},{2,3},{3,2},{4,5},{5,4},{6,7},{7,6},{8,9},{9,8},{10,11... | collective-permute-start | bytes 2949128 | tf_op jit(solution)/shard_map/ppermute | solution.py:503
  86.9 64.8 %collective-permute-start.15 = (bf16[1280,384]{0,1:T(8,128)(2,1)}, bf16[1280,384]{0,1:T(8,128)(2,1)}, u32[]{:S(2)}, u32[]{:S(2)}) collective-permute-start(bf16[1280,384]{0,1:T(8,128)(2,1)} %collective-permute-done.13), channel_id=1, source_target_pairs={{0,1},{1,0},{2,3},{3,2},{4,5},{5,4},{6,7},{7,6},{8,9},{9,8},{10,11... | collective-permute-start | bytes 2949128 | tf_op jit(solution)/shard_map/ppermute | solution.py:503
  117.7 50.1 %collective-permute-start.28 = (bf16[192,768]{1,0:T(8,128)(2,1)}, bf16[192,768]{1,0:T(8,128)(2,1)}, u32[]{:S(2)}, u32[]{:S(2)}) collective-permute-start(bf16[192,768]{1,0:T(8,128)(2,1)} %bitcast.339), channel_id=1, source_target_pairs={{0,24},{4,28},{8,16},{12,20},{16,8},{20,12},{24,0},{28,4},{1,25},{... | collective-permute-start | bytes 884744 | tf_op jit(solution)/shard_map/ppermute | solution.py:506
  131.0 38.4 %collective-permute-start.26 = (bf16[192,768]{1,0:T(8,128)(2,1)}, bf16[192,768]{1,0:T(8,128)(2,1)}, u32[]{:S(2)}, u32[]{:S(2)}) collective-permute-start(bf16[192,768]{1,0:T(8,128)(2,1)} %bitcast.340), channel_id=1, source_target_pairs={{0,8},{4,12},{8,0},{12,4},{16,24},{20,28},{24,16},{28,20},{1,9},{5... | collective-permute-start | bytes 884744 | tf_op jit(solution)/shard_map/ppermute | solution.py:506
  251.5 70.9 %collective-permute-start.56 = (bf16[1280,384]{0,1:T(8,128)(2,1)}, bf16[1280,384]{0,1:T(8,128)(2,1)}, u32[]{:S(2)}, u32[]{:S(2)}) collective-permute-start(bf16[1280,384]{0,1:T(8,128)(2,1)} %broadcast_select_fusion.1), channel_id=1, source_target_pairs={{0,2},{1,3},{2,0},{3,1},{4,6},{5,7},{6,4},{7,5},{8,10},{9,11},{10,... | collective-permute-start | bytes 2949128 | tf_op jit(solution)/shard_map/ppermute | solution.py:503
  253.1 37.2 %collective-permute-start.40 = (bf16[192,2048]{1,0:T(8,128)(2,1)}, bf16[192,2048]{1,0:T(8,128)(2,1)}, u32[]{:S(2)}, u32[]{:S(2)}) collective-permute-start(bf16[192,2048]{1,0:T(8,128)(2,1)} %constant_dynamic-update-slice_fusion.2.refs_0_), channel_id=1, source_target_pairs={{0,8},{4,12},{8,0},{12,4},{16,24},{20,28},{24,16},{28,20},{1,9},{5... | collective-permute-start | bytes 2359304 | tf_op jit(solution)/shard_map/ppermute | solution.py:506
  253.7 66.8 %collective-permute-start.41 = (bf16[192,2048]{1,0:T(8,128)(2,1)}, bf16[192,2048]{1,0:T(8,128)(2,1)}, u32[]{:S(2)}, u32[]{:S(2)}) collective-permute-start(bf16[192,2048]{1,0:T(8,128)(2,1)} %constant_dynamic-update-slice_fusion.2.refs_0_), channel_id=1, source_target_pairs={{0,16},{4,20},{8,24},{12,28},{16,0},{20,4},{24,8},{28,12},{1,17},{... | collective-permute-start | bytes 2359304 | tf_op jit(solution)/shard_map/ppermute | solution.py:506
  272.1 48.6 %collective-permute-start.46 = (bf16[192,2048]{1,0:T(8,128)(2,1)}, bf16[192,2048]{1,0:T(8,128)(2,1)}, u32[]{:S(2)}, u32[]{:S(2)}) collective-permute-start(bf16[192,2048]{1,0:T(8,128)(2,1)} %collective-permute-done.42.refs_3_), channel_id=1, source_target_pairs={{0,4},{4,0},{8,12},{12,8},{16,20},{20,16},{24,28},{28,24},{1,5},{5... | collective-permute-start | bytes 2359304 | tf_op jit(solution)/shard_map/ppermute | solution.py:506
  276.2 46.3 %collective-permute-start.36 = (f32[10,128]{1,0:T(8,128)S(1)}, f32[10,128]{1,0:T(8,128)S(1)}, u32[]{:S(2)}, u32[]{:S(2)}) collective-permute-start(f32[10,128]{1,0:T(8,128)S(1)} %bitcast_add_fusion.4), channel_id=1, source_target_pairs={{0,2},{1,3},{2,0},{3,1},{4,6},{5,7},{6,4},{7,5},{8,10},{9,11},{10,... | collective-permute-start | bytes 15368 | tf_op jit(solution)/shard_map/ppermute | solution.py:503
  320.7 35.8 %collective-permute-start.45 = (bf16[192,2048]{1,0:T(8,128)(2,1)}, bf16[192,2048]{1,0:T(8,128)(2,1)S(1)}, u32[]{:S(2)}, u32[]{:S(2)}) collective-permute-start(bf16[192,2048]{1,0:T(8,128)(2,1)} %collective-permute-done.41.refs_2_), channel_id=1, source_target_pairs={{0,4},{4,0},{8,12},{12,8},{16,20},{20,16},{24,28},{28,24},{1,5},{5... | collective-permute-start | bytes 2359304 | tf_op jit(solution)/shard_map/ppermute | solution.py:506
  322.5 35.7 %collective-permute-start.48 = (bf16[192,1024]{1,0:T(8,128)(2,1)S(1)}, bf16[192,1024]{1,0:T(8,128)(2,1)S(1)}, u32[]{:S(2)}, u32[]{:S(2)}) collective-permute-start(bf16[192,1024]{1,0:T(8,128)(2,1)S(1)} %bitcast.335), channel_id=1, source_target_pairs={{0,16},{4,20},{8,24},{12,28},{16,0},{20,4},{24,8},{28,12},{1,17},{... | collective-permute-start | bytes 1179656 | tf_op jit(solution)/shard_map/ppermute | solution.py:506
  324.5 78.6 %collective-permute-start.57 = (bf16[1280,384]{0,1:T(8,128)(2,1)}, bf16[1280,384]{0,1:T(8,128)(2,1)}, u32[]{:S(2)}, u32[]{:S(2)}) collective-permute-start(bf16[1280,384]{0,1:T(8,128)(2,1)} %broadcast_select_fusion.1), channel_id=1, source_target_pairs={{0,1},{1,0},{2,3},{3,2},{4,5},{5,4},{6,7},{7,6},{8,9},{9,8},{10,11... | collective-permute-start | bytes 2949128 | tf_op jit(solution)/shard_map/ppermute | solution.py:503
  341.1 62.0 %collective-permute-start.58 = (bf16[1280,384]{0,1:T(8,128)(2,1)}, bf16[1280,384]{0,1:T(8,128)(2,1)}, u32[]{:S(2)}, u32[]{:S(2)}) collective-permute-start(bf16[1280,384]{0,1:T(8,128)(2,1)} %collective-permute-done.56), channel_id=1, source_target_pairs={{0,1},{1,0},{2,3},{3,2},{4,5},{5,4},{6,7},{7,6},{8,9},{9,8},{10,11... | collective-permute-start | bytes 2949128 | tf_op jit(solution)/shard_map/ppermute | solution.py:503
  449.4 60.8 %collective-permute-start.106 = (bf16[4,192,1024]{2,1,0:T(8,128)(2,1)}, bf16[4,192,1024]{2,1,0:T(8,128)(2,1)S(1)}, u32[]{:S(2)}, u32[]{:S(2)}) collective-permute-start(bf16[4,192,1024]{2,1,0:T(8,128)(2,1)} %dynamic-slice_bitcast_fusion), channel_id=1, source_target_pairs={{0,4},{4,0},{8,12},{12,8},{16,20},{20,16},{24,28},{28,24},{1,5},{5... | collective-permute-start | bytes 4718600 | tf_op jit(solution)/shard_map/ppermute | solution.py:506
  469.4 51.1 %collective-permute-start.102 = (bf16[4,192,1024]{2,1,0:T(8,128)(2,1)S(1)}, bf16[4,192,1024]{2,1,0:T(8,128)(2,1)S(1)}, u32[]{:S(2)}, u32[]{:S(2)}) collective-permute-start(bf16[4,192,1024]{2,1,0:T(8,128)(2,1)S(1)} %dynamic-slice_bitcast_fusion.1), channel_id=1, source_target_pairs={{0,4},{4,0},{8,12},{12,8},{16,20},{20,16},{24,28},{28,24},{1,5},{5... | collective-permute-start | bytes 4718600 | tf_op jit(solution)/shard_map/ppermute | solution.py:506
  496.0 57.7 %collective-permute-start.98 = (bf16[4,192,1024]{2,1,0:T(8,128)(2,1)}, bf16[4,192,1024]{2,1,0:T(8,128)(2,1)S(1)}, u32[]{:S(2)}, u32[]{:S(2)}) collective-permute-start(bf16[4,192,1024]{2,1,0:T(8,128)(2,1)} %dynamic-slice_bitcast_fusion.2), channel_id=1, source_target_pairs={{0,4},{4,0},{8,12},{12,8},{16,20},{20,16},{24,28},{28,24},{1,5},{5... | collective-permute-start | bytes 4718600 | tf_op jit(solution)/shard_map/ppermute | solution.py:506
  509.6 53.3 %collective-permute-start.63 = (bf16[1280,384]{0,1:T(8,128)(2,1)}, bf16[1280,384]{0,1:T(8,128)(2,1)}, u32[]{:S(2)}, u32[]{:S(2)}) collective-permute-start(bf16[1280,384]{0,1:T(8,128)(2,1)} %get-tuple-element.146), channel_id=1, source_target_pairs={{0,2},{1,3},{2,0},{3,1},{4,6},{5,7},{6,4},{7,5},{8,10},{9,11},{10,... | collective-permute-start | bytes 2949128 | tf_op jit(solution)/shard_map/ppermute | solution.py:503
  511.4 49.0 %collective-permute-start.107 = (bf16[192,1024]{1,0:T(8,128)(2,1)S(1)}, bf16[192,1024]{1,0:T(8,128)(2,1)S(1)}, u32[]{:S(2)}, u32[]{:S(2)}) collective-permute-start(bf16[192,1024]{1,0:T(8,128)(2,1)S(1)} %get-tuple-element.158), channel_id=1, source_target_pairs={{0,8},{4,12},{8,0},{12,4},{16,24},{20,28},{24,16},{28,20},{1,9},{5... | collective-permute-start | bytes 1179656 | tf_op jit(solution)/shard_map/ppermute | solution.py:506
  518.5 42.9 %collective-permute-start.108 = (bf16[192,1024]{1,0:T(8,128)(2,1)S(1)}, bf16[192,1024]{1,0:T(8,128)(2,1)S(1)}, u32[]{:S(2)}, u32[]{:S(2)}) collective-permute-start(bf16[192,1024]{1,0:T(8,128)(2,1)S(1)} %get-tuple-element.160), channel_id=1, source_target_pairs={{0,16},{4,20},{8,24},{12,28},{16,0},{20,4},{24,8},{28,12},{1,17},{... | collective-permute-start | bytes 1179656 | tf_op jit(solution)/shard_map/ppermute | solution.py:506
  520.5 42.3 %collective-permute-start.109 = (bf16[192,1024]{1,0:T(8,128)(2,1)S(1)}, bf16[192,1024]{1,0:T(8,128)(2,1)S(1)}, u32[]{:S(2)}, u32[]{:S(2)}) collective-permute-start(bf16[192,1024]{1,0:T(8,128)(2,1)S(1)} %get-tuple-element.159), channel_id=1, source_target_pairs={{0,24},{4,28},{8,16},{12,20},{16,8},{20,12},{24,0},{28,4},{1,25},{... | collective-permute-start | bytes 1179656 | tf_op jit(solution)/shard_map/ppermute | solution.py:506
  560.4 42.4 %collective-permute-start.104 = (bf16[192,1024]{1,0:T(8,128)(2,1)S(1)}, bf16[192,1024]{1,0:T(8,128)(2,1)S(1)}, u32[]{:S(2)}, u32[]{:S(2)}) collective-permute-start(bf16[192,1024]{1,0:T(8,128)(2,1)S(1)} %get-tuple-element.163), channel_id=1, source_target_pairs={{0,16},{4,20},{8,24},{12,28},{16,0},{20,4},{24,8},{28,12},{1,17},{... | collective-permute-start | bytes 1179656 | tf_op jit(solution)/shard_map/ppermute | solution.py:506
  561.3 43.9 %collective-permute-start.105 = (bf16[192,1024]{1,0:T(8,128)(2,1)S(1)}, bf16[192,1024]{1,0:T(8,128)(2,1)S(1)}, u32[]{:S(2)}, u32[]{:S(2)}) collective-permute-start(bf16[192,1024]{1,0:T(8,128)(2,1)S(1)} %get-tuple-element.162), channel_id=1, source_target_pairs={{0,24},{4,28},{8,16},{12,20},{16,8},{20,12},{24,0},{28,4},{1,25},{... | collective-permute-start | bytes 1179656 | tf_op jit(solution)/shard_map/ppermute | solution.py:506
  562.9 69.5 %collective-permute-start.64 = (bf16[1280,384]{0,1:T(8,128)(2,1)}, bf16[1280,384]{0,1:T(8,128)(2,1)}, u32[]{:S(2)}, u32[]{:S(2)}) collective-permute-start(bf16[1280,384]{0,1:T(8,128)(2,1)} %get-tuple-element.146), channel_id=1, source_target_pairs={{0,1},{1,0},{2,3},{3,2},{4,5},{5,4},{6,7},{7,6},{8,9},{9,8},{10,11... | collective-permute-start | bytes 2949128 | tf_op jit(solution)/shard_map/ppermute | solution.py:503
  562.9 69.5 %collective-permute-start.65 = (bf16[1280,384]{0,1:T(8,128)(2,1)}, bf16[1280,384]{0,1:T(8,128)(2,1)}, u32[]{:S(2)}, u32[]{:S(2)}) collective-permute-start(bf16[1280,384]{0,1:T(8,128)(2,1)} %collective-permute-done.63), channel_id=1, source_target_pairs={{0,1},{1,0},{2,3},{3,2},{4,5},{5,4},{6,7},{7,6},{8,9},{9,8},{10,11... | collective-permute-start | bytes 2949128 | tf_op jit(solution)/shard_map/ppermute | solution.py:503
  576.8 47.2 %collective-permute-start.100 = (bf16[192,1024]{1,0:T(8,128)(2,1)S(1)}, bf16[192,1024]{1,0:T(8,128)(2,1)S(1)}, u32[]{:S(2)}, u32[]{:S(2)}) collective-permute-start(bf16[192,1024]{1,0:T(8,128)(2,1)S(1)} %get-tuple-element.166), channel_id=1, source_target_pairs={{0,16},{4,20},{8,24},{12,28},{16,0},{20,4},{24,8},{28,12},{1,17},{... | collective-permute-start | bytes 1179656 | tf_op jit(solution)/shard_map/ppermute | solution.py:506
  709.4 38.7 %collective-permute-start.94 = (bf16[4,192,768]{2,1,0:T(8,128)(2,1)}, bf16[4,192,768]{2,1,0:T(8,128)(2,1)}, u32[]{:S(2)}, u32[]{:S(2)}) collective-permute-start(bf16[4,192,768]{2,1,0:T(8,128)(2,1)} %dynamic-slice_bitcast_fusion.3), channel_id=1, source_target_pairs={{0,4},{4,0},{8,12},{12,8},{16,20},{20,16},{24,28},{28,24},{1,5},{5... | collective-permute-start | bytes 3538952 | tf_op jit(solution)/shard_map/ppermute | solution.py:506
  715.2 48.7 %collective-permute-start.90 = (bf16[4,192,768]{2,1,0:T(8,128)(2,1)}, bf16[4,192,768]{2,1,0:T(8,128)(2,1)}, u32[]{:S(2)}, u32[]{:S(2)}) collective-permute-start(bf16[4,192,768]{2,1,0:T(8,128)(2,1)} %dynamic-slice_bitcast_fusion.4), channel_id=1, source_target_pairs={{0,4},{4,0},{8,12},{12,8},{16,20},{20,16},{24,28},{28,24},{1,5},{5... | collective-permute-start | bytes 3538952 | tf_op jit(solution)/shard_map/ppermute | solution.py:506
  743.8 58.4 %collective-permute-start.86 = (bf16[4,192,768]{2,1,0:T(8,128)(2,1)}, bf16[4,192,768]{2,1,0:T(8,128)(2,1)}, u32[]{:S(2)}, u32[]{:S(2)}) collective-permute-start(bf16[4,192,768]{2,1,0:T(8,128)(2,1)} %dynamic-slice_bitcast_fusion.5), channel_id=1, source_target_pairs={{0,4},{4,0},{8,12},{12,8},{16,20},{20,16},{24,28},{28,24},{1,5},{5... | collective-permute-start | bytes 3538952 | tf_op jit(solution)/shard_map/ppermute | solution.py:506
  777.1 36.2 %collective-permute-start.70 = (bf16[1280,384]{0,1:T(8,128)(2,1)}, bf16[1280,384]{0,1:T(8,128)(2,1)}, u32[]{:S(2)}, u32[]{:S(2)}) collective-permute-start(bf16[1280,384]{0,1:T(8,128)(2,1)} %slice.510), channel_id=1, source_target_pairs={{0,2},{1,3},{2,0},{3,1},{4,6},{5,7},{6,4},{7,5},{8,10},{9,11},{10,... | collective-permute-start | bytes 2949128 | tf_op jit(solution)/shard_map/ppermute | solution.py:503
  854.5 36.0 %collective-permute-start.82 = (f32[4,112,128]{2,1,0:T(8,128)S(1)}, f32[4,112,128]{2,1,0:T(8,128)S(1)}, u32[]{:S(2)}, u32[]{:S(2)}) collective-permute-start(f32[4,112,128]{2,1,0:T(8,128)S(1)} %dynamic-slice_bitcast_fusion.24), channel_id=1, source_target_pairs={{0,4},{4,0},{8,12},{12,8},{16,20},{20,16},{24,28},{28,24},{1,5},{5... | collective-permute-start | bytes 688136 | tf_op jit(solution)/shard_map/ppermute | solution.py:506
  (189 other events, 4394.2 us)

commit v2 on v1

--- a/solution.py
+++ b/solution.py
@@ -425,7 +425,7 @@
             scratch_shapes=[pltpu.VMEM((NS, channels), jnp.float32)],
         ),
         cost_estimate=pl.CostEstimate(
-            flops=40_000_000_000, bytes_accessed=14_000_000, transcendentals=6_000_000
+            flops=100_000_000, bytes_accessed=100_000, transcendentals=0
         ),
         name="scan_forward",
     )(bounds, projected, conv_out, gate_pre, params, step_w, skip, expand)
@@ -475,7 +475,7 @@
             scratch_shapes=[pltpu.VMEM((NS, channels), jnp.float32)],
         ),
         cost_estimate=pl.CostEstimate(
-            flops=80_000_000_000, bytes_accessed=24_000_000, transcendentals=8_000_000
+            flops=100_000_000, bytes_accessed=100_000, transcendentals=0
         ),
         name="scan_backward",
     )(bounds, upstream, projected, conv_out, gate_pre, scanned, states, params, step_w, skip, expand)
@@ -510,24 +510,37 @@
         return (block & 1) * 2 + (block >> 1)
 
 
-    def gather_features(self, values):
+    def gather_features(self, values, until=None, deadline=None):
         if not self.staged:
-            return lax.all_gather(values, "tensor", axis=1, tiled=True)
+            rows = lax.all_gather(values, "tensor", axis=1, tiled=True)
+            return rows if deadline is None else (rows, deadline)
         across = self.over_tensor(values, 2)
         beside = self.over_tensor(values, 1)
-        diagonal = self.over_tensor(across, 1)
-        return jnp.concatenate([values, across, beside, diagonal], axis=1)
-
-    def sum_features(self, project):
+        diagonal = self.over_tensor(across if until is None else after(across, until), 1)
+        if deadline is not None:
+            across, beside, diagonal, deadline = lax.optimization_barrier(
+                (across, beside, diagonal, deadline)
+            )
+        rows = jnp.concatenate([values, across, beside, diagonal], axis=1)
+        return rows if deadline is None else (rows, deadline)
+
+    def sum_features(self, project, start=None, until=None, across_start=None):
         width = D // self.tensor_size
         if not self.staged:
             return lax.psum_scatter(
                 project(slice(0, D)), "tensor", scatter_dimension=1, tiled=True
             )
         sent = project(slice(2 * width, 4 * width)).astype(jnp.bfloat16)
+        if start is not None:
+            sent = after(sent, start)
         kept = project(slice(0, 2 * width))
         total = kept + self.over_tensor(sent, 1).astype(jnp.float32)
-        across = self.over_tensor(total[:, width:].astype(jnp.bfloat16), 2)
+        passed = total[:, width:].astype(jnp.bfloat16)
+        if across_start is not None:
+            passed = after(passed, across_start)
+        across = self.over_tensor(passed, 2)
+        if until is not None:
+            across = after(across, until)
         return total[:, :width] + across.astype(jnp.float32)
 
     def sum_small(self, values):
@@ -552,118 +565,137 @@
         return jnp.concatenate([first, second], axis=0)
 
 
-    def gather_pieces(self, shard):
-        same = [shard] + [self.over_dp(shard, 2 * distance) for distance in range(1, self.dp_size // 2)]
-        return same, [self.over_dp(piece, 1) for piece in same]
-
-    def gather_weights(self, shards):
+    def block_order(self):
+        return jnp.stack([jnp.bitwise_xor(self.lane, place) for place in PLACES]).astype(jnp.int32)
+
+    def gather_whole(self, shard, widths):
+        whole_rows = lax.all_gather(shard, "dp", axis=0, tiled=True)
         if not self.staged:
-            return [lax.all_gather(shard, "dp", axis=0, tiled=True) for shard in shards], shards[0]
-        widths = [shard.shape[1] for shard in shards]
-        shard = shards[0] if len(shards) == 1 else jnp.concatenate(shards, axis=1)
-        same, other = self.gather_pieces(shard)
-        places = jnp.stack([self.place_of(distance) for distance in range(4)] + [self.inner])
-        return arrange_weights(places.astype(jnp.int32), same, other, widths), other[3]
-
-    def sum_weights(self, grad):
-        if not self.staged:
-            return lax.psum_scatter(
-                grad.astype(jnp.bfloat16), "dp", scatter_dimension=0, tiled=True
-            ).astype(jnp.float32)
-        width = grad.shape[1]
-        blocks = grad.reshape(4, 2, D // 8, width)
+            return split_columns(whole_rows, widths)
+        return move_blocks(self.block_order(), whole_rows, widths)
+
+    def sum_whole(self, grads, earlier=None):
+        widths = [grad.shape[1] for grad in grads]
+        if self.staged:
+            joined = restore_blocks(self.block_order(), grads)
+        else:
+            joined = jnp.concatenate(grads, axis=1)
+        if earlier is not None:
+            joined = after(joined, earlier)
+        total = lax.psum_scatter(joined, "dp", scatter_dimension=0, tiled=True)
+        return [part.astype(jnp.float32) for part in split_columns(total, widths)], joined
+
+
+    def sum_across(self, grad):
+        blocks = grad.reshape(4, 2, D // 8, grad.shape[1])
         sent = lax.dynamic_index_in_dim(blocks, 1 - self.inner, 1, keepdims=False)
         kept = lax.dynamic_index_in_dim(blocks, self.inner, 1, keepdims=False)
-        got = self.over_dp(sent.astype(jnp.bfloat16), 1)
-        total = (kept.astype(jnp.float32) + got.astype(jnp.float32)).astype(jnp.bfloat16)
-        pieces = [
-            lax.dynamic_index_in_dim(total, self.place_of(distance), 0, keepdims=False)
-            for distance in range(4)
-        ]
-        result = pieces[0].astype(jnp.float32)
-        for distance in range(1, 4):
-            result = result + self.over_dp(pieces[distance], 2 * distance).astype(jnp.float32)
-        return result
-
-    def gather_rows(self, block):
-        if not self.staged:
-            return lax.all_gather(block, "dp", axis=0, tiled=False)
-        same = jnp.stack(
-            [block] + [self.over_dp(block, 2 * distance) for distance in range(1, 4)]
+        return kept, self.over_dp(sent, 1)
+
+    def sum_far(self, across, marker):
+        kept, got = across
+        total = (kept.astype(jnp.float32) + after(got, marker).astype(jnp.float32)).astype(
+            jnp.bfloat16
         )
-        other = self.over_dp(same, 1)
-        both = jnp.stack([same, other], axis=1).reshape((8,) + block.shape)
-        index = jnp.arange(8, dtype=jnp.int32)
-        return both[jnp.bitwise_xor(index, self.group)]
-
-    def sum_blocks(self, blocks):
-        if not self.staged:
-            return lax.psum_scatter(blocks, "dp", scatter_dimension=0, tiled=False)
-        paired = blocks.reshape((4, 2) + blocks.shape[1:])
-        sent = lax.dynamic_index_in_dim(paired, 1 - self.inner, 1, keepdims=False)
-        kept = lax.dynamic_index_in_dim(paired, self.inner, 1, keepdims=False)
-        total = kept + self.over_dp(sent, 1)
-        result = lax.dynamic_index_in_dim(total, self.outer, 0, keepdims=False)
-        for distance in range(1, 4):
-            piece = lax.dynamic_index_in_dim(
-                total, jnp.bitwise_xor(self.outer, distance), 0, keepdims=False
-            )
-            result = result + self.over_dp(piece, 2 * distance)
-        return result
+
+        def pair(near, far):
+            return [
+                lax.dynamic_index_in_dim(total, self.place_of(place), 0, keepdims=False)
+                for place in (near, far)
+            ]
+
+        return pair(0, 1), self.over_dp(jnp.concatenate(pair(2, 3), axis=0), 4)
+
+    def sum_near(self, far, marker):
+        (own, near), got = far
+        got = after(got, marker).astype(jnp.float32)
+        rows = own.shape[0]
+        sent = (near.astype(jnp.float32) + got[rows:]).astype(jnp.bfloat16)
+        return own.astype(jnp.float32) + got[:rows], self.over_dp(sent, 2)
+
+    def sum_end(self, near):
+        total, got = near
+        return total + got.astype(jnp.float32)
 
     def exchange(self, blocks):
-        got = [blocks[0]]
-        for flip in range(1, self.dp_size):
-            got.append(self.over_dp(blocks[flip], flip))
-        return jnp.stack(got)
-
-
-def arrange_kernel(widths, places_ref, *refs):
-    same, other, outs = refs[:4], refs[4:8], refs[8:]
-    step = pl.program_id(0)
-    rows = same[0].shape[0]
-    first = pl.multiple_of(places_ref[4] * rows, 16)
-    second = pl.multiple_of((1 - places_ref[4]) * rows, 16)
-    for distance in range(4):
-
-        @pl.when(step == distance)
-        def _(distance=distance):
-            start = 0
-            for out, width in zip(outs, widths):
-                columns = slice(start, start + width)
-                out[pl.ds(first, rows), :] = same[distance][:, columns]
-                out[pl.ds(second, rows), :] = other[distance][:, columns]
-                start += width
-
-
-def arrange_weights(places, same, other, widths):
-    rows, width = same[0].shape
+        return lax.all_to_all(blocks, "dp", split_axis=0, concat_axis=0, tiled=True)
+
+
+def split_columns(values, widths):
+    parts, start = [], 0
+    for width in widths:
+        parts.append(values[:, start : start + width])
+        start += width
+    return parts
+
+
+def move_kernel(order_ref, whole_ref, *outs):
+    start = 0
+    for out in outs:
+        width = out.shape[1]
+        out[...] = whole_ref[:, start : start + width]
+        start += width
+
+
+def move_blocks(order, gathered, widths):
+    rows, width = gathered.shape
+    block = rows // 4
     return pl.pallas_call(
-        functools.partial(arrange_kernel, widths),
-        out_shape=[jax.ShapeDtypeStruct((8 * rows, part), jnp.bfloat16) for part in widths],
+        move_kernel,
+        out_shape=[jax.ShapeDtypeStruct((rows, part), jnp.bfloat16) for part in widths],
         grid_spec=pltpu.PrefetchScalarGridSpec(
             num_scalar_prefetch=1,
             grid=(4,),
-            in_specs=[whole((rows, width))] * 8,
+            in_specs=[pl.BlockSpec((block, width), lambda i, order_ref: (order_ref[i], 0))],
             out_specs=[
-                pl.BlockSpec((2 * rows, part), lambda i, places_ref: (places_ref[i], 0))
-                for part in widths
+                pl.BlockSpec((block, part), lambda i, order_ref: (i, 0)) for part in widths
             ],
         ),
         cost_estimate=pl.CostEstimate(
-            flops=0, bytes_accessed=32 * rows * width, transcendentals=0
-        ),
-        name="arrange_weights",
-    )(places, *same, *other)
-
-
-def pack_rows(parts):
+            flops=0, bytes_accessed=4 * rows * width, transcendentals=0
+        ),
+        name="move_blocks",
+    )(order, gathered)
+
+
+def restore_kernel(order_ref, *refs):
+    out, start = refs[-1], 0
+    for ref in refs[:-1]:
+        width = ref.shape[1]
+        out[:, start : start + width] = ref[...]
+        start += width
+
+
+def restore_blocks(order, grads):
+    rows = grads[0].shape[0]
+    block = rows // 4
+    width = sum(grad.shape[1] for grad in grads)
+    return pl.pallas_call(
+        restore_kernel,
+        out_shape=jax.ShapeDtypeStruct((rows, width), jnp.bfloat16),
+        grid_spec=pltpu.PrefetchScalarGridSpec(
+            num_scalar_prefetch=1,
+            grid=(4,),
+            in_specs=[
+                pl.BlockSpec((block, grad.shape[1]), lambda i, order_ref: (i, 0))
+                for grad in grads
+            ],
+            out_specs=pl.BlockSpec((block, width), lambda i, order_ref: (order_ref[i], 0)),
+        ),
+        cost_estimate=pl.CostEstimate(
+            flops=0, bytes_accessed=4 * rows * width, transcendentals=0
+        ),
+        name="restore_blocks",
+    )(order, *grads)
+
+
+def pack_rows(parts, lanes):
     blocks = parts[0].shape[0]
     flat = jnp.concatenate([part.reshape(blocks, -1) for part in parts], axis=1)
     size = flat.shape[1]
-    rows = -(-size // (16 * LANES)) * 16
-    flat = jnp.pad(flat, ((0, 0), (0, rows * LANES - size)))
-    return flat.reshape(blocks, rows, LANES)
+    rows = -(-size // (16 * lanes)) * 16
+    flat = jnp.pad(flat, ((0, 0), (0, rows * lanes - size)))
+    return flat.reshape(blocks, rows, lanes)
 
 
 def unpack_rows(packed, shapes):
@@ -736,47 +768,41 @@
     slot = jnp.minimum(segment, SPG - 1)
     position = row_ids - jnp.where(slot == 0, 0, starts[slot])
     span = LMAX // dp_size
-    ranks = jnp.arange(dp_size, dtype=jnp.int32)
-    source_rows = (
-        jnp.bitwise_xor(position // span, group) * (SPG * span) + slot * span + position % span
-    )
+
+    small_parts = (
+        proj_weight,
+        mixer_gain,
+        conv_taps,
+        conv_bias,
+        proj_gains,
+        step_weight,
+        step_bias,
+        log_rate,
+        skip_gain,
+        ffn_gain,
+    )
+    small_shapes = [part.shape for part in small_parts]
+    small = pack_rows([part[None] for part in small_parts], tokens.shape[2])
+    small_rows = small.shape[1]
+    order = jnp.arange(dp_size, dtype=jnp.int32)
+    if wires.staged:
+        order = jnp.bitwise_xor(order, group)
+    dealt = tokens[deal.reshape(dp_size, SPG)[order].reshape(-1)].reshape(dp_size, SPG * span, -1)
+    sent = jnp.concatenate([dealt, jnp.broadcast_to(small, (dp_size,) + small.shape[1:])], axis=1)
+    if wires.staged:
+        arrived = jnp.stack(
+            [sent[0]] + [wires.over_dp(sent[flip], flip) for flip in range(1, dp_size)]
+        )
+    else:
+        arrived = wires.exchange(sent)
+    flat_rows = arrived.reshape(dp_size * (SPG * span + small_rows), -1)
+    origin = position // span
+    if wires.staged:
+        origin = jnp.bitwise_xor(origin, group)
+    source_rows = origin * (SPG * span + small_rows) + slot * span + position % span
     source_rows = jnp.where(live_rows, source_rows, 0)
-
-    dealt = deal.reshape(dp_size, SPG)[jnp.bitwise_xor(ranks, group)]
-    arrived = wires.exchange(tokens[dealt.reshape(-1)].reshape((dp_size, SPG) + tokens.shape[1:]))
-    flat_rows = arrived.reshape(dp_size * SPG * span, -1)
     packed = jnp.where(live_rows[:, None], flat_rows[source_rows], 0.0).astype(f32)
-
-    small_shapes = [
-        proj_weight.shape,
-        mixer_gain.shape,
-        conv_taps.shape,
-        conv_bias.shape,
-        proj_gains.shape,
-        step_weight.shape,
-        step_bias.shape,
-        log_rate.shape,
-        skip_gain.shape,
-        ffn_gain.shape,
-    ]
-    small = pack_rows(
-        [
-            part[None]
-            for part in (
-                proj_weight,
-                mixer_gain,
-                conv_taps,
-                conv_bias,
-                proj_gains,
-                step_weight,
-                step_bias,
-                log_rate,
-                skip_gain,
-                ffn_gain,
-            )
-        ]
-    )[0]
-    small = unpack_rows(wires.gather_rows(small), small_shapes)
+    small = unpack_rows(arrived[:, SPG * span :][order], small_shapes)
 
     def along_last(part):
         return jnp.moveaxis(part, 0, -2).reshape(part.shape[1:-1] + (-1,))
@@ -786,60 +812,78 @@
         along_last(part).astype(f32) for part in small[1:]
     ]
 
-    (inner_all, gate_all), mark = wires.gather_weights(
-        list(after((inner_weight, gate_weight), arrived))
-    )
-    (out_all,), mark = wires.gather_weights([after(out_weight.T, mark)])
-    (ffn_gate_all, ffn_up_all), mark = wires.gather_weights(
-        list(after((ffn_gate, ffn_up), mark))
-    )
-    (ffn_down_all,), mark = wires.gather_weights([after(ffn_down.T, mark)])
+    staged = wires.staged
+    in_width, out_width = [inner_weight.shape[1]], [out_weight.shape[0]]
+    down_width, ffn_widths = [ffn_down.shape[0]], [ffn_gate.shape[1], ffn_up.shape[1]]
+    inner_all, gate_all, out_all = wires.gather_whole(
+        jnp.concatenate([inner_weight, gate_weight, out_weight.T], axis=1), in_width * 2 + out_width
+    )
 
     inverse_in = row_scale(wires, packed)
     mixer_rows = wires.gather_features((packed * inverse_in[:, None] * gain_all).astype(bf16))
+    ffn_gate_all, ffn_up_all, ffn_down_all = wires.gather_whole(
+        after(jnp.concatenate([ffn_gate, ffn_up, ffn_down.T], axis=1), (inner_all, mixer_rows)),
+        ffn_widths + down_width,
+    )
     inner_pre = contract(mixer_rows, inner_all, 1, 0)
+    conv_out = conv_silu(inner_pre, taps_all, bias_all, segment).astype(bf16)
+    proj_terms = contract(conv_out, proj_all, 1, 0)
+    projected = wires.sum_rows(proj_terms, f32)
     gate_pre = contract(mixer_rows, gate_all, 1, 0)
-    conv_out = conv_silu(inner_pre, taps_all, bias_all, segment).astype(bf16)
-    projected = wires.sum_rows(contract(conv_out, proj_all, 1, 0), f32)
     operands = scan_operands(step_w_all, step_b_all, rate_all, skip_all, gains_all, HEAD_WIDTH)
+    out_cot = jnp.where(live_rows[:, None], out_grad, 0.0).astype(bf16)
     gated, scanned, states = scan_forward(
         bounds, projected, conv_out, gate_pre, operands, HEAD_WIDTH
     )
+    cot_rows, gated = wires.gather_features(after(out_cot, proj_terms), deadline=gated)
     residual = packed + wires.sum_features(lambda rows: contract(gated, out_all[rows], 1, 1))
 
     inverse_mid = row_scale(wires, residual)
-    ffn_rows = wires.gather_features((residual * inverse_mid[:, None] * ffn_gain_all).astype(bf16))
+    ffn_rows = wires.gather_features((residual * inverse_mid[:, None] * ffn_gain_all).astype(bf16), ffn_gate_all)
     gate_ffn = contract(ffn_rows, ffn_gate_all, 1, 0)
     up_ffn = contract(ffn_rows, ffn_up_all, 1, 0)
     logistic = jax.nn.sigmoid(gate_ffn)
     activated = gate_ffn * logistic
     hidden = (activated * up_ffn).astype(bf16)
-    final_rows = residual + wires.sum_features(
-        lambda rows: contract(hidden, ffn_down_all[rows], 1, 1)
-    )
-    output = jnp.where(live_rows[:, None], final_rows, 0.0).astype(bf16)
-
-    out_cot = jnp.where(live_rows[:, None], out_grad, 0.0).astype(bf16)
-    cot_rows = wires.gather_features(out_cot)
+
     hidden_grad = contract(cot_rows, ffn_down_all, 1, 0)
     gate_grad = (hidden_grad * up_ffn * logistic * (1.0 + gate_ffn * (1.0 - logistic))).astype(bf16)
     up_grad = (hidden_grad * activated).astype(bf16)
+    ffn_gate_terms = contract(ffn_rows, gate_grad, 0, 0).astype(bf16)
+    ffn_up_terms = contract(ffn_rows, up_grad, 0, 0).astype(bf16)
+    down_terms = contract(cot_rows, hidden, 0, 0).astype(bf16)
+    (ffn_down_grad, ffn_gate_grad, ffn_up_grad), sums_ready = wires.sum_whole(
+        [down_terms, ffn_gate_terms, ffn_up_terms]
+    )
     mid_grad = wires.sum_features(
         lambda rows: contract(gate_grad, ffn_gate_all[rows], 1, 1)
-        + contract(up_grad, ffn_up_all[rows], 1, 1)
-    )
-    ffn_down_grad = wires.sum_weights(contract(cot_rows, hidden, 0, 0).astype(bf16)).T
-    ffn_gate_grad = wires.sum_weights(contract(ffn_rows, gate_grad, 0, 0).astype(bf16))
-    ffn_up_grad = wires.sum_weights(contract(ffn_rows, up_grad, 0, 0).astype(bf16))
+        + contract(up_grad, ffn_up_all[rows], 1, 1),
+        until=sums_ready,
+    )
     mid_back, ffn_gain_grad = norm_back(wires, residual, inverse_mid, ffn_gain_all, mid_grad)
     residual_grad = out_cot.astype(f32) + mid_back
-
-    branch_rows = wires.gather_features(residual_grad.astype(bf16))
+    branch = residual_grad.astype(bf16)
+    branch_rows = wires.gather_features(branch)
     gated_grad = contract(branch_rows, out_all, 1, 0)
-    out_weight_grad = wires.sum_weights(contract(branch_rows, gated, 0, 0).astype(bf16)).T
+    final_rows = residual + wires.sum_features(
+        lambda rows: contract(hidden, ffn_down_all[rows], 1, 1), start=branch_rows
+    )
+    out_terms = contract(branch_rows, gated, 0, 0).astype(bf16)
+    if staged:
+        out_across = wires.sum_across(out_terms)
+        gated_grad = after(gated_grad, out_across[0])
+    else:
+        (out_weight_grad,), unused_sums = wires.sum_whole([out_terms])
     proj_part, conv_core_grad, gate_low, step_w_part, row_parts, skip_part = scan_backward(
         bounds, gated_grad, projected, conv_out, gate_pre, scanned, states, operands, HEAD_WIDTH
     )
+    gate_terms = contract(after(mixer_rows, proj_part), gate_low, 0, 0).astype(bf16)
+    if staged:
+        proj_part, final_rows = lax.optimization_barrier((proj_part, final_rows))
+    output = jnp.where(live_rows[:, None], final_rows, 0.0).astype(bf16)
+    if staged:
+        out_far = wires.sum_far(out_across, proj_part)
+        proj_part = after(proj_part, out_far[0])
     head_count = step_b_all.shape[0]
     gains_grad = wires.sum_small(row_parts)[0]
     proj_low = wires.sum_rows(proj_part, bf16).astype(bf16)
@@ -852,45 +896,57 @@
     unused_conv, conv_pull = jax.vjp(conv_piece, inner_pre, taps_all, bias_all)
     inner_grad, taps_grad, bias_grad = conv_pull(conv_grad)
     inner_low = inner_grad.astype(bf16)
+    inner_terms = contract(mixer_rows, inner_low, 0, 0).astype(bf16)
+    earlier = ffn_gate_grad
+    if staged:
+        out_near = wires.sum_near(out_far, inner_terms)
+        earlier = (ffn_gate_grad, out_near[0])
+    (inner_weight_grad, gate_weight_grad), last_joined = wires.sum_whole(
+        [inner_terms, gate_terms], earlier
+    )
     in_grad = wires.sum_features(
         lambda rows: contract(inner_low, inner_all[rows], 1, 1)
-        + contract(gate_low, gate_all[rows], 1, 1)
-    )
-    gate_weight_grad = wires.sum_weights(contract(mixer_rows, gate_low, 0, 0).astype(bf16))
-    inner_weight_grad = wires.sum_weights(contract(mixer_rows, inner_low, 0, 0).astype(bf16))
+        + contract(gate_low, gate_all[rows], 1, 1),
+        until=inner_terms,
+    )
     in_back, mixer_gain_grad = norm_back(wires, packed, inverse_in, gain_all, in_grad)
 
+    def by_index(part):
+        split = part.reshape(part.shape[:-1] + (dp_size, part.shape[-1] // dp_size))
+        return jnp.moveaxis(split, -2, 0)
+
+    small_grads = pack_rows(
+        [
+            part.astype(bf16)
+            for part in (
+                proj_weight_grad.reshape(dp_size, -1, proj_weight_grad.shape[1]),
+                by_index(mixer_gain_grad),
+                by_index(taps_grad),
+                by_index(bias_grad),
+                by_index(gains_grad),
+                by_index(step_w_part[:R, :head_count]),
+                by_index(row_parts[1, :head_count]),
+                by_index(row_parts[2, :head_count]),
+                by_index(skip_part[0]),
+                by_index(ffn_gain_grad),
+            )
+        ],
+        tokens.shape[2],
+    )
+
     grad_packed = (residual_grad + in_back).astype(bf16)
-    place = jnp.arange(span, dtype=jnp.int32)
-    slot_position = (jnp.bitwise_xor(ranks, group) * span)[:, None, None] + place[None, None, :]
+    slot_position = jnp.arange(LMAX, dtype=jnp.int32).reshape(dp_size, 1, span)
     slot_live = slot_position < group_lengths[None, :, None]
     slot_rows = jnp.where(slot_live, starts[None, :, None] + slot_position, 0).reshape(-1)
     leaving = jnp.where(slot_live.reshape(-1)[:, None], grad_packed[slot_rows], 0.0)
-    returned = wires.exchange(leaving.reshape(dp_size, SPG, span, -1))
+    leaving = leaving.reshape(dp_size, SPG * span, -1)
+    if staged:
+        out_weight_grad = wires.sum_end(out_near)
+    returned = wires.exchange(jnp.concatenate([leaving, small_grads], axis=1))
     inverse_deal = jnp.zeros_like(deal).at[deal].set(
         jnp.arange(deal.shape[0], dtype=jnp.int32)
     )
-    came_from = jnp.bitwise_xor(inverse_deal // SPG, group) * SPG + inverse_deal % SPG
-    tokens_grad = returned.reshape((dp_size * SPG, span, -1))[came_from]
-
-    def by_index(part):
-        split = part.reshape(part.shape[:-1] + (dp_size, part.shape[-1] // dp_size))
-        return jnp.moveaxis(split, -2, 0)
-
-    small_grads = pack_rows(
-        [
-            proj_weight_grad.reshape(dp_size, -1, proj_weight_grad.shape[1]),
-            by_index(mixer_gain_grad),
-            by_index(taps_grad),
-            by_index(bias_grad),
-            by_index(gains_grad),
-            by_index(step_w_part[:R, :head_count]),
-            by_index(row_parts[1, :head_count]),
-            by_index(row_parts[2, :head_count]),
-            by_index(skip_part[0]),
-            by_index(ffn_gain_grad),
-        ]
-    )
+    tokens_grad = returned[:, : SPG * span].reshape(dp_size * SPG, span, -1)[inverse_deal]
     (
         proj_weight_grad,
         mixer_gain_grad,
@@ -902,26 +958,29 @@
         rate_grad,
         skip_grad,
         ffn_gain_grad,
-    ) = [part[0] for part in unpack_rows(wires.sum_blocks(small_grads)[None], small_shapes)]
+    ) = unpack_rows(
+        jnp.sum(returned[:, SPG * span :].astype(f32), axis=0)[None], small_shapes
+    )
+
     return (
         output,
         tokens_grad,
-        mixer_gain_grad,
+        mixer_gain_grad[0],
         inner_weight_grad,
         gate_weight_grad,
-        taps_grad,
-        bias_grad,
-        proj_weight_grad,
-        gains_grad,
-        step_w_grad,
-        step_b_grad,
-        rate_grad,
-        skip_grad,
-        out_weight_grad,
-        ffn_gain_grad,
+        taps_grad[0],
+        bias_grad[0],
+        proj_weight_grad[0],
+        gains_grad[0],
+        step_w_grad[0],
+        step_b_grad[0],
+        rate_grad[0],
+        skip_grad[0],
+        out_weight_grad.T,
+        ffn_gain_grad[0],
         ffn_gate_grad,
         ffn_up_grad,
-        ffn_down_grad,
+        ffn_down_grad.T,
     )
 
 

time: 913 us -> 736 us (0.81)
  starting transfers between devices: 156 us -> 46.4 us
  waiting for transfers between devices: 391 us -> 297 us
  other arithmetic: 63.9 us -> 80.3 us
  between operations: 2.85 us -> 15.4 us
  matrix products: 134 us -> 123 us
    ppermute x74 -> x10, waiting for transfers between devices: 356 us -> 75.3 us  [over_dp(): return lax.ppermute(values, 'dp', swap_pairs(self.dp_size, flip))]
    ppermute x74 -> x10, starting transfers between devices: 139 us -> 18.6 us  [over_dp(): return lax.ppermute(values, 'dp', swap_pairs(self.dp_size, flip))]
    ppermute x36, waiting for transfers between devices: 35.1 us -> 129 us  [over_tensor(): return lax.ppermute(values, 'tensor', swap_pairs(self.tensor_size, flip))]
    all_to_all x0 -> x1, waiting for transfers between devices: none -> 58.1 us  [exchange(): return lax.all_to_all(blocks, 'dp', split_axis=0, concat_axis=0, tiled=True)]
    all_gather x0 -> x2, waiting for transfers between devices: none -> 34.1 us  [gather_whole(): whole_rows = lax.all_gather(shard, 'dp', axis=0, tiled=True)]
    concatenate x0 -> x6, other arithmetic: none -> 16.3 us  [the longest x2 9.48 us: gather_features(): rows = jnp.concatenate([values, across, beside, diagonal], axis=1)]
    dot_general x27, matrix products: 134 us -> 123 us  [contract(): lax.dot_general(left, right, (((left_dim,), (right_dim,)), ((), ())), pre...]
  transfers between devices with their start and end apart: 110 -> 51, of which waited for: 43 -> 28; matrix products, arithmetic and copies ran while one was open for 20% -> 30% of each run, Pallas kernels for 2% -> 13%
where the time goes in v2:
time: 736 us; the launch traced here: 728 us
  waiting for transfers between devices  297 us (40%)
  matrix products  123 us (17%)
  Pallas kernels  101 us (14%)
  other arithmetic  80.3 us (11%)
  local copies, waits for them, and re-layouts  65.5 us (9%)
  starting transfers between devices  46.4 us (6%)
  between operations  15.4 us (2%)
    ppermute x36, waiting for transfers between devices, over_tensor(): return lax.ppermute(values, 'tensor', swap_pairs(self.tensor_size, flip))  129 us
    dot_general x27, matrix products, contract(): lax.dot_general(left, right, (((left_dim,), (right_dim,)), ((), ())), pre...  123 us
    ppermute x10, waiting for transfers between devices, over_dp(): return lax.ppermute(values, 'dp', swap_pairs(self.dp_size, flip))  75.3 us
    all_to_all x1, waiting for transfers between devices, exchange(): return lax.all_to_all(blocks, 'dp', split_axis=0, concat_axis=0, tiled=True)  58.1 us
    pallas_call x1, Pallas kernels, scan_backward(): pl.pallas_call(functools.partial(scan_backward_kernel, head_width), out_s...  44.6 us
    all_gather x2, waiting for transfers between devices, gather_whole(): whole_rows = lax.all_gather(shard, 'dp', axis=0, tiled=True)  34.1 us
    pallas_call x1, Pallas kernels, scan_forward(): pl.pallas_call(functools.partial(scan_forward_kernel, head_width), out_sh...  26.3 us
    ppermute x36, starting transfers between devices, over_tensor(): return lax.ppermute(values, 'tensor', swap_pairs(self.tensor_size, flip))  22.8 us
  transfers between devices with their start and end apart: 51, of which 28 were waited for; matrix products, arithmetic and copies ran while one was open for 30% of the time, Pallas kernels for 13%

profile of v2, /device:TPU:0, one launch (start us, length us, event | category | flops | bytes accessed | tf_op | source)
XLA Modules:
  0.0 727.8 jit_solution(2511095304217949546)
XLA Ops:
  39.4 13.6 %collective-permute-done.1 = bf16[304,384]{1,0:T(8,128)(2,1)} collective-permute-done((bf16[304,384]{1,0:T(8,128)(2,1)}, bf16[304,384]{1,0:T(8,128)(2,1)}, u32[]{:S(2)}, u32[]{:S(2)}) %collective-permute-start.1) | collective-permute-done | bytes 233504 | tf_op jit(solution)/shard_map/ppermute | solution.py:506
  57.0 7.4 %collective-permute-done.2 = bf16[304,384]{1,0:T(8,128)(2,1)} collective-permute-done((bf16[304,384]{1,0:T(8,128)(2,1)S(1)}, bf16[304,384]{1,0:T(8,128)(2,1)}, u32[]{:S(2)}, u32[]{:S(2)}) %collective-permute-start.2) | collective-permute-done | bytes 233504 | tf_op jit(solution)/shard_map/ppermute | solution.py:506
  66.4 7.7 %collective-permute-done.4 = bf16[304,384]{1,0:T(8,128)(2,1)S(1)} collective-permute-done((bf16[304,384]{1,0:T(8,128)(2,1)S(1)}, bf16[304,384]{1,0:T(8,128)(2,1)S(1)}, u32[]{:S(2)}, u32[]{:S(2)}) %collective-permute-start.4) | collective-permute-done | bytes 233504 | tf_op jit(solution)/shard_map/ppermute | solution.py:506
  78.4 7.0 collective-permute-done.6
  98.7 21.5 %collective-permute-done.9 = bf16[1280,384]{0,1:T(8,128)(2,1)S(1)} collective-permute-done((bf16[1280,384]{0,1:T(8,128)(2,1)S(1)}, bf16[1280,384]{0,1:T(8,128)(2,1)S(1)}, u32[]{:S(2)}, u32[]{:S(2)}) %collective-permute-start.9) | collective-permute-done | bytes 983072 | tf_op jit(solution)/shard_map/ppermute | solution.py:503
  123.2 6.9 pad_maximum_fusion
  130.1 24.1 %all-gather.3.cloned.1.call-done.whole_ref = bf16[1536,2304]{1,0:T(8,128)(2,1)} async-done(((bf16[192,2304]{1,0:T(8,128)(2,1)}), bf16[1536,2304]{1,0:T(8,128)(2,1)}) %all-gather.3.cloned.1.call-update) | async-done | bytes 7077904 | tf_op jit(solution)/shard_map/all_gather | solution.py:572
  154.2 7.0 move_blocks.2
  166.6 6.9 fusion.82
  173.6 5.5 multiply_convert_fusion.3
  187.0 23.1 %collective-permute-done.16 = f32[640,128]{1,0:T(8,128)S(1)} collective-permute-done((f32[640,128]{1,0:T(8,128)S(1)}, f32[640,128]{1,0:T(8,128)S(1)}, u32[]{:S(2)}, u32[]{:S(2)}) %collective-permute-start.16) | collective-permute-done | bytes 327712 | tf_op jit(solution)/shard_map/ppermute | solution.py:503
  210.7 8.1 %fusion.84.gate_ref = f32[1280,768]{1,0:T(8,128)} fusion(bf16[1280,1536]{0,1:T(8,128)(2,1)} %pad_maximum_fusion, bf16[1536,768]{1,0:T(8,128)(2,1)} %get-tuple-element.53), kind=kOutput, calls=%fused_computation.285 | convolution fusion | flops 3019898880 | bytes 10223616 | tf_op jit(solution)/shard_map/dot_general | solution.py:25
  219.8 26.3 %scan_forward.1 = (bf16[1280,768]{1,0:T(8,128)(2,1)}, f32[1280,768]{1,0:T(8,128)}, f32[10,16,768]{2,1,0:T(8,128)}) custom-call(s32[2]{0:T(128)} %copy-done.58, f32[1280,128]{1,0:T(8,128)} %pad_maximum_fusion.6.proj_ref, bf16[1280,768]{1,0:T(8,128)(2,1)} %copy-done.8, f32[1280,768]{1,0:T(8,128)} %fusion.84.gate_ref, f32[8,128]{1,0:T(8,128)} %maximum_maximum_fusion.params_ref, ...), custom_call_target="tpu_custom_call" | custom-call | flops 100000000 | bytes 100000 | tf_op jit(solution)/shard_map/scan_forward/pallas_call | solution.py:401
  257.3 22.3 %collective-permute-done.19 = bf16[1280,384]{0,1:T(8,128)(2,1)S(1)} collective-permute-done((bf16[1280,384]{0,1:T(8,128)(2,1)S(1)}, bf16[1280,384]{0,1:T(8,128)(2,1)S(1)}, u32[]{:S(2)}, u32[]{:S(2)}) %collective-permute-start.19) | collective-permute-done | bytes 983072 | tf_op jit(solution)/shard_map/ppermute | solution.py:503
  287.7 9.9 %all-gather.5.cloned.1.call-done.whole_ref = bf16[1536,3072]{1,0:T(8,128)(2,1)} async-done(((bf16[192,3072]{1,0:T(8,128)(2,1)}), bf16[1536,3072]{1,0:T(8,128)(2,1)}) %all-gather.5.cloned.1.call-update) | async-done | bytes 9437200 | tf_op jit(solution)/shard_map/all_gather | solution.py:572
  297.7 8.7 %move_blocks.3 = (bf16[1536,1024]{1,0:T(8,128)(2,1)}, bf16[1536,1024]{1,0:T(8,128)(2,1)}, bf16[1536,1024]{1,0:T(8,128)(2,1)}) custom-call(s32[4]{0:T(128)} %pad_add_fusion.2.order_ref, bf16[1536,3072]{1,0:T(8,128)(2,1)} %all-gather.5.cloned.1.call-done.whole_ref), custom_call_target="tpu_custom_call" | custom-call | bytes 18874368 | tf_op jit(solution)/shard_map/move_blocks/pallas_call | solution.py:643
  313.7 8.6 %fusion.71 = f32[1280,1024]{1,0:T(8,128)} fusion(bf16[1536,1024]{1,0:T(8,128)(2,1)S(1)} %copy-done.68, bf16[1280,384]{0,1:T(8,128)(2,1)S(1)} %collective-permute-done.24, bf16[1280,384]{0,1:T(8,128)(2,1)} %collective-permute-done.23, bf16[1280,384]{0,1:T(8,128)(2,1)} %collective-permute-done.22, bf16[1280,384]{0,1:T(8,128)(2,1)} %multiply_convert_fusion.4), kind=kOutput, calls=%fused_computation.273 | convolution fusion | flops 4042260480 | bytes 12320768 | tf_op jit(solution)/shard_map/dot_general | solution.py:25
  322.3 8.7 %fusion.72 = f32[1280,1024]{1,0:T(8,128)} fusion(bf16[1536,1024]{1,0:T(8,128)(2,1)S(1)} %copy-done.67, bf16[1280,384]{0,1:T(8,128)(2,1)S(1)} %collective-permute-done.24, bf16[1280,384]{0,1:T(8,128)(2,1)} %collective-permute-done.23, bf16[1280,384]{0,1:T(8,128)(2,1)} %collective-permute-done.22, bf16[1280,384]{0,1:T(8,128)(2,1)} %multiply_convert_fusion.4), kind=kOutput, calls=%fused_computation.274 | convolution fusion | flops 4042260480 | bytes 12320768 | tf_op jit(solution)/shard_map/dot_general | solution.py:25
  331.0 10.5 %multiply_convert_fusion = (bf16[1280,1024]{1,0:T(8,128)(2,1)S(1)}, bf16[1280,1024]{1,0:T(8,128)(2,1)}, bf16[1280,1024]{1,0:T(8,128)(2,1)S(1)}) fusion(f32[1280,1024]{1,0:T(8,128)} %fusion.72, f32[1280,1024]{1,0:T(8,128)} %fusion.71, bf16[1280,1536]{0,1:T(8,128)(2,1)S(1)} %constant_dynamic-update-slice_fusion, bf16[1536,1024]{1,0:T(8,128)(2,1)S(1)} %copy-done.65), kind=kOutput, calls=%fused_computation.16 | convolution fusion | flops 4046192640 | bytes 25427968 | tf_op jit(solution)/shard_map/dot_general | solution.py:25
  351.5 8.6 %convolution_convert_fusion.1.refs_1_ = bf16[1536,1024]{1,0:T(8,128)(2,1)} fusion(bf16[1280,1024]{1,0:T(8,128)(2,1)} %get-tuple-element.181, bf16[1280,384]{0,1:T(8,128)(2,1)S(1)} %collective-permute-done.24, bf16[1280,384]{0,1:T(8,128)(2,1)} %collective-permute-done.23, bf16[1280,384]{0,1:T(8,128)(2,1)} %collective-permute-done.22, ...), kind=kOutput, calls=%fused_computation.50 | convolution fusion | flops 4043833344 | bytes 9699328 | tf_op jit(solution)/shard_map/dot_general | solution.py:25
  366.8 8.0 %convolution_convert_fusion.refs_2_ = bf16[1536,1024]{1,0:T(8,128)(2,1)} fusion(bf16[1280,1024]{1,0:T(8,128)(2,1)S(1)} %get-tuple-element.182, bf16[1280,384]{0,1:T(8,128)(2,1)S(1)} %collective-permute-done.24, bf16[1280,384]{0,1:T(8,128)(2,1)} %collective-permute-done.23, bf16[1280,384]{0,1:T(8,128)(2,1)} %collective-permute-done.22, ...), kind=kOutput, calls=%fused_computation.49 | convolution fusion | flops 4043833344 | bytes 9699328 | tf_op jit(solution)/shard_map/dot_general | solution.py:25
  374.8 5.6 convolution_convert_fusion.2.refs_0_
  380.4 8.3 %restore_blocks.2 = bf16[1536,3072]{1,0:T(8,128)(2,1)} custom-call(s32[4]{0:T(128)} %pad_add_fusion.2.order_ref, bf16[1536,1024]{1,0:T(8,128)(2,1)} %convolution_convert_fusion.2.refs_0_, bf16[1536,1024]{1,0:T(8,128)(2,1)} %convolution_convert_fusion.1.refs_1_, bf16[1536,1024]{1,0:T(8,128)(2,1)} %convolution_convert_fusion.refs_2_), custom_call_target="tpu_custom_call" | custom-call | bytes 18874368 | tf_op jit(solution)/shard_map/restore_blocks/pallas_call | solution.py:673
  402.2 21.1 %collective-permute-done.29 = bf16[1280,384]{0,1:T(8,128)(2,1)S(1)} collective-permute-done((bf16[1280,384]{0,1:T(8,128)(2,1)S(1)}, bf16[1280,384]{0,1:T(8,128)(2,1)S(1)}, u32[]{:S(2)}, u32[]{:S(2)}) %collective-permute-start.29) | collective-permute-done | bytes 983072 | tf_op jit(solution)/shard_map/ppermute | solution.py:503
  444.7 5.3 fusion.85.upstream_ref
  450.0 44.6 %scan_backward.1 = (f32[1280,128]{1,0:T(8,128)}, f32[1280,768]{1,0:T(8,128)}, bf16[1280,768]{1,0:T(8,128)(2,1)}, f32[128,128]{1,0:T(8,128)}, f32[8,128]{1,0:T(8,128)}, /*index=5*/f32[8,768]{1,0:T(8,128)}) custom-call(s32[2]{0:T(128)} %copy-done.58, f32[1280,768]{1,0:T(8,128)} %fusion.85.upstream_ref, f32[1280,128]{1,0:T(8,128)} %pad_maximum_fusion.6.proj_ref, ...), custom_call_target="tpu_custom_call" | custom-call | flops 100000000 | bytes 100000 | tf_op jit(solution)/shard_map/scan_backward/pallas_call | solution.py:442
  511.3 6.1 fusion.73
  533.2 33.4 %collective-permute-done.44 = bf16[384,768]{1,0:T(8,128)(2,1)} collective-permute-done((bf16[384,768]{1,0:T(8,128)(2,1)}, bf16[384,768]{1,0:T(8,128)(2,1)}, u32[]{:S(2)}, u32[]{:S(2)}) %collective-permute-start.44) | collective-permute-done | bytes 589856 | tf_op jit(solution)/shard_map/ppermute | solution.py:506
  574.4 5.9 restore_blocks.3
  603.3 17.4 %collective-permute-done.43 = f32[8,128]{1,0:T(8,128)S(1)} collective-permute-done((f32[8,128]{1,0:T(8,128)S(1)}, f32[8,128]{1,0:T(8,128)S(1)}, u32[]{:S(2)}, u32[]{:S(2)}) %collective-permute-start.43) | collective-permute-done | bytes 4128 | tf_op jit(solution)/shard_map/ppermute | solution.py:503
  633.4 7.5 %gather_fusion.5 = bf16[2048,384]{1,0:T(8,128)(2,1)S(1)} fusion(bf16[1280,384]{1,0:T(8,128)(2,1)S(1)} %copy.119, s32[2048]{0:T(1024)S(1)} %broadcast_clamp_fusion), kind=kCustom, calls=%fused_computation.5 | custom fusion | bytes 3153920 | tf_op jit(solution)/shard_map/gather | solution.py:941
  651.5 58.1 %all-to-all-done = bf16[8,304,384]{2,1,0:T(8,128)(2,1)S(1)} async-done(((bf16[8,304,384]{2,1,0:T(8,128)(2,1)}), bf16[8,304,384]{2,1,0:T(8,128)(2,1)S(1)}, u32[]{:S(2)}, u32[]{:S(2)}) %all-to-all-start) | async-done | bytes 1867808 | tf_op jit(solution)/shard_map/all_to_all | solution.py:621
  (464 shorter events, 248.8 us)
Async XLA Ops:
  7.2 147.0 %all-gather.3.cloned.1.call-start = ((), (), s32[]{:S(2)}) async-start(), calls=%async_computation.3 | async-start | bytes 7962624 | tf_op jit(solution)/shard_map/all_gather | solution.py:572
  9.5 288.1 %all-gather.5.cloned.1.call-start = ((), (), s32[]{:S(2)}) async-start(), calls=%async_computation.4 | async-start | bytes 10616832 | tf_op jit(solution)/shard_map/all_gather | solution.py:572
  19.6 15.1 %collective-permute-start = (bf16[304,384]{1,0:T(8,128)(2,1)}, bf16[304,384]{1,0:T(8,128)(2,1)}, u32[]{:S(2)}, u32[]{:S(2)}) collective-permute-start(bf16[304,384]{1,0:T(8,128)(2,1)} %get-tuple-element.187), channel_id=1, source_target_pairs={{0,4},{4,0},{8,12},{12,8},{16,20},{20,16},{24,28},{28,24},{1,5},{5... | collective-permute-start | bytes 700424 | tf_op jit(solution)/shard_map/ppermute | solution.py:506
  22.5 30.5 %collective-permute-start.1 = (bf16[304,384]{1,0:T(8,128)(2,1)}, bf16[304,384]{1,0:T(8,128)(2,1)}, u32[]{:S(2)}, u32[]{:S(2)}) collective-permute-start(bf16[304,384]{1,0:T(8,128)(2,1)} %get-tuple-element.188), channel_id=1, source_target_pairs={{0,8},{4,12},{8,0},{12,4},{16,24},{20,28},{24,16},{28,20},{1,9},{5... | collective-permute-start | bytes 700424 | tf_op jit(solution)/shard_map/ppermute | solution.py:506
  24.1 40.4 %collective-permute-start.2 = (bf16[304,384]{1,0:T(8,128)(2,1)S(1)}, bf16[304,384]{1,0:T(8,128)(2,1)}, u32[]{:S(2)}, u32[]{:S(2)}) collective-permute-start(bf16[304,384]{1,0:T(8,128)(2,1)S(1)} %get-tuple-element.189), channel_id=1, source_target_pairs={{0,12},{4,8},{8,4},{12,0},{16,28},{20,24},{24,20},{28,16},{1,13},{... | collective-permute-start | bytes 700424 | tf_op jit(solution)/shard_map/ppermute | solution.py:506
  24.1 41.3 %collective-permute-start.3 = (bf16[304,384]{1,0:T(8,128)(2,1)S(1)}, bf16[304,384]{1,0:T(8,128)(2,1)}, u32[]{:S(2)}, u32[]{:S(2)}) collective-permute-start(bf16[304,384]{1,0:T(8,128)(2,1)S(1)} %get-tuple-element.190), channel_id=1, source_target_pairs={{0,16},{4,20},{8,24},{12,28},{16,0},{20,4},{24,8},{28,12},{1,17},{... | collective-permute-start | bytes 700424 | tf_op jit(solution)/shard_map/ppermute | solution.py:506
  27.1 47.0 %collective-permute-start.4 = (bf16[304,384]{1,0:T(8,128)(2,1)S(1)}, bf16[304,384]{1,0:T(8,128)(2,1)S(1)}, u32[]{:S(2)}, u32[]{:S(2)}) collective-permute-start(bf16[304,384]{1,0:T(8,128)(2,1)S(1)} %get-tuple-element.191), channel_id=1, source_target_pairs={{0,20},{4,16},{8,28},{12,24},{16,4},{20,0},{24,12},{28,8},{1,21},{... | collective-permute-start | bytes 700424 | tf_op jit(solution)/shard_map/ppermute | solution.py:506
  34.7 43.6 %collective-permute-start.5 = (bf16[304,384]{1,0:T(8,128)(2,1)S(1)}, bf16[304,384]{1,0:T(8,128)(2,1)S(1)}, u32[]{:S(2)}, u32[]{:S(2)}) collective-permute-start(bf16[304,384]{1,0:T(8,128)(2,1)S(1)} %get-tuple-element.192), channel_id=1, source_target_pairs={{0,24},{4,28},{8,16},{12,20},{16,8},{20,12},{24,0},{28,4},{1,25},{... | collective-permute-start | bytes 700424 | tf_op jit(solution)/shard_map/ppermute | solution.py:506
  53.0 32.3 %collective-permute-start.6 = (bf16[304,384]{1,0:T(8,128)(2,1)S(1)}, bf16[304,384]{1,0:T(8,128)(2,1)S(1)}, u32[]{:S(2)}, u32[]{:S(2)}) collective-permute-start(bf16[304,384]{1,0:T(8,128)(2,1)S(1)} %get-tuple-element.185), channel_id=1, source_target_pairs={{0,28},{4,24},{8,20},{12,16},{16,12},{20,8},{24,4},{28,0},{1,29},{... | collective-permute-start | bytes 700424 | tf_op jit(solution)/shard_map/ppermute | solution.py:506
  97.1 23.1 %collective-permute-start.9 = (bf16[1280,384]{0,1:T(8,128)(2,1)S(1)}, bf16[1280,384]{0,1:T(8,128)(2,1)S(1)}, u32[]{:S(2)}, u32[]{:S(2)}) collective-permute-start(bf16[1280,384]{0,1:T(8,128)(2,1)S(1)} %fusion.10), channel_id=1, source_target_pairs={{0,2},{1,3},{2,0},{3,1},{4,6},{5,7},{6,4},{7,5},{8,10},{9,11},{10,... | collective-permute-start | bytes 2949128 | tf_op jit(solution)/shard_map/ppermute | solution.py:503
  98.7 24.5 %collective-permute-start.10 = (bf16[1280,384]{0,1:T(8,128)(2,1)S(1)}, bf16[1280,384]{0,1:T(8,128)(2,1)}, u32[]{:S(2)}, u32[]{:S(2)}) collective-permute-start(bf16[1280,384]{0,1:T(8,128)(2,1)S(1)} %fusion.10), channel_id=1, source_target_pairs={{0,1},{1,0},{2,3},{3,2},{4,5},{5,4},{6,7},{7,6},{8,9},{9,8},{10,11... | collective-permute-start | bytes 2949128 | tf_op jit(solution)/shard_map/ppermute | solution.py:503
  161.2 423.0 %reduce-scatter.3.cloned.1.call-start = ((), (), s32[]{:S(2)}) async-start(), calls=%async_computation.5 | async-start | bytes 10616832 | tf_op jit(solution)/shard_map/reduce_scatter | solution.py:585
  179.8 30.4 %collective-permute-start.12 = (bf16[1280,384]{0,1:T(8,128)(2,1)S(1)}, bf16[1280,384]{0,1:T(8,128)(2,1)}, u32[]{:S(2)}, u32[]{:S(2)}) collective-permute-start(bf16[1280,384]{0,1:T(8,128)(2,1)S(1)} %copy-done.17), channel_id=1, source_target_pairs={{0,2},{1,3},{2,0},{3,1},{4,6},{5,7},{6,4},{7,5},{8,10},{9,11},{10,... | collective-permute-start | bytes 2949128 | tf_op jit(solution)/shard_map/ppermute | solution.py:503
  185.3 24.8 %collective-permute-start.16 = (f32[640,128]{1,0:T(8,128)S(1)}, f32[640,128]{1,0:T(8,128)S(1)}, u32[]{:S(2)}, u32[]{:S(2)}) collective-permute-start(f32[640,128]{1,0:T(8,128)S(1)} %dynamic-slice_add_fusion), channel_id=1, source_target_pairs={{0,2},{1,3},{2,0},{3,1},{4,6},{5,7},{6,4},{7,5},{8,10},{9,11},{10,... | collective-permute-start | bytes 983048 | tf_op jit(solution)/shard_map/ppermute | solution.py:503
  186.8 59.3 %collective-permute-start.13 = (bf16[1280,384]{0,1:T(8,128)(2,1)S(1)}, bf16[1280,384]{0,1:T(8,128)(2,1)}, u32[]{:S(2)}, u32[]{:S(2)}) collective-permute-start(bf16[1280,384]{0,1:T(8,128)(2,1)S(1)} %copy-done.17), channel_id=1, source_target_pairs={{0,1},{1,0},{2,3},{3,2},{4,5},{5,4},{6,7},{7,6},{8,9},{9,8},{10,11... | collective-permute-start | bytes 2949128 | tf_op jit(solution)/shard_map/ppermute | solution.py:503
  210.2 35.9 %collective-permute-start.14 = (bf16[1280,384]{0,1:T(8,128)(2,1)}, bf16[1280,384]{0,1:T(8,128)(2,1)}, u32[]{:S(2)}, u32[]{:S(2)}) collective-permute-start(bf16[1280,384]{0,1:T(8,128)(2,1)} %collective-permute-done.12), channel_id=1, source_target_pairs={{0,1},{1,0},{2,3},{3,2},{4,5},{5,4},{6,7},{7,6},{8,9},{9,8},{10,11... | collective-permute-start | bytes 2949128 | tf_op jit(solution)/shard_map/ppermute | solution.py:503
  255.7 23.9 %collective-permute-start.19 = (bf16[1280,384]{0,1:T(8,128)(2,1)S(1)}, bf16[1280,384]{0,1:T(8,128)(2,1)S(1)}, u32[]{:S(2)}, u32[]{:S(2)}) collective-permute-start(bf16[1280,384]{0,1:T(8,128)(2,1)S(1)} %slice.580), channel_id=1, source_target_pairs={{0,2},{1,3},{2,0},{3,1},{4,6},{5,7},{6,4},{7,5},{8,10},{9,11},{10,... | collective-permute-start | bytes 2949128 | tf_op jit(solution)/shard_map/ppermute | solution.py:503
  286.2 23.4 %collective-permute-start.22 = (bf16[1280,384]{0,1:T(8,128)(2,1)}, bf16[1280,384]{0,1:T(8,128)(2,1)}, u32[]{:S(2)}, u32[]{:S(2)}) collective-permute-start(bf16[1280,384]{0,1:T(8,128)(2,1)} %multiply_convert_fusion.4), channel_id=1, source_target_pairs={{0,2},{1,3},{2,0},{3,1},{4,6},{5,7},{6,4},{7,5},{8,10},{9,11},{10,... | collective-permute-start | bytes 2949128 | tf_op jit(solution)/shard_map/ppermute | solution.py:503
  287.7 25.9 %collective-permute-start.23 = (bf16[1280,384]{0,1:T(8,128)(2,1)}, bf16[1280,384]{0,1:T(8,128)(2,1)}, u32[]{:S(2)}, u32[]{:S(2)}) collective-permute-start(bf16[1280,384]{0,1:T(8,128)(2,1)} %multiply_convert_fusion.4), channel_id=1, source_target_pairs={{0,1},{1,0},{2,3},{3,2},{4,5},{5,4},{6,7},{7,6},{8,9},{9,8},{10,11... | collective-permute-start | bytes 2949128 | tf_op jit(solution)/shard_map/ppermute | solution.py:503
  348.7 11.4 %collective-permute-start.25 = (bf16[1280,768]{0,1:T(8,128)(2,1)S(1)}, bf16[1280,768]{0,1:T(8,128)(2,1)S(1)}, u32[]{:S(2)}, u32[]{:S(2)}) collective-permute-start(bf16[1280,768]{0,1:T(8,128)(2,1)S(1)} %add_convert_fusion.2), channel_id=1, source_target_pairs={{0,1},{1,0},{2,3},{3,2},{4,5},{5,4},{6,7},{7,6},{8,9},{9,8},{10,11... | collective-permute-start | bytes 5898248 | tf_op jit(solution)/shard_map/ppermute | solution.py:503
  365.3 23.9 %collective-permute-start.26 = (bf16[1280,384]{0,1:T(8,128)(2,1)}, bf16[1280,384]{0,1:T(8,128)(2,1)S(1)}, u32[]{:S(2)}, u32[]{:S(2)}) collective-permute-start(bf16[1280,384]{0,1:T(8,128)(2,1)} %slice.579), channel_id=1, source_target_pairs={{0,2},{1,3},{2,0},{3,1},{4,6},{5,7},{6,4},{7,5},{8,10},{9,11},{10,... | collective-permute-start | bytes 2949128 | tf_op jit(solution)/shard_map/ppermute | solution.py:503
  394.6 324.3 %reduce-scatter.5.cloned.1.call-start = ((), (), s32[]{:S(2)}) async-start(), calls=%async_computation.6 | async-start | bytes 5308416 | tf_op jit(solution)/shard_map/reduce_scatter | solution.py:585
  400.7 22.6 %collective-permute-start.29 = (bf16[1280,384]{0,1:T(8,128)(2,1)S(1)}, bf16[1280,384]{0,1:T(8,128)(2,1)S(1)}, u32[]{:S(2)}, u32[]{:S(2)}) collective-permute-start(bf16[1280,384]{0,1:T(8,128)(2,1)S(1)} %get-tuple-element.172), channel_id=1, source_target_pairs={{0,2},{1,3},{2,0},{3,1},{4,6},{5,7},{6,4},{7,5},{8,10},{9,11},{10,... | collective-permute-start | bytes 2949128 | tf_op jit(solution)/shard_map/ppermute | solution.py:503
  402.2 24.7 %collective-permute-start.30 = (bf16[1280,384]{0,1:T(8,128)(2,1)S(1)}, bf16[1280,384]{0,1:T(8,128)(2,1)S(1)}, u32[]{:S(2)}, u32[]{:S(2)}) collective-permute-start(bf16[1280,384]{0,1:T(8,128)(2,1)S(1)} %get-tuple-element.172), channel_id=1, source_target_pairs={{0,1},{1,0},{2,3},{3,2},{4,5},{5,4},{6,7},{7,6},{8,9},{9,8},{10,11... | collective-permute-start | bytes 2949128 | tf_op jit(solution)/shard_map/ppermute | solution.py:503
  437.7 56.9 %collective-permute-start.33 = (bf16[1280,384]{0,1:T(8,128)(2,1)}, bf16[1280,384]{0,1:T(8,128)(2,1)}, u32[]{:S(2)}, u32[]{:S(2)}) collective-permute-start(bf16[1280,384]{0,1:T(8,128)(2,1)} %slice.578), channel_id=1, source_target_pairs={{0,2},{1,3},{2,0},{3,1},{4,6},{5,7},{6,4},{7,5},{8,10},{9,11},{10,... | collective-permute-start | bytes 2949128 | tf_op jit(solution)/shard_map/ppermute | solution.py:503
  443.8 53.9 %collective-permute-start.34 = (bf16[4,192,768]{2,1,0:T(8,128)(2,1)}, bf16[4,192,768]{2,1,0:T(8,128)(2,1)}, u32[]{:S(2)}, u32[]{:S(2)}) collective-permute-start(bf16[4,192,768]{2,1,0:T(8,128)(2,1)} %get-tuple-element.183), channel_id=1, source_target_pairs={{0,4},{4,0},{8,12},{12,8},{16,20},{20,16},{24,28},{28,24},{1,5},{5... | collective-permute-start | bytes 3538952 | tf_op jit(solution)/shard_map/ppermute | solution.py:506
  509.2 57.5 %collective-permute-start.44 = (bf16[384,768]{1,0:T(8,128)(2,1)}, bf16[384,768]{1,0:T(8,128)(2,1)}, u32[]{:S(2)}, u32[]{:S(2)}) collective-permute-start(bf16[384,768]{1,0:T(8,128)(2,1)} %pad_maximum_fusion.7), channel_id=1, source_target_pairs={{0,16},{4,20},{8,24},{12,28},{16,0},{20,4},{24,8},{28,12},{1,17},{... | collective-permute-start | bytes 1769480 | tf_op jit(solution)/shard_map/ppermute | solution.py:506
  528.6 61.7 %collective-permute-start.38 = (bf16[1280,768]{0,1:T(8,128)(2,1)}, bf16[1280,768]{0,1:T(8,128)(2,1)}, u32[]{:S(2)}, u32[]{:S(2)}) collective-permute-start(bf16[1280,768]{0,1:T(8,128)(2,1)} %add_convert_fusion), channel_id=1, source_target_pairs={{0,1},{1,0},{2,3},{3,2},{4,5},{5,4},{6,7},{7,6},{8,9},{9,8},{10,11... | collective-permute-start | bytes 5898248 | tf_op jit(solution)/shard_map/ppermute | solution.py:503
  568.6 13.8 %collective-permute-start.45 = (bf16[192,768]{1,0:T(8,128)(2,1)}, bf16[192,768]{1,0:T(8,128)(2,1)}, u32[]{:S(2)}, u32[]{:S(2)}) collective-permute-start(bf16[192,768]{1,0:T(8,128)(2,1)} %fusion.36), channel_id=1, source_target_pairs={{0,8},{4,12},{8,0},{12,4},{16,24},{20,28},{24,16},{28,20},{1,9},{5... | collective-permute-start | bytes 884744 | tf_op jit(solution)/shard_map/ppermute | solution.py:506
  596.6 24.8 %collective-permute-start.39 = (bf16[1280,384]{0,1:T(8,128)(2,1)}, bf16[1280,384]{0,1:T(8,128)(2,1)}, u32[]{:S(2)}, u32[]{:S(2)}) collective-permute-start(bf16[1280,384]{0,1:T(8,128)(2,1)} %slice.577), channel_id=1, source_target_pairs={{0,2},{1,3},{2,0},{3,1},{4,6},{5,7},{6,4},{7,5},{8,10},{9,11},{10,... | collective-permute-start | bytes 2949128 | tf_op jit(solution)/shard_map/ppermute | solution.py:503
  601.2 19.5 %collective-permute-start.43 = (f32[8,128]{1,0:T(8,128)S(1)}, f32[8,128]{1,0:T(8,128)S(1)}, u32[]{:S(2)}, u32[]{:S(2)}) collective-permute-start(f32[8,128]{1,0:T(8,128)S(1)} %get-tuple-element.227), channel_id=1, source_target_pairs={{0,2},{1,3},{2,0},{3,1},{4,6},{5,7},{6,4},{7,5},{8,10},{9,11},{10,... | collective-permute-start | bytes 12296 | tf_op jit(solution)/shard_map/ppermute | solution.py:503
  642.7 66.9 %all-to-all-start = ((bf16[8,304,384]{2,1,0:T(8,128)(2,1)}), bf16[8,304,384]{2,1,0:T(8,128)(2,1)S(1)}, u32[]{:S(2)}, u32[]{:S(2)}) async-start(bf16[8,304,384]{2,1,0:T(8,128)(2,1)} %pad_maximum_fusion.3), calls=%async_computation | async-start | bytes 3735552 | tf_op jit(solution)/shard_map/all_to_all | solution.py:621
  (99 other events, 1175.1 us)
Sparse Core Ops, SparseCore 0:
  10.2 143.9 all-gather.2
  161.3 136.2 all-gather.4
  394.7 184.1 reduce-scatter.2
  587.1 122.6 reduce-scatter.4

commit v3 on v2

--- a/solution.py
+++ b/solution.py
@@ -869,11 +869,6 @@
         lambda rows: contract(hidden, ffn_down_all[rows], 1, 1), start=branch_rows
     )
     out_terms = contract(branch_rows, gated, 0, 0).astype(bf16)
-    if staged:
-        out_across = wires.sum_across(out_terms)
-        gated_grad = after(gated_grad, out_across[0])
-    else:
-        (out_weight_grad,), unused_sums = wires.sum_whole([out_terms])
     proj_part, conv_core_grad, gate_low, step_w_part, row_parts, skip_part = scan_backward(
         bounds, gated_grad, projected, conv_out, gate_pre, scanned, states, operands, HEAD_WIDTH
     )
@@ -881,9 +876,6 @@
     if staged:
         proj_part, final_rows = lax.optimization_barrier((proj_part, final_rows))
     output = jnp.where(live_rows[:, None], final_rows, 0.0).astype(bf16)
-    if staged:
-        out_far = wires.sum_far(out_across, proj_part)
-        proj_part = after(proj_part, out_far[0])
     head_count = step_b_all.shape[0]
     gains_grad = wires.sum_small(row_parts)[0]
     proj_low = wires.sum_rows(proj_part, bf16).astype(bf16)
@@ -897,12 +889,8 @@
     inner_grad, taps_grad, bias_grad = conv_pull(conv_grad)
     inner_low = inner_grad.astype(bf16)
     inner_terms = contract(mixer_rows, inner_low, 0, 0).astype(bf16)
-    earlier = ffn_gate_grad
-    if staged:
-        out_near = wires.sum_near(out_far, inner_terms)
-        earlier = (ffn_gate_grad, out_near[0])
-    (inner_weight_grad, gate_weight_grad), last_joined = wires.sum_whole(
-        [inner_terms, gate_terms], earlier
+    (inner_weight_grad, gate_weight_grad, out_weight_grad), last_joined = wires.sum_whole(
+        [inner_terms, gate_terms, out_terms], ffn_gate_grad
     )
     in_grad = wires.sum_features(
         lambda rows: contract(inner_low, inner_all[rows], 1, 1)
@@ -940,8 +928,6 @@
     slot_rows = jnp.where(slot_live, starts[None, :, None] + slot_position, 0).reshape(-1)
     leaving = jnp.where(slot_live.reshape(-1)[:, None], grad_packed[slot_rows], 0.0)
     leaving = leaving.reshape(dp_size, SPG * span, -1)
-    if staged:
-        out_weight_grad = wires.sum_end(out_near)
     returned = wires.exchange(jnp.concatenate([leaving, small_grads], axis=1))
     inverse_deal = jnp.zeros_like(deal).at[deal].set(
         jnp.arange(deal.shape[0], dtype=jnp.int32)

time: 736 us -> 708 us (0.962)
  other arithmetic: 80.3 us -> 67 us
    ppermute x10 -> x7, waiting for transfers between devices: 75.3 us -> 39.9 us  [over_dp(): return lax.ppermute(values, 'dp', swap_pairs(self.dp_size, flip))]
    reduce_scatter x2, waiting for transfers between devices: 0.01 us -> 27 us  [sum_whole(): total = lax.psum_scatter(joined, 'dp', scatter_dimension=0, tiled=True)]
    ppermute x36, waiting for transfers between devices: 129 us -> 151 us  [over_tensor(): return lax.ppermute(values, 'tensor', swap_pairs(self.tensor_size, flip))]
    all_to_all x1, waiting for transfers between devices: 58.1 us -> 39.3 us  [exchange(): return lax.all_to_all(blocks, 'dp', split_axis=0, concat_axis=0, tiled=True)]
    ppermute x10 -> x7, starting transfers between devices: 18.6 us -> 15.5 us  [over_dp(): return lax.ppermute(values, 'dp', swap_pairs(self.dp_size, flip))]
    unnamed x176 -> x166, local copies, waits for them, and re-layouts: 17.6 us -> 18.1 us
  transfers between devices with their start and end apart: 51 -> 48, of which waited for: 28 -> 30; matrix products, arithmetic and copies ran while one was open for 30% -> 29% of each run, Pallas kernels for 13% -> 14%
where the time goes in v3:
time: 708 us; the launch traced here: 700 us
  waiting for transfers between devices  291 us (41%)
  matrix products  120 us (17%)
  Pallas kernels  102 us (14%)
  other arithmetic  67 us (9%)
  local copies, waits for them, and re-layouts  63.8 us (9%)
  starting transfers between devices  41.4 us (6%)
  between operations  15.4 us (2%)
    ppermute x36, waiting for transfers between devices, over_tensor(): return lax.ppermute(values, 'tensor', swap_pairs(self.tensor_size, flip))  151 us
    dot_general x27, matrix products, contract(): lax.dot_general(left, right, (((left_dim,), (right_dim,)), ((), ())), pre...  120 us
    pallas_call x1, Pallas kernels, scan_backward(): pl.pallas_call(functools.partial(scan_backward_kernel, head_width), out_s...  44.4 us
    ppermute x7, waiting for transfers between devices, over_dp(): return lax.ppermute(values, 'dp', swap_pairs(self.dp_size, flip))  39.9 us
    all_to_all x1, waiting for transfers between devices, exchange(): return lax.all_to_all(blocks, 'dp', split_axis=0, concat_axis=0, tiled=True)  39.3 us
    all_gather x2, waiting for transfers between devices, gather_whole(): whole_rows = lax.all_gather(shard, 'dp', axis=0, tiled=True)  33.9 us
    reduce_scatter x2, waiting for transfers between devices, sum_whole(): total = lax.psum_scatter(joined, 'dp', scatter_dimension=0, tiled=True)  27 us
    pallas_call x1, Pallas kernels, scan_forward(): pl.pallas_call(functools.partial(scan_forward_kernel, head_width), out_sh...  26.5 us
  transfers between devices with their start and end apart: 48, of which 30 were waited for; matrix products, arithmetic and copies ran while one was open for 29% of the time, Pallas kernels for 14%

profile of v3, /device:TPU:0, one launch (start us, length us, event | category | flops | bytes accessed | tf_op | source)
XLA Modules:
  0.0 700.5 jit_solution(6363979947442705357)
XLA Ops:
  39.4 13.6 %collective-permute-done.1 = bf16[304,384]{1,0:T(8,128)(2,1)} collective-permute-done((bf16[304,384]{1,0:T(8,128)(2,1)}, bf16[304,384]{1,0:T(8,128)(2,1)}, u32[]{:S(2)}, u32[]{:S(2)}) %collective-permute-start.1) | collective-permute-done | bytes 233504 | tf_op jit(solution)/shard_map/ppermute | solution.py:506
  57.0 7.4 %collective-permute-done.2 = bf16[304,384]{1,0:T(8,128)(2,1)} collective-permute-done((bf16[304,384]{1,0:T(8,128)(2,1)S(1)}, bf16[304,384]{1,0:T(8,128)(2,1)}, u32[]{:S(2)}, u32[]{:S(2)}) %collective-permute-start.2) | collective-permute-done | bytes 233504 | tf_op jit(solution)/shard_map/ppermute | solution.py:506
  66.4 7.7 %collective-permute-done.4 = bf16[304,384]{1,0:T(8,128)(2,1)S(1)} collective-permute-done((bf16[304,384]{1,0:T(8,128)(2,1)S(1)}, bf16[304,384]{1,0:T(8,128)(2,1)S(1)}, u32[]{:S(2)}, u32[]{:S(2)}) %collective-permute-start.4) | collective-permute-done | bytes 233504 | tf_op jit(solution)/shard_map/ppermute | solution.py:506
  78.4 7.0 collective-permute-done.6
  98.7 21.6 %collective-permute-done.9 = bf16[1280,384]{0,1:T(8,128)(2,1)S(1)} collective-permute-done((bf16[1280,384]{0,1:T(8,128)(2,1)S(1)}, bf16[1280,384]{0,1:T(8,128)(2,1)S(1)}, u32[]{:S(2)}, u32[]{:S(2)}) %collective-permute-start.9) | collective-permute-done | bytes 983072 | tf_op jit(solution)/shard_map/ppermute | solution.py:503
  123.2 6.9 pad_maximum_fusion
  130.1 24.1 %all-gather.3.cloned.1.call-done.whole_ref = bf16[1536,2304]{1,0:T(8,128)(2,1)} async-done(((bf16[192,2304]{1,0:T(8,128)(2,1)}), bf16[1536,2304]{1,0:T(8,128)(2,1)}) %all-gather.3.cloned.1.call-update) | async-done | bytes 7077904 | tf_op jit(solution)/shard_map/all_gather | solution.py:572
  154.2 7.0 %move_blocks.2 = (bf16[1536,768]{1,0:T(8,128)(2,1)}, bf16[1536,768]{1,0:T(8,128)(2,1)}, bf16[1536,768]{1,0:T(8,128)(2,1)}) custom-call(s32[4]{0:T(128)} %pad_add_fusion.2.order_ref, bf16[1536,2304]{1,0:T(8,128)(2,1)} %all-gather.3.cloned.1.call-done.whole_ref), custom_call_target="tpu_custom_call" | custom-call | bytes 14155776 | tf_op jit(solution)/shard_map/move_blocks/pallas_call | solution.py:643
  166.7 6.9 fusion.81
  187.0 23.1 %collective-permute-done.16 = f32[640,128]{1,0:T(8,128)S(1)} collective-permute-done((f32[640,128]{1,0:T(8,128)S(1)}, f32[640,128]{1,0:T(8,128)S(1)}, u32[]{:S(2)}, u32[]{:S(2)}) %collective-permute-start.16) | collective-permute-done | bytes 327712 | tf_op jit(solution)/shard_map/ppermute | solution.py:503
  210.8 8.1 %fusion.83.gate_ref = f32[1280,768]{1,0:T(8,128)} fusion(bf16[1280,1536]{0,1:T(8,128)(2,1)} %pad_maximum_fusion, bf16[1536,768]{1,0:T(8,128)(2,1)} %get-tuple-element.49), kind=kOutput, calls=%fused_computation.274 | convolution fusion | flops 3019898880 | bytes 10223616 | tf_op jit(solution)/shard_map/dot_general | solution.py:25
  219.8 26.5 %scan_forward.1 = (bf16[1280,768]{1,0:T(8,128)(2,1)}, f32[1280,768]{1,0:T(8,128)}, f32[10,16,768]{2,1,0:T(8,128)}) custom-call(s32[2]{0:T(128)} %copy-done.50, f32[1280,128]{1,0:T(8,128)} %pad_maximum_fusion.6.proj_ref, bf16[1280,768]{1,0:T(8,128)(2,1)} %copy-done.8, f32[1280,768]{1,0:T(8,128)} %fusion.83.gate_ref, f32[8,128]{1,0:T(8,128)} %maximum_maximum_fusion.params_ref, ...), custom_call_target="tpu_custom_call" | custom-call | flops 100000000 | bytes 100000 | tf_op jit(solution)/shard_map/scan_forward/pallas_call | solution.py:401
  257.5 22.3 %collective-permute-done.19 = bf16[1280,384]{0,1:T(8,128)(2,1)S(1)} collective-permute-done((bf16[1280,384]{0,1:T(8,128)(2,1)S(1)}, bf16[1280,384]{0,1:T(8,128)(2,1)S(1)}, u32[]{:S(2)}, u32[]{:S(2)}) %collective-permute-start.19) | collective-permute-done | bytes 983072 | tf_op jit(solution)/shard_map/ppermute | solution.py:503
  287.9 9.8 %all-gather.5.cloned.1.call-done.whole_ref = bf16[1536,3072]{1,0:T(8,128)(2,1)} async-done(((bf16[192,3072]{1,0:T(8,128)(2,1)}), bf16[1536,3072]{1,0:T(8,128)(2,1)}) %all-gather.5.cloned.1.call-update) | async-done | bytes 9437200 | tf_op jit(solution)/shard_map/all_gather | solution.py:572
  297.7 8.3 %move_blocks.3 = (bf16[1536,1024]{1,0:T(8,128)(2,1)}, bf16[1536,1024]{1,0:T(8,128)(2,1)}, bf16[1536,1024]{1,0:T(8,128)(2,1)}) custom-call(s32[4]{0:T(128)} %pad_add_fusion.2.order_ref, bf16[1536,3072]{1,0:T(8,128)(2,1)} %all-gather.5.cloned.1.call-done.whole_ref), custom_call_target="tpu_custom_call" | custom-call | bytes 18874368 | tf_op jit(solution)/shard_map/move_blocks/pallas_call | solution.py:643
  313.9 6.1 fusion.70
  319.9 8.6 %fusion.71 = f32[1280,1024]{1,0:T(8,128)} fusion(bf16[1536,1024]{1,0:T(8,128)(2,1)S(1)} %copy-done.59, bf16[1280,384]{0,1:T(8,128)(2,1)S(1)} %collective-permute-done.24, bf16[1280,384]{0,1:T(8,128)(2,1)} %collective-permute-done.23, bf16[1280,384]{0,1:T(8,128)(2,1)} %collective-permute-done.22, bf16[1280,384]{0,1:T(8,128)(2,1)} %multiply_convert_fusion.4), kind=kOutput, calls=%fused_computation.263 | convolution fusion | flops 4042260480 | bytes 12320768 | tf_op jit(solution)/shard_map/dot_general | solution.py:25
  328.6 10.7 %multiply_convert_fusion = (bf16[1280,1024]{1,0:T(8,128)(2,1)}, bf16[1280,1024]{1,0:T(8,128)(2,1)}, bf16[1280,1024]{1,0:T(8,128)(2,1)}) fusion(f32[1280,1024]{1,0:T(8,128)} %fusion.71, f32[1280,1024]{1,0:T(8,128)S(1)} %fusion.70, bf16[1280,1536]{0,1:T(8,128)(2,1)S(1)} %constant_dynamic-update-slice_fusion, bf16[1536,1024]{1,0:T(8,128)(2,1)S(1)} %copy-done.57), kind=kOutput, calls=%fused_computation.16 | convolution fusion | flops 4046192640 | bytes 25427968 | tf_op jit(solution)/shard_map/dot_general | solution.py:25
  347.5 7.8 %convolution_convert_fusion.1.refs_1_ = bf16[1536,1024]{1,0:T(8,128)(2,1)} fusion(bf16[1280,1024]{1,0:T(8,128)(2,1)S(1)} %copy-done.74, bf16[1280,384]{0,1:T(8,128)(2,1)S(1)} %collective-permute-done.24, bf16[1280,384]{0,1:T(8,128)(2,1)} %collective-permute-done.23, bf16[1280,384]{0,1:T(8,128)(2,1)} %collective-permute-done.22, ...), kind=kOutput, calls=%fused_computation.50 | convolution fusion | flops 4043833344 | bytes 9699328 | tf_op jit(solution)/shard_map/dot_general | solution.py:25
  355.3 7.9 %convolution_convert_fusion.refs_2_ = bf16[1536,1024]{1,0:T(8,128)(2,1)} fusion(bf16[1280,1024]{1,0:T(8,128)(2,1)S(1)} %copy-done.70, bf16[1280,384]{0,1:T(8,128)(2,1)S(1)} %collective-permute-done.24, bf16[1280,384]{0,1:T(8,128)(2,1)} %collective-permute-done.23, bf16[1280,384]{0,1:T(8,128)(2,1)} %collective-permute-done.22, ...), kind=kOutput, calls=%fused_computation.49 | convolution fusion | flops 4043833344 | bytes 9699328 | tf_op jit(solution)/shard_map/dot_general | solution.py:25
  363.2 5.6 convolution_convert_fusion.2.refs_0_
  368.8 8.3 %restore_blocks.2 = bf16[1536,3072]{1,0:T(8,128)(2,1)} custom-call(s32[4]{0:T(128)} %pad_add_fusion.2.order_ref, bf16[1536,1024]{1,0:T(8,128)(2,1)} %convolution_convert_fusion.2.refs_0_, bf16[1536,1024]{1,0:T(8,128)(2,1)} %convolution_convert_fusion.1.refs_1_, bf16[1536,1024]{1,0:T(8,128)(2,1)} %convolution_convert_fusion.refs_2_), custom_call_target="tpu_custom_call" | custom-call | bytes 18874368 | tf_op jit(solution)/shard_map/restore_blocks/pallas_call | solution.py:673
  387.8 21.9 %collective-permute-done.26 = bf16[1280,384]{0,1:T(8,128)(2,1)S(1)} collective-permute-done((bf16[1280,384]{0,1:T(8,128)(2,1)S(1)}, bf16[1280,384]{0,1:T(8,128)(2,1)S(1)}, u32[]{:S(2)}, u32[]{:S(2)}) %collective-permute-start.26) | collective-permute-done | bytes 983072 | tf_op jit(solution)/shard_map/ppermute | solution.py:503
  418.6 21.7 %collective-permute-done.29 = bf16[1280,384]{0,1:T(8,128)(2,1)S(1)} collective-permute-done((bf16[1280,384]{0,1:T(8,128)(2,1)S(1)}, bf16[1280,384]{0,1:T(8,128)(2,1)S(1)}, u32[]{:S(2)}, u32[]{:S(2)}) %collective-permute-start.29) | collective-permute-done | bytes 983072 | tf_op jit(solution)/shard_map/ppermute | solution.py:503
  455.8 44.4 %scan_backward.1 = (f32[1280,128]{1,0:T(8,128)}, f32[1280,768]{1,0:T(8,128)}, bf16[1280,768]{1,0:T(8,128)(2,1)}, f32[128,128]{1,0:T(8,128)}, f32[8,128]{1,0:T(8,128)}, /*index=5*/f32[8,768]{1,0:T(8,128)}) custom-call(s32[2]{0:T(128)} %copy-done.50, f32[1280,768]{1,0:T(8,128)} %fusion.84.upstream_ref, f32[1280,128]{1,0:T(8,128)} %pad_maximum_fusion.6.proj_ref, ...), custom_call_target="tpu_custom_call" | custom-call | flops 100000000 | bytes 100000 | tf_op jit(solution)/shard_map/scan_backward/pallas_call | solution.py:442
  518.4 6.1 fusion.72
  528.9 7.4 %convolution_convert_fusion.5.refs_0_ = bf16[1536,768]{1,0:T(8,128)(2,1)} fusion(bf16[1280,1536]{0,1:T(8,128)(2,1)} %pad_maximum_fusion, bf16[1280,768]{1,0:T(8,128)(2,1)} %add_convert_fusion.1), kind=kOutput, calls=%fused_computation.54 | convolution fusion | flops 3021078528 | bytes 8257536 | tf_op jit(solution)/shard_map/dot_general | solution.py:25
  536.3 7.1 %restore_blocks.3 = bf16[1536,2304]{1,0:T(8,128)(2,1)} custom-call(s32[4]{0:T(128)} %pad_add_fusion.2.order_ref, bf16[1536,768]{1,0:T(8,128)(2,1)} %convolution_convert_fusion.5.refs_0_, bf16[1536,768]{1,0:T(8,128)(2,1)} %convolution_convert_fusion.4.refs_1_, bf16[1536,768]{1,0:T(8,128)(2,1)} %convolution_convert_fusion.3.refs_2_), custom_call_target="tpu_custom_call" | custom-call | bytes 14155776 | tf_op jit(solution)/shard_map/restore_blocks/pallas_call | solution.py:673
  568.7 17.1 %collective-permute-done.42 = f32[8,128]{1,0:T(8,128)S(1)} collective-permute-done((f32[8,128]{1,0:T(8,128)S(1)}, f32[8,128]{1,0:T(8,128)S(1)}, u32[]{:S(2)}, u32[]{:S(2)}) %collective-permute-start.42) | collective-permute-done | bytes 4128 | tf_op jit(solution)/shard_map/ppermute | solution.py:503
  598.4 7.5 %gather_fusion.5 = bf16[2048,384]{1,0:T(8,128)(2,1)S(1)} fusion(bf16[1280,384]{1,0:T(8,128)(2,1)S(1)} %copy.119, s32[2048]{0:T(1024)S(1)} %broadcast_clamp_fusion), kind=kCustom, calls=%fused_computation.5 | custom fusion | bytes 3153920 | tf_op jit(solution)/shard_map/gather | solution.py:929
  615.7 39.3 %all-to-all-done = bf16[8,304,384]{2,1,0:T(8,128)(2,1)S(1)} async-done(((bf16[8,304,384]{2,1,0:T(8,128)(2,1)}), bf16[8,304,384]{2,1,0:T(8,128)(2,1)S(1)}, u32[]{:S(2)}, u32[]{:S(2)}) %all-to-all-start) | async-done | bytes 1867808 | tf_op jit(solution)/shard_map/all_to_all | solution.py:621
  664.3 27.0 %reduce-scatter.5.cloned.1.call-done = bf16[192,2304]{1,0:T(8,128)(2,1)} async-done(((bf16[1536,2304]{1,0:T(8,128)(2,1)}), bf16[192,2304]{1,0:T(8,128)(2,1)}) %reduce-scatter.5.cloned.1.call-update) | async-done | bytes 884752 | tf_op jit(solution)/shard_map/reduce_scatter | solution.py:585
  (441 shorter events, 230.4 us)
Async XLA Ops:
  7.2 147.0 %all-gather.3.cloned.1.call-start = ((), (), s32[]{:S(2)}) async-start(), calls=%async_computation.3 | async-start | bytes 7962624 | tf_op jit(solution)/shard_map/all_gather | solution.py:572
  9.5 288.2 %all-gather.5.cloned.1.call-start = ((), (), s32[]{:S(2)}) async-start(), calls=%async_computation.4 | async-start | bytes 10616832 | tf_op jit(solution)/shard_map/all_gather | solution.py:572
  19.6 15.1 %collective-permute-start = (bf16[304,384]{1,0:T(8,128)(2,1)}, bf16[304,384]{1,0:T(8,128)(2,1)}, u32[]{:S(2)}, u32[]{:S(2)}) collective-permute-start(bf16[304,384]{1,0:T(8,128)(2,1)} %get-tuple-element.175), channel_id=1, source_target_pairs={{0,4},{4,0},{8,12},{12,8},{16,20},{20,16},{24,28},{28,24},{1,5},{5... | collective-permute-start | bytes 700424 | tf_op jit(solution)/shard_map/ppermute | solution.py:506
  22.5 30.5 %collective-permute-start.1 = (bf16[304,384]{1,0:T(8,128)(2,1)}, bf16[304,384]{1,0:T(8,128)(2,1)}, u32[]{:S(2)}, u32[]{:S(2)}) collective-permute-start(bf16[304,384]{1,0:T(8,128)(2,1)} %get-tuple-element.176), channel_id=1, source_target_pairs={{0,8},{4,12},{8,0},{12,4},{16,24},{20,28},{24,16},{28,20},{1,9},{5... | collective-permute-start | bytes 700424 | tf_op jit(solution)/shard_map/ppermute | solution.py:506
  24.1 40.4 %collective-permute-start.2 = (bf16[304,384]{1,0:T(8,128)(2,1)S(1)}, bf16[304,384]{1,0:T(8,128)(2,1)}, u32[]{:S(2)}, u32[]{:S(2)}) collective-permute-start(bf16[304,384]{1,0:T(8,128)(2,1)S(1)} %get-tuple-element.177), channel_id=1, source_target_pairs={{0,12},{4,8},{8,4},{12,0},{16,28},{20,24},{24,20},{28,16},{1,13},{... | collective-permute-start | bytes 700424 | tf_op jit(solution)/shard_map/ppermute | solution.py:506
  24.1 41.3 %collective-permute-start.3 = (bf16[304,384]{1,0:T(8,128)(2,1)S(1)}, bf16[304,384]{1,0:T(8,128)(2,1)}, u32[]{:S(2)}, u32[]{:S(2)}) collective-permute-start(bf16[304,384]{1,0:T(8,128)(2,1)S(1)} %get-tuple-element.178), channel_id=1, source_target_pairs={{0,16},{4,20},{8,24},{12,28},{16,0},{20,4},{24,8},{28,12},{1,17},{... | collective-permute-start | bytes 700424 | tf_op jit(solution)/shard_map/ppermute | solution.py:506
  27.1 47.0 %collective-permute-start.4 = (bf16[304,384]{1,0:T(8,128)(2,1)S(1)}, bf16[304,384]{1,0:T(8,128)(2,1)S(1)}, u32[]{:S(2)}, u32[]{:S(2)}) collective-permute-start(bf16[304,384]{1,0:T(8,128)(2,1)S(1)} %get-tuple-element.179), channel_id=1, source_target_pairs={{0,20},{4,16},{8,28},{12,24},{16,4},{20,0},{24,12},{28,8},{1,21},{... | collective-permute-start | bytes 700424 | tf_op jit(solution)/shard_map/ppermute | solution.py:506
  34.7 43.6 %collective-permute-start.5 = (bf16[304,384]{1,0:T(8,128)(2,1)S(1)}, bf16[304,384]{1,0:T(8,128)(2,1)S(1)}, u32[]{:S(2)}, u32[]{:S(2)}) collective-permute-start(bf16[304,384]{1,0:T(8,128)(2,1)S(1)} %get-tuple-element.180), channel_id=1, source_target_pairs={{0,24},{4,28},{8,16},{12,20},{16,8},{20,12},{24,0},{28,4},{1,25},{... | collective-permute-start | bytes 700424 | tf_op jit(solution)/shard_map/ppermute | solution.py:506
  53.0 32.3 %collective-permute-start.6 = (bf16[304,384]{1,0:T(8,128)(2,1)S(1)}, bf16[304,384]{1,0:T(8,128)(2,1)S(1)}, u32[]{:S(2)}, u32[]{:S(2)}) collective-permute-start(bf16[304,384]{1,0:T(8,128)(2,1)S(1)} %get-tuple-element.173), channel_id=1, source_target_pairs={{0,28},{4,24},{8,20},{12,16},{16,12},{20,8},{24,4},{28,0},{1,29},{... | collective-permute-start | bytes 700424 | tf_op jit(solution)/shard_map/ppermute | solution.py:506
  97.1 23.1 %collective-permute-start.9 = (bf16[1280,384]{0,1:T(8,128)(2,1)S(1)}, bf16[1280,384]{0,1:T(8,128)(2,1)S(1)}, u32[]{:S(2)}, u32[]{:S(2)}) collective-permute-start(bf16[1280,384]{0,1:T(8,128)(2,1)S(1)} %fusion.10), channel_id=1, source_target_pairs={{0,2},{1,3},{2,0},{3,1},{4,6},{5,7},{6,4},{7,5},{8,10},{9,11},{10,... | collective-permute-start | bytes 2949128 | tf_op jit(solution)/shard_map/ppermute | solution.py:503
  98.7 24.5 %collective-permute-start.10 = (bf16[1280,384]{0,1:T(8,128)(2,1)S(1)}, bf16[1280,384]{0,1:T(8,128)(2,1)}, u32[]{:S(2)}, u32[]{:S(2)}) collective-permute-start(bf16[1280,384]{0,1:T(8,128)(2,1)S(1)} %fusion.10), channel_id=1, source_target_pairs={{0,1},{1,0},{2,3},{3,2},{4,5},{5,4},{6,7},{7,6},{8,9},{9,8},{10,11... | collective-permute-start | bytes 2949128 | tf_op jit(solution)/shard_map/ppermute | solution.py:503
  161.2 382.2 %reduce-scatter.3.cloned.1.call-start = ((), (), s32[]{:S(2)}) async-start(), calls=%async_computation.5 | async-start | bytes 10616832 | tf_op jit(solution)/shard_map/reduce_scatter | solution.py:585
  179.9 30.4 %collective-permute-start.12 = (bf16[1280,384]{0,1:T(8,128)(2,1)S(1)}, bf16[1280,384]{0,1:T(8,128)(2,1)}, u32[]{:S(2)}, u32[]{:S(2)}) collective-permute-start(bf16[1280,384]{0,1:T(8,128)(2,1)S(1)} %copy-done.16), channel_id=1, source_target_pairs={{0,2},{1,3},{2,0},{3,1},{4,6},{5,7},{6,4},{7,5},{8,10},{9,11},{10,... | collective-permute-start | bytes 2949128 | tf_op jit(solution)/shard_map/ppermute | solution.py:503
  185.3 24.8 %collective-permute-start.16 = (f32[640,128]{1,0:T(8,128)S(1)}, f32[640,128]{1,0:T(8,128)S(1)}, u32[]{:S(2)}, u32[]{:S(2)}) collective-permute-start(f32[640,128]{1,0:T(8,128)S(1)} %dynamic-slice_add_fusion), channel_id=1, source_target_pairs={{0,2},{1,3},{2,0},{3,1},{4,6},{5,7},{6,4},{7,5},{8,10},{9,11},{10,... | collective-permute-start | bytes 983048 | tf_op jit(solution)/shard_map/ppermute | solution.py:503
  186.8 59.4 %collective-permute-start.13 = (bf16[1280,384]{0,1:T(8,128)(2,1)S(1)}, bf16[1280,384]{0,1:T(8,128)(2,1)}, u32[]{:S(2)}, u32[]{:S(2)}) collective-permute-start(bf16[1280,384]{0,1:T(8,128)(2,1)S(1)} %copy-done.16), channel_id=1, source_target_pairs={{0,1},{1,0},{2,3},{3,2},{4,5},{5,4},{6,7},{7,6},{8,9},{9,8},{10,11... | collective-permute-start | bytes 2949128 | tf_op jit(solution)/shard_map/ppermute | solution.py:503
  210.2 8.7 %collective-permute-start.17 = (f32[640,128]{1,0:T(8,128)S(1)}, f32[640,128]{1,0:T(8,128)S(1)}, u32[]{:S(2)}, u32[]{:S(2)}) collective-permute-start(f32[640,128]{1,0:T(8,128)S(1)} %add.348), channel_id=1, source_target_pairs={{0,1},{1,0},{2,3},{3,2},{4,5},{5,4},{6,7},{7,6},{8,9},{9,8},{10,11... | collective-permute-start | bytes 983048 | tf_op jit(solution)/shard_map/ppermute | solution.py:503
  210.3 36.0 %collective-permute-start.14 = (bf16[1280,384]{0,1:T(8,128)(2,1)}, bf16[1280,384]{0,1:T(8,128)(2,1)}, u32[]{:S(2)}, u32[]{:S(2)}) collective-permute-start(bf16[1280,384]{0,1:T(8,128)(2,1)} %collective-permute-done.12), channel_id=1, source_target_pairs={{0,1},{1,0},{2,3},{3,2},{4,5},{5,4},{6,7},{7,6},{8,9},{9,8},{10,11... | collective-permute-start | bytes 2949128 | tf_op jit(solution)/shard_map/ppermute | solution.py:503
  255.9 23.9 %collective-permute-start.19 = (bf16[1280,384]{0,1:T(8,128)(2,1)S(1)}, bf16[1280,384]{0,1:T(8,128)(2,1)S(1)}, u32[]{:S(2)}, u32[]{:S(2)}) collective-permute-start(bf16[1280,384]{0,1:T(8,128)(2,1)S(1)} %slice.572), channel_id=1, source_target_pairs={{0,2},{1,3},{2,0},{3,1},{4,6},{5,7},{6,4},{7,5},{8,10},{9,11},{10,... | collective-permute-start | bytes 2949128 | tf_op jit(solution)/shard_map/ppermute | solution.py:503
  286.4 23.4 %collective-permute-start.22 = (bf16[1280,384]{0,1:T(8,128)(2,1)}, bf16[1280,384]{0,1:T(8,128)(2,1)}, u32[]{:S(2)}, u32[]{:S(2)}) collective-permute-start(bf16[1280,384]{0,1:T(8,128)(2,1)} %multiply_convert_fusion.4), channel_id=1, source_target_pairs={{0,2},{1,3},{2,0},{3,1},{4,6},{5,7},{6,4},{7,5},{8,10},{9,11},{10,... | collective-permute-start | bytes 2949128 | tf_op jit(solution)/shard_map/ppermute | solution.py:503
  287.9 25.9 %collective-permute-start.23 = (bf16[1280,384]{0,1:T(8,128)(2,1)}, bf16[1280,384]{0,1:T(8,128)(2,1)}, u32[]{:S(2)}, u32[]{:S(2)}) collective-permute-start(bf16[1280,384]{0,1:T(8,128)(2,1)} %multiply_convert_fusion.4), channel_id=1, source_target_pairs={{0,1},{1,0},{2,3},{3,2},{4,5},{5,4},{6,7},{7,6},{8,9},{9,8},{10,11... | collective-permute-start | bytes 2949128 | tf_op jit(solution)/shard_map/ppermute | solution.py:503
  309.8 4.1 collective-permute-start.24
  347.0 35.0 %collective-permute-start.25 = (bf16[1280,768]{0,1:T(8,128)(2,1)}, bf16[1280,768]{0,1:T(8,128)(2,1)}, u32[]{:S(2)}, u32[]{:S(2)}) collective-permute-start(bf16[1280,768]{0,1:T(8,128)(2,1)} %add_convert_fusion.2), channel_id=1, source_target_pairs={{0,1},{1,0},{2,3},{3,2},{4,5},{5,4},{6,7},{7,6},{8,9},{9,8},{10,11... | collective-permute-start | bytes 5898248 | tf_op jit(solution)/shard_map/ppermute | solution.py:503
  377.1 314.2 %reduce-scatter.5.cloned.1.call-start = ((), (), s32[]{:S(2)}) async-start(), calls=%async_computation.6 | async-start | bytes 7962624 | tf_op jit(solution)/shard_map/reduce_scatter | solution.py:585
  386.5 23.2 %collective-permute-start.26 = (bf16[1280,384]{0,1:T(8,128)(2,1)S(1)}, bf16[1280,384]{0,1:T(8,128)(2,1)S(1)}, u32[]{:S(2)}, u32[]{:S(2)}) collective-permute-start(bf16[1280,384]{0,1:T(8,128)(2,1)S(1)} %slice.571), channel_id=1, source_target_pairs={{0,2},{1,3},{2,0},{3,1},{4,6},{5,7},{6,4},{7,5},{8,10},{9,11},{10,... | collective-permute-start | bytes 2949128 | tf_op jit(solution)/shard_map/ppermute | solution.py:503
  417.2 23.1 %collective-permute-start.29 = (bf16[1280,384]{0,1:T(8,128)(2,1)S(1)}, bf16[1280,384]{0,1:T(8,128)(2,1)S(1)}, u32[]{:S(2)}, u32[]{:S(2)}) collective-permute-start(bf16[1280,384]{0,1:T(8,128)(2,1)S(1)} %get-tuple-element.162), channel_id=1, source_target_pairs={{0,2},{1,3},{2,0},{3,1},{4,6},{5,7},{6,4},{7,5},{8,10},{9,11},{10,... | collective-permute-start | bytes 2949128 | tf_op jit(solution)/shard_map/ppermute | solution.py:503
  418.6 24.0 %collective-permute-start.30 = (bf16[1280,384]{0,1:T(8,128)(2,1)S(1)}, bf16[1280,384]{0,1:T(8,128)(2,1)S(1)}, u32[]{:S(2)}, u32[]{:S(2)}) collective-permute-start(bf16[1280,384]{0,1:T(8,128)(2,1)S(1)} %get-tuple-element.162), channel_id=1, source_target_pairs={{0,1},{1,0},{2,3},{3,2},{4,5},{5,4},{6,7},{7,6},{8,9},{9,8},{10,11... | collective-permute-start | bytes 2949128 | tf_op jit(solution)/shard_map/ppermute | solution.py:503
  449.2 51.0 %collective-permute-start.33 = (bf16[1280,384]{0,1:T(8,128)(2,1)}, bf16[1280,384]{0,1:T(8,128)(2,1)}, u32[]{:S(2)}, u32[]{:S(2)}) collective-permute-start(bf16[1280,384]{0,1:T(8,128)(2,1)} %slice.570), channel_id=1, source_target_pairs={{0,2},{1,3},{2,0},{3,1},{4,6},{5,7},{6,4},{7,5},{8,10},{9,11},{10,... | collective-permute-start | bytes 2949128 | tf_op jit(solution)/shard_map/ppermute | solution.py:503
  505.0 6.3 collective-permute-start.35
  511.4 4.8 collective-permute-start.36
  561.4 25.0 %collective-permute-start.38 = (bf16[1280,384]{0,1:T(8,128)(2,1)}, bf16[1280,384]{0,1:T(8,128)(2,1)}, u32[]{:S(2)}, u32[]{:S(2)}) collective-permute-start(bf16[1280,384]{0,1:T(8,128)(2,1)} %slice.569), channel_id=1, source_target_pairs={{0,2},{1,3},{2,0},{3,1},{4,6},{5,7},{6,4},{7,5},{8,10},{9,11},{10,... | collective-permute-start | bytes 2949128 | tf_op jit(solution)/shard_map/ppermute | solution.py:503
  566.1 19.7 %collective-permute-start.42 = (f32[8,128]{1,0:T(8,128)S(1)}, f32[8,128]{1,0:T(8,128)S(1)}, u32[]{:S(2)}, u32[]{:S(2)}) collective-permute-start(f32[8,128]{1,0:T(8,128)S(1)} %get-tuple-element.212), channel_id=1, source_target_pairs={{0,2},{1,3},{2,0},{3,1},{4,6},{5,7},{6,4},{7,5},{8,10},{9,11},{10,... | collective-permute-start | bytes 12296 | tf_op jit(solution)/shard_map/ppermute | solution.py:503
  607.8 47.2 %all-to-all-start = ((bf16[8,304,384]{2,1,0:T(8,128)(2,1)}), bf16[8,304,384]{2,1,0:T(8,128)(2,1)S(1)}, u32[]{:S(2)}, u32[]{:S(2)}) async-start(bf16[8,304,384]{2,1,0:T(8,128)(2,1)} %pad_maximum_fusion.3), calls=%async_computation | async-start | bytes 3735552 | tf_op jit(solution)/shard_map/all_to_all | solution.py:621
  (91 other events, 1032.3 us)
Sparse Core Ops, SparseCore 0:
  10.2 143.9 all-gather.2
  161.4 136.2 all-gather.4
  377.2 161.9 reduce-scatter.2
  546.3 144.9 reduce-scatter.4
